TPU v7x, 32 devices: a whole 2x2x4 slice. The times are simulated.
32 devices in a mesh: expert: 8 (over z, x), shard: 4 (over y, core).
Axes of the slice: x: 2, y: 2, z: 4, core: 2. Of those that a mesh axis runs over, the one named last changes fastest.
Arguments:
- tokens: bfloat16 [8192, 2048], P(('expert', 'shard')), may hold values from -6 to 6
- out_grad: bfloat16 [8192, 2048], P(('expert', 'shard')), may hold values from -6 to 6
- routes: int32 [8192, 8], P(('expert', 'shard')), may hold values from 0 to 15, as said below
- segments: int32 [8192], P('expert'), may hold values from 0 to 31, never falling along the last dimension, each value on 1 to 1024 neighbouring positions
- capacity: int32 [16], replicated, may hold values from 64 to 128, as said below
- attn_gain: bfloat16 [2048], P('shard'), may hold values from 0.5 to 1.5
- w_qkv: bfloat16 [2048, 6144], P('shard'), may hold values from -0.125 to 0.125
- query_gain: bfloat16 [128], P('shard'), may hold values from 0.5 to 1.5
- key_gain: bfloat16 [128], P('shard'), may hold values from 0.5 to 1.5
- w_out: bfloat16 [2048, 2048], P('shard'), may hold values from -0.5 to 0.5
- ffn_gain: bfloat16 [2048], P('shard'), may hold values from 0.5 to 1.5
- w_router: bfloat16 [2048, 16], P('shard'), may hold values from -0.0625 to 0.0625
- w_gate_up: bfloat16 [16, 2, 2048, 1024], P('expert', None, None, 'shard'), may hold values from -0.125 to 0.125
- w_down: bfloat16 [16, 1024, 2048], P('expert', 'shard'), may hold values from -6 to 6
Outputs:
- layer_out: bfloat16 [8192, 2048], P(('expert', 'shard'))
- tokens_grad: float32 [8192, 2048], P(('expert', 'shard'))
- attn_gain_grad: float32 [2048], P('shard')
- w_qkv_grad: float32 [2048, 6144], P('shard')
- query_gain_grad: float32 [128], P('shard')
- key_gain_grad: float32 [128], P('shard')
- w_out_grad: float32 [2048, 2048], P('shard')
- ffn_gain_grad: float32 [2048], P('shard')
- w_router_grad: float32 [2048, 16], P('shard')
- w_gate_up_grad: float32 [16, 2, 2048, 1024], P('expert', None, None, 'shard')
- w_down_grad: float32 [16, 1024, 2048], P('expert', 'shard')
Inputs may be any that keep to these rules, and one draw needn't show every extreme that they name: `routes`: each token names 8 different experts. `capacity`: some expert has 128 slots. `segments`: document numbers never fall along the tokens.
All inputs are finite; a program needn't handle non-finite values.
Results may differ from a plain program's by a relative error of at most 0.025.
Values may be sent and summed in bfloat16 or wider, within the bound.
No kernel may reach another device: no remote copies, remote signals or barrier semaphores. Data moves between devices by JAX's collectives and lax.ppermute only.
A program may use at most 512 MiB of HBM per device.

v0:
```python
import jax
import jax.numpy as jnp
from jax import lax
from jax.sharding import PartitionSpec as P

HEADS = 16


EPS = 1e-06
THETA = 50000.0
NEG_BIG = -1e30


def rms_scale(values):
    return lax.rsqrt(jnp.mean(values * values, axis=-1, keepdims=True) + EPS)


def norm_back(grad_in, values, scale, gain):
    weighted = grad_in * gain
    value_grad = scale * weighted - values * scale**3 * jnp.mean(
        weighted * values, axis=-1, keepdims=True
    )
    return (value_grad, grad_in * values * scale)


def rotate(values, cosines, sines, factor):
    half_size = values.shape[-1] // 2
    first_half = values[..., :half_size]
    second_half = values[..., half_size:]
    return jnp.concatenate(
        [
            first_half * cosines - factor * second_half * sines,
            second_half * cosines + factor * first_half * sines,
        ],
        axis=-1,
    )


def expert_pass(rows_in, rows_cot, gate_up, down_proj):
    pre_gate = jnp.einsum(
        "secd,edf->secf", rows_in, gate_up[:, 0], preferred_element_type=jnp.float32
    )
    pre_up = jnp.einsum(
        "secd,edf->secf", rows_in, gate_up[:, 1], preferred_element_type=jnp.float32
    )
    sigmoid_gate = jax.nn.sigmoid(pre_gate)
    silu_gate = pre_gate * sigmoid_gate
    activated = (silu_gate * pre_up).astype(jnp.bfloat16)
    expert_out = jnp.einsum(
        "secf,efd->secd", activated, down_proj, preferred_element_type=jnp.float32
    )
    act_back = jnp.einsum("secd,efd->secf", rows_cot, down_proj, preferred_element_type=jnp.float32)
    gate_back = (
        act_back * pre_up * (sigmoid_gate + pre_gate * sigmoid_gate * (1.0 - sigmoid_gate))
    ).astype(jnp.bfloat16)
    up_back = (act_back * silu_gate).astype(jnp.bfloat16)
    down_grad = jnp.einsum(
        "secf,secd->efd", activated, rows_cot, preferred_element_type=jnp.float32
    )
    gate_grad = jnp.einsum("secd,secf->edf", rows_in, gate_back, preferred_element_type=jnp.float32)
    up_grad = jnp.einsum("secd,secf->edf", rows_in, up_back, preferred_element_type=jnp.float32)
    rows_back = jnp.einsum(
        "secf,edf->secd", gate_back, gate_up[:, 0], preferred_element_type=jnp.float32
    )
    rows_back = rows_back + jnp.einsum(
        "secf,edf->secd", up_back, gate_up[:, 1], preferred_element_type=jnp.float32
    )
    return (expert_out, rows_back, jnp.stack([gate_grad, up_grad], axis=1), down_grad)


def on_device(
    tokens,
    out_grad,
    routes,
    segments,
    capacity,
    attn_gain,
    w_qkv,
    query_gain,
    key_gain,
    w_out,
    ffn_gain,
    w_router,
    w_gate_up,
    w_down,
):
    n_expert = lax.axis_size("expert")
    row_count, model_width = tokens.shape
    head_count = HEADS
    head_size = model_width // head_count
    seq_length = segments.shape[0]
    expert_count = capacity.shape[0]
    local_experts = w_down.shape[0]
    route_count = routes.shape[1]
    slot_count = row_count * route_count // expert_count
    shard_index = lax.axis_index("shard")
    full_qkv, full_out, full_router, gain_one, gain_query, gain_key, gain_two = (
        lax.all_gather(w_qkv, "shard", axis=0, tiled=True),
        lax.all_gather(w_out, "shard", axis=0, tiled=True),
        lax.all_gather(w_router, "shard", axis=0, tiled=True),
        lax.all_gather(attn_gain, "shard", axis=0, tiled=True),
        lax.all_gather(query_gain, "shard", axis=0, tiled=True),
        lax.all_gather(key_gain, "shard", axis=0, tiled=True),
        lax.all_gather(ffn_gain, "shard", axis=0, tiled=True),
    )
    gain_one = gain_one.astype(jnp.float32)
    gain_query = gain_query.astype(jnp.float32)
    gain_key = gain_key.astype(jnp.float32)
    gain_two = gain_two.astype(jnp.float32)
    tok_float = tokens.astype(jnp.float32)
    cot_float = out_grad.astype(jnp.float32)
    scale_one = rms_scale(tok_float)
    normed_one = (tok_float * scale_one * gain_one).astype(jnp.bfloat16)
    qkv_pre = jnp.dot(normed_one, full_qkv, preferred_element_type=jnp.float32)
    query_pre = qkv_pre[:, :model_width].reshape(row_count, head_count, head_size)
    key_pre = qkv_pre[:, model_width : 2 * model_width].reshape(row_count, head_count, head_size)
    value_pre = qkv_pre[:, 2 * model_width :]
    query_scale = rms_scale(query_pre)
    key_scale = rms_scale(key_pre)
    half_size = head_size // 2
    position = (shard_index * row_count + jnp.arange(row_count, dtype=jnp.int32)).astype(
        jnp.float32
    )
    frequency = THETA ** (-(2.0 * jnp.arange(half_size, dtype=jnp.float32)) / head_size)
    angles = position[:, None] * frequency[None, :]
    cosines = jnp.cos(angles)[:, None, :]
    sines = jnp.sin(angles)[:, None, :]
    query_low = rotate(query_pre * query_scale * gain_query, cosines, sines, 1.0).astype(
        jnp.bfloat16
    )
    key_low = rotate(key_pre * key_scale * gain_key, cosines, sines, 1.0).astype(jnp.bfloat16)
    value_low = value_pre.astype(jnp.bfloat16)
    keys_all, values_all = (
        lax.all_gather(key_low.reshape(row_count, model_width), "shard", axis=0, tiled=True),
        lax.all_gather(value_low, "shard", axis=0, tiled=True),
    )
    keys_all = keys_all.reshape(seq_length, head_count, head_size)
    values_all = values_all.reshape(seq_length, head_count, head_size)
    own_docs = lax.dynamic_slice_in_dim(segments, shard_index * row_count, row_count)
    same_doc = (own_docs[:, None] == segments[None, :])[None]
    score_scale = head_size ** (-0.5)

    def masked_scores():
        raw = (
            jnp.einsum("qhd,khd->hqk", query_low, keys_all, preferred_element_type=jnp.float32)
            * score_scale
        )
        return jnp.where(same_doc, raw, NEG_BIG)

    scores = masked_scores()
    row_max = jnp.max(scores, axis=-1, keepdims=True)
    shifted = jnp.exp(scores - row_max)
    row_total = jnp.sum(shifted, axis=-1, keepdims=True)
    probs = shifted / row_total
    log_total = row_max + jnp.log(row_total)
    mixed_heads = jnp.einsum(
        "hqk,khd->qhd", probs.astype(jnp.bfloat16), values_all, preferred_element_type=jnp.float32
    )
    mixed_low = mixed_heads.reshape(row_count, model_width).astype(jnp.bfloat16)
    hidden = tok_float + jnp.dot(mixed_low, full_out, preferred_element_type=jnp.float32)
    scale_two = rms_scale(hidden)
    ffn_low = (hidden * scale_two * gain_two).astype(jnp.bfloat16)
    logits = jnp.dot(ffn_low, full_router, preferred_element_type=jnp.float32)
    router = jax.nn.softmax(logits, axis=-1)
    expert_ids = jnp.arange(expert_count, dtype=jnp.int32)
    chosen_mask = routes[:, :, None] == expert_ids[None, None, :]
    gate_values = jnp.sum(jnp.where(chosen_mask, router[:, None, :], 0.0), axis=-1)
    flat_routes = routes.reshape(-1)
    one_hot = (flat_routes[:, None] == expert_ids[None, :]).astype(jnp.int32)
    earlier = jnp.sum((jnp.cumsum(one_hot, axis=0) - one_hot) * one_hot, axis=-1)
    limit_of_pair = jnp.sum(one_hot * capacity[None, :], axis=-1)
    kept_mask = earlier < limit_of_pair
    slot_index = jnp.where(kept_mask, flat_routes * slot_count + earlier, expert_count * slot_count)
    pair_count = row_count * route_count
    source_pair = (
        jnp.full((expert_count * slot_count + 1,), pair_count, jnp.int32)
        .at[slot_index]
        .set(jnp.arange(pair_count, dtype=jnp.int32))[: expert_count * slot_count]
    )
    kept_float = kept_mask.reshape(row_count, route_count).astype(jnp.float32)
    pair_weight = gate_values * kept_float
    padded_in = jnp.concatenate([ffn_low, jnp.zeros((1, model_width), jnp.bfloat16)], axis=0)
    pair_cot = (
        (pair_weight[:, :, None] * cot_float[:, None, :])
        .astype(jnp.bfloat16)
        .reshape(pair_count, model_width)
    )
    padded_cot = jnp.concatenate([pair_cot, jnp.zeros((1, model_width), jnp.bfloat16)], axis=0)
    send_shape = (n_expert, local_experts * slot_count, model_width)
    send_rows = padded_in[source_pair // route_count].reshape(send_shape)
    send_cot = padded_cot[source_pair].reshape(send_shape)
    recv_rows, recv_cot = (
        lax.all_to_all(send_rows, "expert", split_axis=0, concat_axis=0, tiled=True),
        lax.all_to_all(send_cot, "expert", split_axis=0, concat_axis=0, tiled=True),
    )
    grid_shape = (n_expert, local_experts, slot_count, model_width)
    recv_rows = recv_rows.reshape(grid_shape)
    recv_cot = recv_cot.reshape(grid_shape)
    full_gate_up, full_down = (
        lax.all_gather(w_gate_up, "shard", axis=3, tiled=True),
        lax.all_gather(w_down, "shard", axis=1, tiled=True),
    )
    expert_out, rows_back, gate_up_part, down_part = expert_pass(
        recv_rows, recv_cot, full_gate_up, full_down
    )
    back_out = expert_out.astype(jnp.bfloat16)
    back_rows = rows_back.astype(jnp.bfloat16)
    gate_up_grad, down_grad = (
        lax.psum_scatter(
            gate_up_part.astype(jnp.bfloat16), "shard", scatter_dimension=3, tiled=True
        ).astype(jnp.float32),
        lax.psum_scatter(
            down_part.astype(jnp.bfloat16), "shard", scatter_dimension=1, tiled=True
        ).astype(jnp.float32),
    )
    ret_out, ret_back = (
        lax.all_to_all(
            back_out.reshape(send_shape), "expert", split_axis=0, concat_axis=0, tiled=True
        ),
        lax.all_to_all(
            back_rows.reshape(send_shape), "expert", split_axis=0, concat_axis=0, tiled=True
        ),
    )
    pair_slot = jnp.where(kept_mask, slot_index, 0).reshape(row_count, route_count)
    pair_out = ret_out.reshape(expert_count * slot_count, model_width)[pair_slot].astype(
        jnp.float32
    )
    expert_mix = jnp.sum(pair_weight[:, :, None] * pair_out, axis=1)
    layer_out = (hidden + expert_mix).astype(jnp.bfloat16)
    gate_grad = jnp.sum(cot_float[:, None, :] * pair_out, axis=-1) * kept_float
    router_back = jnp.sum(jnp.where(chosen_mask, gate_grad[:, :, None], 0.0), axis=1)
    logit_back = (
        router * (router_back - jnp.sum(router * router_back, axis=-1, keepdims=True))
    ).astype(jnp.bfloat16)
    router_grad = jnp.dot(ffn_low.T, logit_back, preferred_element_type=jnp.float32)
    pair_back = ret_back.reshape(expert_count * slot_count, model_width)[pair_slot].astype(
        jnp.float32
    )
    ffn_back = jnp.sum(pair_back * kept_float[:, :, None], axis=1)
    ffn_back = ffn_back + jnp.dot(logit_back, full_router.T, preferred_element_type=jnp.float32)
    hidden_part, gain_two_terms = norm_back(ffn_back, hidden, scale_two, gain_two)
    hidden_back = cot_float + hidden_part
    mix_back = hidden_back.astype(jnp.bfloat16)
    out_grad_w = jnp.dot(mixed_low.T, mix_back, preferred_element_type=jnp.float32)
    head_back = jnp.dot(mix_back, full_out.T, preferred_element_type=jnp.float32).astype(
        jnp.bfloat16
    )
    head_back = head_back.reshape(row_count, head_count, head_size)
    probs_again = jnp.exp(masked_scores() - log_total)
    prob_back = jnp.einsum(
        "qhd,khd->hqk", head_back, values_all, preferred_element_type=jnp.float32
    )
    score_back = (
        probs_again * (prob_back - jnp.sum(probs_again * prob_back, axis=-1, keepdims=True))
    ).astype(jnp.bfloat16)
    query_back = (
        jnp.einsum("hqk,khd->qhd", score_back, keys_all, preferred_element_type=jnp.float32)
        * score_scale
    )
    key_part = (
        jnp.einsum("hqk,qhd->khd", score_back, query_low, preferred_element_type=jnp.float32)
        * score_scale
    )
    value_part = jnp.einsum(
        "hqk,qhd->khd",
        probs_again.astype(jnp.bfloat16),
        head_back,
        preferred_element_type=jnp.float32,
    )
    key_back, value_back = (
        lax.psum_scatter(
            key_part.reshape(seq_length, model_width).astype(jnp.bfloat16),
            "shard",
            scatter_dimension=0,
            tiled=True,
        ).astype(jnp.float32),
        lax.psum_scatter(
            value_part.reshape(seq_length, model_width).astype(jnp.bfloat16),
            "shard",
            scatter_dimension=0,
            tiled=True,
        ).astype(jnp.float32),
    )
    query_round = lax.optimization_barrier(query_back.astype(jnp.bfloat16)).astype(jnp.float32)
    key_round = lax.optimization_barrier(key_back.astype(jnp.bfloat16)).astype(jnp.float32)
    query_normed_back = rotate(query_round, cosines, sines, -1.0)
    key_normed_back = rotate(
        key_round.reshape(row_count, head_count, head_size), cosines, sines, -1.0
    )
    query_pre_back, query_terms = norm_back(query_normed_back, query_pre, query_scale, gain_query)
    key_pre_back, key_terms = norm_back(key_normed_back, key_pre, key_scale, gain_key)
    qkv_back = jnp.concatenate(
        [
            query_pre_back.reshape(row_count, model_width).astype(jnp.bfloat16),
            key_pre_back.reshape(row_count, model_width).astype(jnp.bfloat16),
            value_back.astype(jnp.bfloat16),
        ],
        axis=1,
    )
    qkv_grad = jnp.dot(normed_one.T, qkv_back, preferred_element_type=jnp.float32)
    normed_back = jnp.dot(qkv_back, full_qkv.T, preferred_element_type=jnp.float32)
    token_part, gain_one_terms = norm_back(normed_back, tok_float, scale_one, gain_one)
    tokens_grad = hidden_back + token_part
    shard_sums = (
        lax.psum_scatter(
            qkv_grad.astype(jnp.bfloat16), "shard", scatter_dimension=0, tiled=True
        ).astype(jnp.float32),
        lax.psum_scatter(
            out_grad_w.astype(jnp.bfloat16), "shard", scatter_dimension=0, tiled=True
        ).astype(jnp.float32),
        lax.psum_scatter(
            router_grad.astype(jnp.bfloat16), "shard", scatter_dimension=0, tiled=True
        ).astype(jnp.float32),
        lax.psum_scatter(
            jnp.sum(gain_one_terms, axis=0).astype(jnp.bfloat16),
            "shard",
            scatter_dimension=0,
            tiled=True,
        ).astype(jnp.float32),
        lax.psum_scatter(
            jnp.sum(query_terms, axis=(0, 1)).astype(jnp.bfloat16),
            "shard",
            scatter_dimension=0,
            tiled=True,
        ).astype(jnp.float32),
        lax.psum_scatter(
            jnp.sum(key_terms, axis=(0, 1)).astype(jnp.bfloat16),
            "shard",
            scatter_dimension=0,
            tiled=True,
        ).astype(jnp.float32),
        lax.psum_scatter(
            jnp.sum(gain_two_terms, axis=0).astype(jnp.bfloat16),
            "shard",
            scatter_dimension=0,
            tiled=True,
        ).astype(jnp.float32),
    )
    qkv_total, out_total, router_total, gain_one_total, query_total, key_total, gain_two_total = (
        lax.psum(shard_sums[0].astype(jnp.bfloat16), "expert").astype(jnp.float32),
        lax.psum(shard_sums[1].astype(jnp.bfloat16), "expert").astype(jnp.float32),
        lax.psum(shard_sums[2].astype(jnp.bfloat16), "expert").astype(jnp.float32),
        lax.psum(shard_sums[3].astype(jnp.bfloat16), "expert").astype(jnp.float32),
        lax.psum(shard_sums[4].astype(jnp.bfloat16), "expert").astype(jnp.float32),
        lax.psum(shard_sums[5].astype(jnp.bfloat16), "expert").astype(jnp.float32),
        lax.psum(shard_sums[6].astype(jnp.bfloat16), "expert").astype(jnp.float32),
    )
    return (
        layer_out,
        tokens_grad,
        gain_one_total,
        qkv_total,
        query_total,
        key_total,
        out_total,
        gain_two_total,
        router_total,
        gate_up_grad,
        down_grad,
    )


def solution(mesh):
    placed = (
        P(("expert", "shard"), None),
        P(("expert", "shard"), None),
        P(("expert", "shard"), None),
        P("expert"),
        P(),
        P("shard"),
        P("shard", None),
        P("shard"),
        P("shard"),
        P("shard", None),
        P("shard"),
        P("shard", None),
        P("expert", None, None, "shard"),
        P("expert", "shard", None),
    )
    return jax.shard_map(
        on_device,
        mesh=mesh,
        in_specs=placed,
        out_specs=(
            P(("expert", "shard"), None),
            P(("expert", "shard"), None),
            P("shard"),
            P("shard", None),
            P("shard"),
            P("shard"),
            P("shard", None),
            P("shard"),
            P("shard", None),
            P("expert", None, None, "shard"),
            P("expert", "shard", None),
        ),
        check_vma=False,
    )
```

profile of v0, /device:TPU:0, one launch (start us, length us, event | category | flops | bytes accessed | tf_op | source)
XLA Modules:
  0.0 2082.1 jit_solution(13702281081617248424)
XLA Ops:
  26.7 140.4 %all-gather.9.cloned.1.call-done = bf16[2048,6144]{1,0:T(8,128)(2,1)} async-done(((bf16[512,6144]{1,0:T(8,128)(2,1)}), bf16[2048,6144]{1,0:T(8,128)(2,1)}) %all-gather.9.cloned.1.call-update) | async-done | bytes 25165840 | tf_op jit(solution)/shard_map/all_gather | solution.py:98
  249.8 20.4 all-gather.11.cloned.1.call-done
  280.0 49.8 %all-gather.15.cloned.1.call-done = bf16[2048,2048]{1,0:T(8,128)(2,1)} async-done(((bf16[512,2048]{1,0:T(8,128)(2,1)}), bf16[2048,2048]{1,0:T(8,128)(2,1)}) %all-gather.15.cloned.1.call-update) | async-done | bytes 8388624 | tf_op jit(solution)/shard_map/all_gather | solution.py:99
  375.4 20.8 %gather_fusion.2 = bf16[2048,2048]{1,0:T(8,128)(2,1)} fusion(bf16[2049,2048]{1,0:T(8,128)(2,1)} %concatenate.30, s32[2048]{0:T(1024)S(1)} %get-tuple-element.146), kind=kCustom, calls=%fused_computation.2 | custom fusion | bytes 16785408 | tf_op jit(solution)/shard_map/gather | solution.py:191
  396.3 141.2 %all-to-all-done = bf16[8,256,2048]{2,1,0:T(8,128)(2,1)} async-done(((bf16[8,256,2048]{2,1,0:T(8,128)(2,1)}), bf16[8,256,2048]{2,1,0:T(8,128)(2,1)}, u32[]{:S(2)}, u32[]{:S(2)}) %all-to-all-start) | async-done | bytes 8388640 | tf_op jit(solution)/shard_map/all_to_all | solution.py:193
  551.2 15.8 fusion.27
  580.2 29.4 %all-gather.19.cloned.1.call-done = bf16[2,1024,2048]{2,1,0:T(8,128)(2,1)} async-done(((bf16[2,256,2048]{2,1,0:T(8,128)(2,1)}), bf16[2,1024,2048]{2,1,0:T(8,128)(2,1)}) %all-gather.19.cloned.1.call-update) | async-done | bytes 8388624 | tf_op jit(solution)/shard_map/all_gather | solution.py:201
  609.7 115.5 %all-to-all-done.2 = bf16[8,256,2048]{2,1,0:T(8,128)(2,1)} async-done(((bf16[8,256,2048]{2,1,0:T(8,128)(2,1)}), bf16[8,256,2048]{2,1,0:T(8,128)(2,1)}, u32[]{:S(2)}, u32[]{:S(2)}) %all-to-all-start.2) | async-done | bytes 8388640 | tf_op jit(solution)/shard_map/all_to_all | solution.py:194
  725.1 20.2 fusion.13
  745.4 15.5 convert_bitcast_fusion
  774.1 15.8 fusion.24
  789.9 17.0 fusion.8
  815.3 140.8 %all-to-all-done.1 = bf16[8,256,2048]{2,1,0:T(8,128)(2,1)} async-done(((bf16[8,256,2048]{2,1,0:T(8,128)(2,1)}), bf16[8,256,2048]{2,1,0:T(8,128)(2,1)}, u32[]{:S(2)}, u32[]{:S(2)}) %all-to-all-start.1) | async-done | bytes 8388640 | tf_op jit(solution)/shard_map/all_to_all | solution.py:217
  961.9 21.1 %gather_fusion.1 = bf16[2048,2048]{1,0:T(8,128)(2,1)} fusion(bf16[2048,2048]{1,0:T(8,128)(2,1)} %bitcast.25, s32[2048]{0:T(1024)S(1)} %broadcast_clamp_fusion), kind=kCustom, calls=%fused_computation.1 | custom fusion | bytes 16785408 | tf_op jit(solution)/shard_map/gather | solution.py:225
  992.7 150.7 %all-to-all-done.3 = bf16[8,256,2048]{2,1,0:T(8,128)(2,1)} async-done(((bf16[8,256,2048]{2,1,0:T(8,128)(2,1)}), bf16[8,256,2048]{2,1,0:T(8,128)(2,1)}, u32[]{:S(2)}, u32[]{:S(2)}) %all-to-all-start.3) | async-done | bytes 8388640 | tf_op jit(solution)/shard_map/all_to_all | solution.py:220
  1143.4 20.8 gather_fusion.3
  1306.3 16.6 convolution_convert_fusion
  1322.9 15.5 bitcast_convert_fusion
  1353.7 18.6 fusion.9
  1387.2 178.1 %reduce-scatter.12.cloned.1.call-done = bf16[512,6144]{1,0:T(8,128)(2,1)} async-done(((bf16[2048,6144]{1,0:T(8,128)(2,1)}), bf16[512,6144]{1,0:T(8,128)(2,1)}) %reduce-scatter.12.cloned.1.call-update) | async-done | bytes 6291472 | tf_op jit(solution)/shard_map/reduce_scatter | solution.py:305
  1566.5 72.7 %reduce-scatter.20.cloned.1.call-done = bf16[2,256,2048]{2,1,0:T(8,128)(2,1)} async-done(((bf16[2,1024,2048]{2,1,0:T(8,128)(2,1)}), bf16[2,256,2048]{2,1,0:T(8,128)(2,1)}) %reduce-scatter.20.cloned.1.call-update) | async-done | bytes 2097168 | tf_op jit(solution)/shard_map/reduce_scatter | solution.py:212
  1664.0 37.7 %all-reduce.8 = (bf16[512]{0:T(512)(128)(2,1)S(1)}, bf16[32]{0:T(256)(128)(2,1)S(1)}, bf16[32]{0:T(256)(128)(2,1)S(1)}, bf16[512]{0:T(512)(128)(2,1)S(1)}, bf16[512,16]{0,1:T(8,128)(2,1)S(1)}) all-reduce(bf16[512]{0:T(512)(128)(2,1)S(1)} %dynamic-slice.3, ...), channel_id=1, replica_groups=mesh['expert'=8,'shard'=4] {'expert'}, use_global_device_ids=true, to_apply=%region_28.29 | all-reduce | flops 9280 | bytes 37120 | tf_op jit(solution)/shard_map/psum | solution.py:343
  1708.2 81.1 %reduce-scatter.18.cloned.1.call-done = bf16[2,2,2048,256]{3,2,0,1:T(8,128)(2,1)} async-done(((bf16[2,2,2048,1024]{3,2,0,1:T(8,128)(2,1)}), bf16[2,2,2048,256]{3,2,0,1:T(8,128)(2,1)}) %reduce-scatter.18.cloned.1.call-update) | async-done | bytes 4194320 | tf_op jit(solution)/shard_map/reduce_scatter | solution.py:209
  1795.6 267.7 %all-reduce.14.cloned.1.call-done = (bf16[512,6144]{1,0:T(8,128)(2,1)}, bf16[512,2048]{1,0:T(8,128)(2,1)}) async-done(((bf16[512,6144]{1,0:T(8,128)(2,1)}, bf16[512,2048]{1,0:T(8,128)(2,1)}), (bf16[512,6144]{1,0:T(8,128)(2,1)}, bf16[512,2048]{1,0:T(8,128)(2,1)})) %all-reduce.14.cloned.1.call-update) | async-done | bytes 8388624 | tf_op jit(solution)/shard_map/psum | solution.py:340
  (372 shorter events, 441.4 us)
Async XLA Ops:
  7.2 159.9 %all-gather.9.cloned.1.call-start = ((), (), s32[]{:S(2)}) async-start(), calls=%async_computation.11 | async-start | bytes 31457280 | tf_op jit(solution)/shard_map/all_gather | solution.py:98
  8.0 225.5 %all-gather.13.cloned.1.call-start = ((), (), s32[]{:S(2)}) async-start(), calls=%async_computation.13 | async-start | bytes 5242880 | tf_op jit(solution)/shard_map/all_gather | solution.py:134
  14.3 152.9 %copy-start.34 = (f32[4,1,512]{2,1,0:T(1,128)}, f32[4,1,512]{2,1,0:T(1,128)S(1)}, u32[]{:S(2)}) copy-start(f32[4,1,512]{2,1,0:T(1,128)S(1)} %convert_element_type.280) | copy-start | bytes 24580
  25.5 141.6 %copy-start.56 = (f32[256]{0:T(256)}, f32[256]{0:T(256)S(1)}, u32[]{:S(2)}) copy-start(f32[256]{0:T(256)S(1)} %get-tuple-element.154) | copy-start | bytes 3076
  26.7 166.3 %copy-start.30 = (f32[256,64]{1,0:T(8,128)}, f32[256,64]{1,0:T(8,128)S(1)}, u32[]{:S(2)}) copy-start(f32[256,64]{1,0:T(8,128)S(1)} %get-tuple-element.152) | copy-start | bytes 196612
  198.3 71.8 %all-gather.11.cloned.1.call-start = ((), (), s32[]{:S(2)}) async-start(), calls=%async_computation.12 | async-start | bytes 5242880 | tf_op jit(solution)/shard_map/all_gather | solution.py:135
  201.1 128.7 %all-gather.15.cloned.1.call-start = ((), (), s32[]{:S(2)}) async-start(), calls=%async_computation.14 | async-start | bytes 10485760 | tf_op jit(solution)/shard_map/all_gather | solution.py:99
  201.7 349.5 %all-gather.17.cloned.1.call-start = ((), (), s32[]{:S(2)}) async-start(), calls=%async_computation.15 | async-start | bytes 20971520 | tf_op jit(solution)/shard_map/all_gather | solution.py:200
  212.9 123.4 %copy-start.50 = (f32[4,1,512]{2,1,0:T(1,128)}, f32[4,1,512]{2,1,0:T(1,128)S(1)}, u32[]{:S(2)}) copy-start(f32[4,1,512]{2,1,0:T(1,128)S(1)} %convert_element_type.281) | copy-start | bytes 24580
  348.3 189.2 %all-to-all-start = ((bf16[8,256,2048]{2,1,0:T(8,128)(2,1)}), bf16[8,256,2048]{2,1,0:T(8,128)(2,1)}, u32[]{:S(2)}, u32[]{:S(2)}) async-start(bf16[8,256,2048]{2,1,0:T(8,128)(2,1)} %bitcast.269), calls=%async_computation | async-start | bytes 16777216 | tf_op jit(solution)/shard_map/all_to_all | solution.py:193
  537.5 187.6 %all-to-all-start.2 = ((bf16[8,256,2048]{2,1,0:T(8,128)(2,1)}), bf16[8,256,2048]{2,1,0:T(8,128)(2,1)}, u32[]{:S(2)}, u32[]{:S(2)}) async-start(bf16[8,256,2048]{2,1,0:T(8,128)(2,1)} %bitcast.270), calls=%async_computation.2 | async-start | bytes 16777216 | tf_op jit(solution)/shard_map/all_to_all | solution.py:194
  542.5 67.2 %all-gather.19.cloned.1.call-start = ((), (), s32[]{:S(2)}) async-start(), calls=%async_computation.16 | async-start | bytes 10485760 | tf_op jit(solution)/shard_map/all_gather | solution.py:201
  769.1 187.0 %all-to-all-start.1 = ((bf16[8,256,2048]{2,1,0:T(8,128)(2,1)}), bf16[8,256,2048]{2,1,0:T(8,128)(2,1)}, u32[]{:S(2)}, u32[]{:S(2)}) async-start(bf16[8,256,2048]{2,1,0:T(8,128)(2,1)} %bitcast.272), calls=%async_computation.1 | async-start | bytes 16777216 | tf_op jit(solution)/shard_map/all_to_all | solution.py:217
  956.1 187.3 %all-to-all-start.3 = ((bf16[8,256,2048]{2,1,0:T(8,128)(2,1)}), bf16[8,256,2048]{2,1,0:T(8,128)(2,1)}, u32[]{:S(2)}, u32[]{:S(2)}) async-start(bf16[8,256,2048]{2,1,0:T(8,128)(2,1)} %bitcast.271), calls=%async_computation.3 | async-start | bytes 16777216 | tf_op jit(solution)/shard_map/all_to_all | solution.py:220
  961.2 297.9 %reduce-scatter.8.cloned.1.call-start = ((), (), s32[]{:S(2)}) async-start(), calls=%async_computation.17 | async-start | bytes 5242880 | tf_op jit(solution)/shard_map/reduce_scatter | solution.py:271
  992.7 184.2 %copy-start.52 = (bf16[256,16]{0,1:T(8,128)(2,1)}, bf16[256,16]{0,1:T(8,128)(2,1)S(1)}, u32[]{:S(2)}) copy-start(bf16[256,16]{0,1:T(8,128)(2,1)S(1)} %multiply_convert_fusion.4) | copy-start | bytes 24580
  1216.2 90.1 %reduce-scatter.10.cloned.1.call-start = ((), (), s32[]{:S(2)}) async-start(), calls=%async_computation.18 | async-start | bytes 5242880 | tf_op jit(solution)/shard_map/reduce_scatter | solution.py:277
  1233.3 153.9 %reduce-scatter.14.cloned.1.call-start = ((), (), s32[]{:S(2)}) async-start(), calls=%async_computation.20 | async-start | bytes 10485760 | tf_op jit(solution)/shard_map/reduce_scatter | solution.py:308
  1241.1 324.2 %reduce-scatter.12.cloned.1.call-start = ((), (), s32[]{:S(2)}) async-start(), calls=%async_computation.19 | async-start | bytes 31457280 | tf_op jit(solution)/shard_map/reduce_scatter | solution.py:305
  1322.9 316.4 %reduce-scatter.20.cloned.1.call-start = ((), (), s32[]{:S(2)}) async-start(), calls=%async_computation.23 | async-start | bytes 10485760 | tf_op jit(solution)/shard_map/reduce_scatter | solution.py:212
  1338.5 325.5 %reduce-scatter.16.cloned.1.call-start = ((), (), s32[]{:S(2)}) async-start(), calls=%async_computation.21 | async-start | bytes 81920 | tf_op jit(solution)/shard_map/reduce_scatter | solution.py:311
  1373.2 416.0 %reduce-scatter.18.cloned.1.call-start = ((), (), s32[]{:S(2)}) async-start(), calls=%async_computation.22 | async-start | bytes 20971520 | tf_op jit(solution)/shard_map/reduce_scatter | solution.py:209
  1387.1 676.2 %all-reduce.14.cloned.1.call-start = ((), (), s32[]{:S(2)}) async-start(), calls=%async_computation.24 | async-start | bytes 16777216 | tf_op jit(solution)/shard_map/psum | solution.py:340
  1643.4 61.1 %copy-start.6 = (f32[256,2048]{1,0:T(8,128)S(1)}, f32[256,2048]{1,0:T(8,128)}, u32[]{:S(2)}) copy-start(f32[256,2048]{1,0:T(8,128)} %copy-done.4) | copy-start | bytes 6291460
  (85 other events, 895.8 us)
Sparse Core Ops, SparseCore 0:
  9.6 157.4 all-gather.8
  198.4 35.0 all-gather.12
  235.6 34.4 all-gather.10
  271.6 58.2 all-gather.14
  331.8 108.4 all-gather.16
  551.3 58.3 all-gather.18
  1216.3 42.7 reduce-scatter.7
  1261.7 44.5 reduce-scatter.9
  1309.4 71.3 reduce-scatter.13
  1383.3 181.8 reduce-scatter.11
  1567.8 71.4 reduce-scatter.19
  1642.1 19.5 reduce-scatter.15
  1664.3 124.8 reduce-scatter.17
  1793.2 269.9 all-reduce.13
where the time goes:
time: 2090 us; the launch traced here: 2080 us
  waiting for transfers between devices  1420 us (68%)
  matrix products  258 us (12%)
  local copies, waits for them, and re-layouts  168 us (8%)
  other arithmetic  124 us (6%)
  blocking collectives  68.8 us (3%)
  starting transfers between devices  30.2 us (1%)
    psum x1, waiting for transfers between devices, on_device(): lax.psum(shard_sums[0].astype(jnp.bfloat16), 'expert').astype(jnp.float32)  268 us
    reduce_scatter x1, waiting for transfers between devices, on_device(): lax.psum_scatter(qkv_grad.astype(jnp.bfloat16), 'shard', scatter_dimensio...  178 us
    all_to_all x1, waiting for transfers between devices, on_device(): lax.all_to_all(back_rows.reshape(send_shape), 'expert', split_axis=0, con...  151 us
    all_to_all x1, waiting for transfers between devices, on_device(): lax.all_to_all(send_rows, 'expert', split_axis=0, concat_axis=0, tiled=True)  141 us
    all_to_all x1, waiting for transfers between devices, on_device(): lax.all_to_all(back_out.reshape(send_shape), 'expert', split_axis=0, conc...  141 us
    all_gather x1, waiting for transfers between devices, on_device(): lax.all_gather(w_qkv, 'shard', axis=0, tiled=True)  140 us
    all_to_all x1, waiting for transfers between devices, on_device(): lax.all_to_all(send_cot, 'expert', split_axis=0, concat_axis=0, tiled=True)  115 us
    reduce_scatter x1, waiting for transfers between devices, on_device(): lax.psum_scatter(gate_up_part.astype(jnp.bfloat16), 'shard', scatter_dime...  81.1 us
  transfers between devices with their start and end apart: 18, of which 15 were waited for; matrix products, arithmetic and copies ran while one was open for 18% of the time, Pallas kernels for 0%

commit v1 on v0

v1 whole, which is shorter than its diff:
```python
import functools

import jax
import jax.numpy as jnp
from jax import lax
from jax.experimental import pallas as pl
from jax.experimental.pallas import tpu as pltpu
from jax.sharding import PartitionSpec as P

HEADS = 16
EPS = 1e-06
THETA = 50000.0
NEG_BIG = -1e30
F32 = jnp.float32
BF16 = jnp.bfloat16


def dot_f32(left, right, dims):
    return lax.dot_general(left, right, (dims, ((), ())), preferred_element_type=F32)


def rms_scale(values):
    return lax.rsqrt(jnp.mean(values * values, axis=-1, keepdims=True) + EPS)


def norm_back(grad_in, values, scale, gain):
    weighted = grad_in * gain
    return scale * weighted - values * scale**3 * jnp.mean(
        weighted * values, axis=-1, keepdims=True
    )


def ring_order(size):
    if size == 8:
        return [0, 2, 4, 6, 7, 5, 3, 1]
    return list(range(size))


def ring_perms(size):
    order = ring_order(size)
    ahead = [(order[i], order[(i + 1) % size]) for i in range(size)]
    return ahead, [(b, a) for a, b in ahead]


def ring_place(size):
    order = ring_order(size)
    places = [0] * size
    for place, index in enumerate(order):
        places[index] = place
    mine = jnp.array(places, jnp.int32)[lax.axis_index("expert")]
    source = jnp.array(order, jnp.int32)[
        jnp.mod(mine - jnp.arange(size, dtype=jnp.int32), size)
    ]
    return mine, source


def tied(value, *others):
    return lax.optimization_barrier((value, others))[0]


def ring_gather(block, size):
    ahead, back = ring_perms(size)
    half = block.shape[0] // 2
    blocks = [block] * size
    from_behind = from_ahead = block
    for step in range(1, size // 2):
        from_behind = lax.ppermute(from_behind, "expert", ahead)
        from_ahead = lax.ppermute(from_ahead, "expert", back)
        blocks[step] = from_behind
        blocks[size - step] = from_ahead
    top = lax.ppermute(from_behind[:half], "expert", ahead)
    bottom = lax.ppermute(from_ahead[half:], "expert", back)
    blocks[size // 2] = jnp.concatenate([top, bottom], axis=0)
    return blocks


def arrivals(size):
    order = [0]
    for step in range(1, size // 2):
        order += [step, size - step]
    return order + [size // 2]


def ring_scatter(pick, size):
    ahead, back = ring_perms(size)
    first = pick(size // 2)
    half = first.shape[0] // 2
    down = lax.ppermute(first[:half].astype(BF16), "expert", back)
    up = lax.ppermute(first[half:].astype(BF16), "expert", ahead)
    hops = [down]
    for step in range(size // 2 - 1, 0, -1):
        own_down, own_up = pick(step).astype(F32), pick(size - step).astype(F32)
        if step == size // 2 - 1:
            zeros = jnp.zeros_like(down)
            down = jnp.concatenate([down, zeros], axis=0)
            up = jnp.concatenate([zeros, up], axis=0)
        down = lax.ppermute((own_down + down.astype(F32)).astype(BF16), "expert", back)
        up = lax.ppermute((own_up + up.astype(F32)).astype(BF16), "expert", ahead)
        hops.append(down)
    return pick(0).astype(F32) + down.astype(F32) + up.astype(F32), hops


def swap(value, bit):
    size = lax.axis_size("shard")
    return lax.ppermute(value, "shard", [(i, i ^ bit) for i in range(size)])


def shard_gather(block):
    far = swap(block, 2)
    near = swap(block, 1)
    return [block, near, far, swap(far, 1)]


def shard_scatter(blocks):
    near = [swap(blocks[3].astype(BF16), 1), swap(blocks[1].astype(BF16), 1)]
    far = swap((blocks[2].astype(F32) + near[0].astype(F32)).astype(BF16), 2)
    return blocks[0].astype(F32) + near[1].astype(F32) + far.astype(F32)


def tree_sum(value, axis):
    size = lax.axis_size(axis)
    bit = 1
    while bit < size:
        value = value + lax.ppermute(value, axis, [(i, i ^ bit) for i in range(size)])
        bit *= 2
    return value


def turned(values, cosines, sines):
    return values * cosines + pltpu.roll(values, values.shape[-1] // 2, 1) * sines


def attention_kernel(scale, chunk, q_ref, k_ref, v_ref, cos_ref, sin_ref, col_ref, row_ref, gq_ref, gk_ref, out_ref):
    cosines, sines = cos_ref[...], sin_ref[...]
    q_pre, k_pre = q_ref[...], k_ref[...]
    query = turned(q_pre * rms_scale(q_pre) * gq_ref[...], cosines, sines).astype(BF16)
    key = turned(k_pre * rms_scale(k_pre) * gk_ref[...], cosines, sines).astype(BF16)
    value = v_ref[...].astype(BF16)
    docs = row_ref[...]
    for start in range(0, q_pre.shape[0], chunk):
        rows = slice(start, start + chunk)
        scores = dot_f32(query[rows], key, ((1,), (1,))) * scale
        scores = jnp.where(col_ref[rows, :] == docs, scores, NEG_BIG)
        shifted = jnp.exp(scores - jnp.max(scores, axis=-1, keepdims=True))
        probs = shifted * (1.0 / jnp.sum(shifted, axis=-1, keepdims=True))
        out_ref[rows, :] = dot_f32(probs.astype(BF16), value, ((1,), (0,))).astype(BF16)


def attention_back_kernel(
    scale, chunk, q_ref, k_ref, v_ref, do_ref, cos_ref, sin_ref, col_ref, row_ref, gq_ref, gk_ref,
    dq_ref, dk_ref, dv_ref, gains_ref, dq_acc, dk_acc, dv_acc,
):
    cosines, sines = cos_ref[...], sin_ref[...]
    q_pre, k_pre = q_ref[...], k_ref[...]
    q_scale, k_scale = rms_scale(q_pre), rms_scale(k_pre)
    query = turned(q_pre * q_scale * gq_ref[...], cosines, sines).astype(BF16)
    key = turned(k_pre * k_scale * gk_ref[...], cosines, sines).astype(BF16)
    value = v_ref[...].astype(BF16)
    docs = row_ref[...]
    for start in range(0, q_pre.shape[0], chunk):
        rows = slice(start, start + chunk)
        out_back = do_ref[rows, :]
        scores = dot_f32(query[rows], key, ((1,), (1,))) * scale
        scores = jnp.where(col_ref[rows, :] == docs, scores, NEG_BIG)
        shifted = jnp.exp(scores - jnp.max(scores, axis=-1, keepdims=True))
        probs = shifted * (1.0 / jnp.sum(shifted, axis=-1, keepdims=True))
        prob_back = dot_f32(out_back, value, ((1,), (1,)))
        score_back = (
            probs * (prob_back - jnp.sum(probs * prob_back, axis=-1, keepdims=True))
        ).astype(BF16)
        dq_acc[rows, :] = dot_f32(score_back, key, ((1,), (0,)))
        dk_part = dot_f32(score_back, query[rows], ((0,), (0,)))
        dv_part = dot_f32(probs.astype(BF16), out_back, ((0,), (0,)))
        if start == 0:
            dk_acc[...] = dk_part
            dv_acc[...] = dv_part
        else:
            dk_acc[...] += dk_part
            dv_acc[...] += dv_part
    dv_ref[...] = dv_acc[...].astype(BF16)

    @pl.when(pl.program_id(0) == 0)
    def _():
        gains_ref[...] = jnp.zeros_like(gains_ref)

    for place, (acc, pre, pre_scale, gain, out) in enumerate(
        (
            (dq_acc, q_pre, q_scale, gq_ref[...], dq_ref),
            (dk_acc, k_pre, k_scale, gk_ref[...], dk_ref),
        )
    ):
        grad = turned((acc[...] * scale).astype(BF16).astype(F32), cosines, -sines)
        gains_ref[place : place + 1, :] += jnp.sum(grad * pre * pre_scale, axis=0, keepdims=True)
        out[...] = norm_back(grad, pre, pre_scale, gain).astype(BF16)


def attention_specs(length, size, heads):
    def column(part):
        return pl.BlockSpec((length, size), lambda h: (0, part * heads + h))

    def whole(*shape):
        return pl.BlockSpec(shape, lambda h: (0, 0))

    pre = [column(0), column(1), column(2)]
    rest = [
        whole(length, size),
        whole(length, size),
        whole(length, 1),
        whole(1, length),
        whole(1, size),
        whole(1, size),
    ]
    return column(0), pre, rest


def attention(qkv_pre, tables, heads, size):
    length = qkv_pre.shape[0]
    own, pre, rest = attention_specs(length, size, heads)
    return pl.pallas_call(
        functools.partial(attention_kernel, size**-0.5, min(256, length)),
        grid=(heads,),
        in_specs=pre + rest,
        out_specs=own,
        out_shape=jax.ShapeDtypeStruct((length, heads * size), BF16),
        cost_estimate=pl.CostEstimate(
            flops=4 * heads * length * length * size,
            bytes_accessed=qkv_pre.size * 4 + length * heads * size * 2,
            transcendentals=heads * length * length,
        ),
        name="attention",
    )(qkv_pre, qkv_pre, qkv_pre, *tables)


def attention_back(qkv_pre, head_back, tables, heads, size):
    length = qkv_pre.shape[0]
    own, pre, rest = attention_specs(length, size, heads)
    shape = jax.ShapeDtypeStruct((length, heads * size), BF16)
    return pl.pallas_call(
        functools.partial(attention_back_kernel, size**-0.5, min(256, length)),
        grid=(heads,),
        in_specs=pre + [own] + rest,
        out_specs=[own, own, own, pl.BlockSpec((2, size), lambda h: (0, 0))],
        out_shape=[shape, shape, shape, jax.ShapeDtypeStruct((2, size), F32)],
        scratch_shapes=[pltpu.VMEM((length, size), F32)] * 3,
        cost_estimate=pl.CostEstimate(
            flops=10 * heads * length * length * size,
            bytes_accessed=qkv_pre.size * 4 + 4 * length * heads * size * 2,
            transcendentals=heads * length * length,
        ),
        name="attention_back",
    )(qkv_pre, qkv_pre, qkv_pre, head_back, *tables)


GROUP = 4
VMEM_BYTES = 60 * 1024 * 1024


def expert_kernel(count, base_ref, *refs):
    x_refs, dy_refs = refs[:count], refs[count : 2 * count]
    slot_ref, router_ref, wg_ref, wu_ref, wd_ref = refs[2 * count : 2 * count + 5]
    rin_ref, rcot_ref, act_ref, gb_ref, ub_ref, terms_ref, rback_ref = refs[
        2 * count + 5 : 2 * count + 12
    ]
    acc_ref, sum_ref, weight_ref, gg_ref = refs[2 * count + 12 :]
    expert, part = pl.program_id(0), pl.program_id(1)
    tokens = x_refs[0].shape[0]
    slots = rin_ref.shape[1] // count

    def pick_of(block):
        places = lax.broadcasted_iota(jnp.int32, (slots, tokens), 0)
        return places == slot_ref[0, block : block + 1, :]

    def low(mask):
        return jnp.where(mask, 1.0, 0.0).astype(BF16)

    @pl.when(part == 0)
    def _():
        mine = base_ref[0] + expert
        for block in range(count):
            rows = pl.ds(block * slots, slots)
            pick = pick_of(block)
            pick_low = low(pick)
            x_block = x_refs[block][...]
            rin_ref[0, rows, :] = dot_f32(pick_low, x_block, ((1,), (0,))).astype(BF16)
            rcot_ref[0, rows, :] = dot_f32(
                pick_low, dy_refs[block][...], ((1,), (0,))
            ).astype(BF16)
            logits = dot_f32(router_ref[...], x_block, ((1,), (1,)))
            powers = jnp.exp(logits - jnp.max(logits, axis=0, keepdims=True))
            router = powers / jnp.sum(powers, axis=0, keepdims=True)
            which = lax.broadcasted_iota(jnp.int32, router.shape, 0)
            gate = jnp.sum(jnp.where(which == mine, router, 0.0), axis=0, keepdims=True)
            weight_ref[rows, :] = jnp.sum(
                jnp.where(pick, gate, 0.0), axis=1, keepdims=True
            )

    rows_in, rows_cot = rin_ref[0], rcot_ref[0]
    w_gate, w_up, w_back = wg_ref[0, 0], wu_ref[0, 0], wd_ref[0, 0]
    weight = weight_ref[...]
    pre_gate = dot_f32(rows_in, w_gate, ((1,), (0,)))
    pre_up = dot_f32(rows_in, w_up, ((1,), (0,)))
    cot_down = dot_f32(rows_cot, w_back, ((1,), (1,)))
    sigmoid = jax.nn.sigmoid(pre_gate)
    silu = pre_gate * sigmoid
    act = silu * pre_up
    share = act * cot_down
    folded = share[:, :128]
    for lane in range(128, share.shape[1], 128):
        folded = folded + share[:, lane : lane + 128]
    act_back = weight * cot_down
    gate_back = (act_back * pre_up * (sigmoid + silu * (1.0 - sigmoid))).astype(BF16)
    up_back = (act_back * silu).astype(BF16)
    act_ref[0] = (weight * act).astype(BF16)
    gb_ref[0] = gate_back
    ub_ref[0] = up_back
    back = dot_f32(gate_back, w_gate, ((1,), (1,))) + dot_f32(up_back, w_up, ((1,), (1,)))

    @pl.when(part == 0)
    def _():
        gg_ref[...] = folded
        acc_ref[...] = back

    @pl.when(part > 0)
    def _():
        gg_ref[...] += folded
        acc_ref[...] += back

    @pl.when(part == pl.num_programs(1) - 1)
    def _():
        for block in range(count):
            rows = pl.ds(block * slots, slots)
            pick = pick_of(block)
            share = jnp.sum(gg_ref[rows, :], axis=1, keepdims=True)
            rback_ref[0, block : block + 1, :] = jnp.sum(
                jnp.where(pick, share, 0.0), axis=0, keepdims=True
            )
            term = dot_f32(low(pick), acc_ref[rows, :].astype(BF16), ((0,), (0,)))

            @pl.when(expert == 0)
            def _():
                sum_ref[block] = term

            @pl.when(expert > 0)
            def _():
                sum_ref[block] += term

            @pl.when(expert == pl.num_programs(0) - 1)
            def _():
                terms_ref[block] = sum_ref[block].astype(BF16)


def weight_spec(shape):
    return pl.BlockSpec((1, 1) + shape[2:], lambda e, j: (j, e, 0, 0))


def expert_group(base, x_blocks, dy_blocks, slot_of, router_rows, w_gate, w_up, w_down, slots):
    count = len(x_blocks)
    tokens, width = x_blocks[0].shape
    parts, experts, hidden = w_down.shape[:3]
    rows = count * slots

    def still(shape):
        return pl.BlockSpec(
            shape, lambda e, j: (0,) * len(shape), pipeline_mode=pl.Buffered(1)
        )

    def per_expert(*shape):
        return pl.BlockSpec((1,) + shape, lambda e, j: (e, 0, 0))

    part = pl.BlockSpec((1, rows, hidden), lambda e, j: (e, 0, j))
    wide = jax.ShapeDtypeStruct((experts, rows, width), BF16)
    deep = jax.ShapeDtypeStruct((experts, rows, parts * hidden), BF16)
    flops = 10 * rows * width * parts * hidden * experts
    return pl.pallas_call(
        functools.partial(expert_kernel, count),
        grid=(experts, parts),
        in_specs=[pl.BlockSpec(memory_space=pltpu.SMEM)]
        + [still((tokens, width))] * (2 * count)
        + [
            per_expert(count, tokens),
            still(router_rows.shape),
            weight_spec(w_gate.shape),
            weight_spec(w_up.shape),
            weight_spec(w_down.shape),
        ],
        out_specs=[
            per_expert(rows, width),
            per_expert(rows, width),
            part,
            part,
            part,
            pl.BlockSpec(
                (count, tokens, width), lambda e, j: (0, 0, 0), pipeline_mode=pl.Buffered(1)
            ),
            per_expert(count, tokens),
        ],
        out_shape=[
            wide,
            wide,
            deep,
            deep,
            deep,
            jax.ShapeDtypeStruct((count, tokens, width), BF16),
            jax.ShapeDtypeStruct((experts, count, tokens), F32),
        ],
        scratch_shapes=[
            pltpu.VMEM((rows, width), F32),
            pltpu.VMEM((count, tokens, width), F32),
            pltpu.VMEM((rows, 1), F32),
            pltpu.VMEM((rows, 128), F32),
        ],
        compiler_params=pltpu.CompilerParams(vmem_limit_bytes=VMEM_BYTES),
        cost_estimate=pl.CostEstimate(
            flops=flops, bytes_accessed=6 * w_gate.size, transcendentals=rows * parts * hidden
        ),
        name="experts",
    )(base, *x_blocks, *dy_blocks, slot_of, router_rows, w_gate, w_up, w_down)


def output_kernel(count, slot_ref, act_ref, wd_ref, terms_ref, acc_ref, sum_ref):
    expert, part = pl.program_id(0), pl.program_id(1)
    tokens = terms_ref.shape[1]
    slots = act_ref.shape[1] // count
    out = dot_f32(act_ref[0], wd_ref[0, 0], ((1,), (0,)))

    @pl.when(part == 0)
    def _():
        acc_ref[...] = out

    @pl.when(part > 0)
    def _():
        acc_ref[...] += out

    @pl.when(part == pl.num_programs(1) - 1)
    def _():
        for block in range(count):
            places = lax.broadcasted_iota(jnp.int32, (slots, tokens), 0)
            pick = jnp.where(places == slot_ref[0, block : block + 1, :], 1.0, 0.0).astype(BF16)
            rows = acc_ref[pl.ds(block * slots, slots), :].astype(BF16)
            term = dot_f32(pick, rows, ((0,), (0,)))

            @pl.when(expert == 0)
            def _():
                sum_ref[block] = term

            @pl.when(expert > 0)
            def _():
                sum_ref[block] += term

            @pl.when(expert == pl.num_programs(0) - 1)
            def _():
                terms_ref[block] = sum_ref[block].astype(BF16)


def expert_output(slot_of, act, w_down):
    experts, count, tokens = slot_of.shape
    parts, _, hidden, width = w_down.shape
    rows = act.shape[1]
    return pl.pallas_call(
        functools.partial(output_kernel, count),
        grid=(experts, parts),
        in_specs=[
            pl.BlockSpec((1, count, tokens), lambda e, j: (e, 0, 0)),
            pl.BlockSpec((1, rows, hidden), lambda e, j: (e, 0, j)),
            weight_spec(w_down.shape),
        ],
        out_specs=pl.BlockSpec((count, tokens, width), lambda e, j: (0, 0, 0)),
        out_shape=jax.ShapeDtypeStruct((count, tokens, width), BF16),
        scratch_shapes=[
            pltpu.VMEM((rows, width), F32),
            pltpu.VMEM((count, tokens, width), F32),
        ],
        compiler_params=pltpu.CompilerParams(vmem_limit_bytes=VMEM_BYTES),
        cost_estimate=pl.CostEstimate(
            flops=2 * rows * width * parts * hidden * experts,
            bytes_accessed=2 * (w_down.size + act.size + count * tokens * width),
            transcendentals=0,
        ),
        name="expert_output",
    )(slot_of, act, w_down)


def grad_kernel(groups, *refs):
    total = None
    for left, right in zip(refs[:groups], refs[groups : 2 * groups]):
        part = dot_f32(left[0], right[0], ((0,), (0,)))
        total = part if total is None else total + part
    refs[-1][0, 0] = total.astype(BF16)


def expert_grad(lefts, rights, parts):
    experts = lefts[0].shape[0]
    hidden = min(lefts[0].shape[2], rights[0].shape[2]) // parts

    def spec(array, cut):
        width = hidden if cut else array.shape[2]
        return pl.BlockSpec(
            (1, array.shape[1], width), lambda e, j: (e, 0, j if cut else 0)
        )

    cut_left = lefts[0].shape[2] < rights[0].shape[2]
    shape = (
        hidden if cut_left else lefts[0].shape[2],
        rights[0].shape[2] if cut_left else hidden,
    )
    rows = sum(left.shape[1] for left in lefts)
    return pl.pallas_call(
        functools.partial(grad_kernel, len(lefts)),
        grid=(experts, parts),
        in_specs=[spec(left, cut_left) for left in lefts]
        + [spec(right, not cut_left) for right in rights],
        out_specs=pl.BlockSpec((1, 1) + shape, lambda e, j: (j, e, 0, 0)),
        out_shape=jax.ShapeDtypeStruct((parts, experts) + shape, BF16),
        compiler_params=pltpu.CompilerParams(vmem_limit_bytes=VMEM_BYTES),
        cost_estimate=pl.CostEstimate(
            flops=2 * rows * shape[0] * shape[1] * parts * experts,
            bytes_accessed=2 * experts * (parts * shape[0] * shape[1] + 3 * rows * shape[0]),
            transcendentals=0,
        ),
        name="expert_grad",
    )(*lefts, *rights)


def on_device(
    tokens,
    out_grad,
    routes,
    segments,
    capacity,
    attn_gain,
    w_qkv,
    query_gain,
    key_gain,
    w_out,
    ffn_gain,
    w_router,
    w_gate_up,
    w_down,
):
    n_expert = lax.axis_size("expert")
    n_shard = lax.axis_size("shard")
    rows, width = tokens.shape
    size = width // HEADS
    heads = HEADS // n_shard
    local_width = heads * size
    length = segments.shape[0]
    expert_count = capacity.shape[0]
    local_experts = w_down.shape[0]
    slots = rows * routes.shape[1] // expert_count
    shard_index = lax.axis_index("shard")
    expert_index = lax.axis_index("expert")
    place, source = ring_place(n_expert)
    part_rows = w_qkv.shape[0]
    slice_rows = part_rows // n_expert
    relative = jnp.bitwise_xor(shard_index, jnp.arange(n_shard, dtype=jnp.int32))

    packed = jnp.concatenate(
        [attn_gain, ffn_gain, query_gain, key_gain, w_router.reshape(-1)]
    )
    packed = lax.all_to_all(
        jnp.broadcast_to(packed[None], (n_shard, packed.shape[0])), "shard", 0, 0, tiled=True
    )
    cuts = [part_rows, 2 * part_rows, 2 * part_rows + size // n_shard]
    cuts.append(cuts[-1] + size // n_shard)
    gain_one = packed[:, : cuts[0]].reshape(1, width).astype(F32)
    gain_two = packed[:, cuts[0] : cuts[1]].reshape(1, width).astype(F32)
    gain_query = packed[:, cuts[1] : cuts[2]].reshape(1, size).astype(F32)
    gain_key = packed[:, cuts[2] : cuts[3]].reshape(1, size).astype(F32)
    full_router = packed[:, cuts[3] :].reshape(width, expert_count)
    router_rows = full_router.T

    own_slice = lax.dynamic_slice_in_dim(w_qkv, expert_index * slice_rows, slice_rows)
    own_slice = own_slice.reshape(slice_rows, 3, n_shard, local_width).transpose(2, 0, 1, 3)
    own_slice = lax.all_to_all(
        own_slice.reshape(n_shard, slice_rows, 3 * local_width), "shard", 0, 0, tiled=True
    )
    w_blocks = ring_gather(
        own_slice.reshape(n_shard * slice_rows, 3 * local_width), n_expert
    )
    w_local = jnp.zeros((n_shard, n_expert, slice_rows, 3 * local_width), BF16)
    for r in arrivals(n_expert):
        w_local = lax.dynamic_update_slice(
            w_local,
            w_blocks[r].reshape(n_shard, 1, slice_rows, 3 * local_width),
            (0, source[r], 0, 0),
        )
    w_local = w_local.reshape(width, 3 * local_width)

    token_parts = shard_gather(tokens)
    token_blocks = jnp.concatenate(token_parts, axis=0)

    dy_blocks = ring_gather(tied(out_grad, w_blocks[n_expert // 2]), n_expert)
    routes_all = lax.all_to_all(
        jnp.broadcast_to(routes[None], (n_expert,) + routes.shape), "expert", 0, 0, tiled=True
    )[source]

    gate_own, up_own = w_gate_up[:, 0], w_gate_up[:, 1]
    gate_full = jnp.stack(shard_gather(tied(gate_own, token_parts[2])))
    up_full = jnp.stack(shard_gather(tied(up_own, token_parts[2])))

    my_experts = expert_index * local_experts + jnp.arange(local_experts, dtype=jnp.int32)
    named = jnp.any(
        routes_all[None, :, :, :] == my_experts[:, None, None, None], axis=3
    )
    order = jnp.arange(rows, dtype=jnp.int32)
    before = (order[:, None] < order[None, :]).astype(BF16)
    earlier = jnp.einsum(
        "ebu,ut->ebt", named.astype(BF16), before, preferred_element_type=F32
    ).astype(jnp.int32)
    my_limits = lax.dynamic_slice_in_dim(capacity, expert_index * local_experts, local_experts)
    slot_of = jnp.where(named & (earlier < my_limits[:, None, None]), earlier, -1)

    position = (
        relative[:, None] * rows + jnp.arange(rows, dtype=jnp.int32)[None, :]
    ).reshape(-1).astype(F32)
    half_size = size // 2
    frequency = THETA ** (-(2.0 * jnp.arange(half_size, dtype=F32)) / size)
    angles = position[:, None] * frequency[None, :]
    cosines, sines = jnp.cos(angles), jnp.sin(angles)
    docs = segments.reshape(n_shard, rows)[relative].reshape(-1)
    tables = (
        jnp.concatenate([cosines, cosines], axis=1),
        jnp.concatenate([-sines, sines], axis=1),
        docs[:, None],
        docs[None, :],
        gain_query,
        gain_key,
    )

    token_float = token_blocks.astype(F32)
    scale_one = rms_scale(token_float)
    normed = (token_float * scale_one * gain_one).astype(BF16)
    qkv_pre = jnp.dot(normed, w_local, preferred_element_type=F32)
    mixed = attention(qkv_pre, tables, heads, size)
    attended = jnp.dot(mixed, w_out, preferred_element_type=F32).astype(BF16)
    own_tokens = tokens.astype(F32)
    hidden = own_tokens + shard_scatter(list(attended.reshape(n_shard, rows, width)))
    scale_two = rms_scale(hidden)
    ffn_low = (hidden * scale_two * gain_two).astype(BF16)
    router = jax.nn.softmax(
        jnp.dot(ffn_low, full_router, preferred_element_type=F32), axis=-1
    )
    down_full = jnp.stack(shard_gather(tied(w_down, ffn_low)))

    ffn_blocks = ring_gather(ffn_low, n_expert)
    arrival = arrivals(n_expert)
    groups = [arrival[i : i + GROUP] for i in range(0, n_expert, GROUP)]
    base = (expert_index * local_experts).reshape(1).astype(jnp.int32)
    results, slot_groups = [], []
    for group in groups:
        slot_groups.append(jnp.stack([slot_of[:, r] for r in group], axis=1))
        results.append(
            expert_group(
                base,
                [ffn_blocks[r] for r in group],
                [dy_blocks[r] for r in group],
                slot_groups[-1],
                router_rows,
                gate_full,
                up_full,
                down_full,
                slots,
            )
        )
    rows_in, rows_cot, act, gate_back, up_back, terms, router_terms = map(list, zip(*results))
    where_is = {r: (g, i) for g, group in enumerate(groups) for i, r in enumerate(group)}

    def picker(arrays):
        return lambda r: arrays[where_is[r][0]][where_is[r][1]]

    ffn_back, hops = ring_scatter(picker(terms), n_expert)
    to_block = jnp.zeros((n_expert,), jnp.int32).at[source].set(
        jnp.arange(n_expert, dtype=jnp.int32)
    )
    back_to = jnp.stack(
        [router_terms[where_is[r][0]][:, where_is[r][1]] for r in range(n_expert)]
    )
    router_back = lax.all_to_all(
        back_to[to_block], "expert", split_axis=0, concat_axis=0, tiled=True
    ).reshape(expert_count, rows).T

    gate_parts = expert_grad(rows_in, gate_back, n_shard)
    gate_grads = shard_scatter(list(gate_parts))
    up_parts = expert_grad(tied(rows_in, hops[0]), up_back, n_shard)
    up_grads = shard_scatter(list(up_parts))
    down_parts = expert_grad(tied(act, hops[1]), rows_cot, n_shard)
    out_terms = [
        expert_output(slots_g, tied(act_g, hops[2]), down_full)
        for slots_g, act_g in zip(slot_groups, act)
    ]
    out_terms[-1] = tied(out_terms[-1], ffn_back)
    out_sum, _ = ring_scatter(picker(out_terms), n_expert)
    layer_out = (hidden + out_sum).astype(BF16)

    logit_back = (
        router * (router_back - jnp.sum(router * router_back, axis=-1, keepdims=True))
    ).astype(BF16)
    router_grad = dot_f32(ffn_low, logit_back, ((0,), (0,)))
    ffn_back = ffn_back + dot_f32(logit_back, full_router, ((1,), (1,)))
    gain_two_part = jnp.sum(ffn_back * hidden * scale_two, axis=0)
    hidden_back = out_grad.astype(F32) + norm_back(ffn_back, hidden, scale_two, gain_two)

    mix_back = jnp.concatenate(shard_gather(hidden_back.astype(BF16)), axis=0)
    down_grad = shard_scatter(list(tied(down_parts, mix_back)))
    head_back = dot_f32(mix_back, w_out, ((1,), (1,))).astype(BF16)
    out_part = dot_f32(mixed, mix_back, ((0,), (0,))).astype(BF16)
    query_back, key_back, value_back, head_gains = attention_back(
        qkv_pre, head_back, tables, heads, size
    )
    qkv_back = jnp.concatenate([query_back, key_back, value_back], axis=1)
    qkv_part = dot_f32(normed, qkv_back, ((0,), (0,))).astype(BF16)
    normed_back = dot_f32(tied(qkv_back, qkv_part), w_local, ((1,), (1,)))
    gain_one_part = jnp.sum(normed_back * token_float * scale_one, axis=0)
    own_back = shard_scatter(list(normed_back.astype(BF16).reshape(n_shard, rows, width)))
    tokens_grad = hidden_back + norm_back(own_back, own_tokens, scale_one[:rows], gain_one)

    def placed_blocks(blocks):
        total = jnp.zeros((n_expert * blocks[0].shape[0], blocks[0].shape[1]), F32)
        for r in arrivals(n_expert):
            total = lax.dynamic_update_slice(
                total, blocks[r].astype(F32), (source[r] * blocks[r].shape[0], 0)
            )
        return total

    out_terms_w = out_part.reshape(n_expert, slice_rows, width)
    out_mine, _ = ring_scatter(
        lambda r: lax.dynamic_index_in_dim(out_terms_w, source[r], 0, keepdims=False), n_expert
    )
    out_total = placed_blocks(ring_gather(out_mine.astype(BF16), n_expert))
    qkv_terms = qkv_part.reshape(n_shard, n_expert, slice_rows, 3 * local_width)
    qkv_mine, _ = ring_scatter(
        lambda r: lax.dynamic_index_in_dim(qkv_terms, source[r], 1, keepdims=False).reshape(
            n_shard * slice_rows, 3 * local_width
        ),
        n_expert,
    )
    qkv_mine = lax.all_to_all(
        qkv_mine.astype(BF16), "shard", split_axis=0, concat_axis=0, tiled=True
    )
    qkv_mine = (
        qkv_mine.reshape(n_shard, slice_rows, 3, local_width)
        .transpose(1, 2, 0, 3)
        .reshape(slice_rows, 3 * width)
    )
    qkv_total = placed_blocks(ring_gather(qkv_mine, n_expert))

    small = jnp.concatenate(
        [
            gain_one_part.reshape(n_shard, -1),
            gain_two_part.reshape(n_shard, -1),
            head_gains[0].reshape(n_shard, -1),
            head_gains[1].reshape(n_shard, -1),
            router_grad.reshape(n_shard, -1),
        ],
        axis=1,
    )
    small = lax.all_to_all(small, "shard", split_axis=0, concat_axis=0, tiled=True)
    small = tree_sum(jnp.sum(small, axis=0).reshape(1, -1), "expert")[0]
    gate_up_grad = jnp.stack([gate_grads, up_grads], axis=1)
    return (
        layer_out,
        tokens_grad,
        small[: cuts[0]],
        qkv_total,
        small[cuts[1] : cuts[2]],
        small[cuts[2] : cuts[3]],
        out_total,
        small[cuts[0] : cuts[1]],
        small[cuts[3] :].reshape(part_rows, expert_count),
        gate_up_grad,
        down_grad,
    )


def solution(mesh):
    placed = (
        P(("expert", "shard"), None),
        P(("expert", "shard"), None),
        P(("expert", "shard"), None),
        P("expert"),
        P(),
        P("shard"),
        P("shard", None),
        P("shard"),
        P("shard"),
        P("shard", None),
        P("shard"),
        P("shard", None),
        P("expert", None, None, "shard"),
        P("expert", "shard", None),
    )
    return jax.shard_map(
        on_device,
        mesh=mesh,
        in_specs=placed,
        out_specs=(
            P(("expert", "shard"), None),
            P(("expert", "shard"), None),
            P("shard"),
            P("shard", None),
            P("shard"),
            P("shard"),
            P("shard", None),
            P("shard"),
            P("shard", None),
            P("expert", None, None, "shard"),
            P("expert", "shard", None),
        ),
        check_vma=False,
    )
```

time: 2090 us -> 1160 us (0.56)
  waiting for transfers between devices: 1420 us -> 489 us
  Pallas kernels: 0 us -> 262 us
  matrix products: 258 us -> 49 us
  starting transfers between devices: 30.2 us -> 127 us
  local copies, waits for them, and re-layouts: 168 us -> 93.9 us
  blocking collectives: 68.8 us -> 0 us
    all_to_all x4 -> x6, waiting for transfers between devices: 548 us -> 19.9 us  [the longest x1 9.99 us: on_device(): lax.all_to_all(qkv_mine.astype(BF16), 'shard', split_axis=0, concat_axis=...]
    ppermute x0 -> x105, waiting for transfers between devices: none -> 469 us  [the longest x30 158 us: swap(): return lax.ppermute(value, 'shard', [(i, i ^ bit) for i in range(size)])]
    reduce_scatter x7 -> x0, waiting for transfers between devices: 353 us -> none  [the longest x1 178 us: on_device(): lax.psum_scatter(qkv_grad.astype(jnp.bfloat16), 'shard', scatter_dimensio...]
    psum x1 -> x0, waiting for transfers between devices: 268 us -> none  [on_device(): lax.psum(shard_sums[0].astype(jnp.bfloat16), 'expert').astype(jnp.float32)]
    pallas_call x0 -> x9, Pallas kernels: none -> 262 us  [the longest x2 127 us: expert_group(): pl.pallas_call(functools.partial(expert_kernel, count), grid=(experts, pa...]
    all_gather x6 -> x0, waiting for transfers between devices: 245 us -> none  [the longest x1 140 us: on_device(): lax.all_gather(w_qkv, 'shard', axis=0, tiled=True)]
    dot_general x24 -> x10, matrix products: 258 us -> 49 us  [the longest x6 32.5 us: dot_f32(): lax.dot_general(left, right, (dims, ((), ())), preferred_element_type=F32)]
    ppermute x0 -> x105, starting transfers between devices: none -> 101 us  [the longest x15 29 us: ring_gather(): from_behind = lax.ppermute(from_behind, 'expert', ahead)]
  transfers between devices with their start and end apart: 18 -> 111, of which waited for: 15 -> 46; matrix products, arithmetic and copies ran while one was open for 18% -> 17% of each run, Pallas kernels for 0% -> 14%
where the time goes in v1:
time: 1160 us
  waiting for transfers between devices  489 us (42%)
  Pallas kernels  262 us (23%)
  starting transfers between devices  127 us (11%)
  other arithmetic  112 us (10%)
  local copies, waits for them, and re-layouts  93.9 us (8%)
  matrix products  49 us (4%)
  between operations  22.3 us (2%)
    ppermute x30, waiting for transfers between devices, swap(): return lax.ppermute(value, 'shard', [(i, i ^ bit) for i in range(size)])  158 us
    pallas_call x2, Pallas kernels, expert_group(): pl.pallas_call(functools.partial(expert_kernel, count), grid=(experts, pa...  127 us
    ppermute x15, waiting for transfers between devices, ring_gather(): from_ahead = lax.ppermute(from_ahead, 'expert', back)  124 us
    ppermute x15, waiting for transfers between devices, ring_gather(): from_behind = lax.ppermute(from_behind, 'expert', ahead)  65 us
    pallas_call x3, Pallas kernels, expert_grad(): pl.pallas_call(functools.partial(grad_kernel, len(lefts)), grid=(experts,...  48.6 us
    ppermute x12, waiting for transfers between devices, ring_scatter(): up = lax.ppermute((own_up + up.astype(F32)).astype(BF16), 'expert', ahead)  48.5 us
    pallas_call x2, Pallas kernels, expert_output(): pl.pallas_call(functools.partial(output_kernel, count), grid=(experts, pa...  36.2 us
    dot_general x6, matrix products, dot_f32(): lax.dot_general(left, right, (dims, ((), ())), preferred_element_type=F32)  32.5 us
  transfers between devices with their start and end apart: 111, of which 46 were waited for; matrix products, arithmetic and copies ran while one was open for 17% of the time, Pallas kernels for 14%

profile of v1, /device:TPU:0, one launch (start us, length us, event | category | flops | bytes accessed | tf_op | source)
XLA Modules:
  0.0 1155.3 jit_solution(2124226582329368100)
XLA Ops:
  87.7 14.6 %collective-permute-done.7 = bf16[256,1536]{1,0:T(8,128)(2,1)S(1)} collective-permute-done((bf16[256,1536]{1,0:T(8,128)(2,1)S(1)}, bf16[256,1536]{1,0:T(8,128)(2,1)S(1)}, u32[]{:S(2)}, u32[]{:S(2)}) %collective-permute-start.7) | collective-permute-done | bytes 786464 | tf_op jit(solution)/shard_map/ppermute | solution.py:67
  126.8 18.8 %attention.1 = bf16[1024,512]{1,0:T(8,128)(2,1)} custom-call(f32[1024,1536]{1,0:T(8,128)} %fusion.42.q_ref.k_ref.v_ref, f32[1024,1536]{1,0:T(8,128)} %fusion.42.q_ref.k_ref.v_ref, f32[1024,1536]{1,0:T(8,128)} %fusion.42.q_ref.k_ref.v_ref, f32[1024,128]{1,0:T(8,128)} %get-tuple-element.230.cos_ref, f32[1024,128]{1,0:T(8,128)} %get-tuple-element.231.sin_ref, ...), custom_call_target="tpu_custom_call" | custom-call | flops 2147483648 | bytes 7340032 | tf_op jit(solution)/shard_map/attention/pallas_call | solution.py:219
  155.6 19.5 %collective-permute-done.18.refs_6_ = bf16[256,2048]{1,0:T(8,128)(2,1)S(1)} collective-permute-done((bf16[256,2048]{1,0:T(8,128)(2,1)S(1)}, bf16[256,2048]{1,0:T(8,128)(2,1)S(1)}, u32[]{:S(2)}, u32[]{:S(2)}) %collective-permute-start.18) | collective-permute-done | bytes 1048608 | tf_op jit(solution)/shard_map/ppermute | solution.py:68
  184.5 38.4 %collective-permute-done.24 = bf16[2,2048,256]{2,1,0:T(8,128)(2,1)S(1)} collective-permute-done((bf16[2,2048,256]{2,1,0:T(8,128)(2,1)S(1)}, bf16[2,2048,256]{2,1,0:T(8,128)(2,1)S(1)}, u32[]{:S(2)}, u32[]{:S(2)}) %collective-permute-start.24) | collective-permute-done | bytes 2097184 | tf_op jit(solution)/shard_map/ppermute | solution.py:105
  228.8 20.3 %collective-permute-done.15.refs_2_ = bf16[256,2048]{1,0:T(8,128)(2,1)} collective-permute-done((bf16[256,2048]{1,0:T(8,128)(2,1)S(1)}, bf16[256,2048]{1,0:T(8,128)(2,1)}, u32[]{:S(2)}, u32[]{:S(2)}) %collective-permute-start.15) | collective-permute-done | bytes 1048608 | tf_op jit(solution)/shard_map/ppermute | solution.py:68
  257.2 14.4 %collective-permute-done.36.refs_6_ = bf16[256,2048]{1,0:T(8,128)(2,1)} collective-permute-done((bf16[256,2048]{1,0:T(8,128)(2,1)}, bf16[256,2048]{1,0:T(8,128)(2,1)}, u32[]{:S(2)}, u32[]{:S(2)}) %collective-permute-start.36) | collective-permute-done | bytes 1048608 | tf_op jit(solution)/shard_map/ppermute | solution.py:68
  273.1 19.6 %collective-permute-done.29.refs_0_ = bf16[256,2048]{1,0:T(8,128)(2,1)} collective-permute-done((bf16[256,2048]{1,0:T(8,128)(2,1)}, bf16[256,2048]{1,0:T(8,128)(2,1)}, u32[]{:S(2)}, u32[]{:S(2)}) %collective-permute-start.29) | collective-permute-done | bytes 1048608 | tf_op jit(solution)/shard_map/ppermute | solution.py:68
  357.5 63.3 %experts.3 = (bf16[2,512,2048]{2,1,0:T(8,128)(2,1)}, bf16[2,512,2048]{2,1,0:T(8,128)(2,1)}, bf16[2,512,1024]{2,1,0:T(8,128)(2,1)}, bf16[2,512,1024]{2,1,0:T(8,12...) custom-call(s32[1]{0:T(128)} %bitcast.26.base_ref, ...), custom_call_target="tpu_custom_call" | custom-call | flops 21474836480 | bytes 25165824 | tf_op jit(solution)/shard_map/experts/pallas_call | solution.py:374
  436.5 63.3 %experts.2 = (bf16[2,512,2048]{2,1,0:T(8,128)(2,1)}, bf16[2,512,2048]{2,1,0:T(8,128)(2,1)}, bf16[2,512,1024]{2,1,0:T(8,128)(2,1)}, bf16[2,512,1024]{2,1,0:T(8,12...) custom-call(s32[1]{0:T(128)} %bitcast.26.base_ref, ...), custom_call_target="tpu_custom_call" | custom-call | flops 21474836480 | bytes 25165824 | tf_op jit(solution)/shard_map/experts/pallas_call | solution.py:374
  510.7 16.4 %expert_grad.3 = bf16[4,2,2048,256]{3,2,1,0:T(8,128)(2,1)} custom-call(bf16[2,512,2048]{2,1,0:T(8,128)(2,1)} %get-tuple-element.64.refs_0_, bf16[2,512,2048]{2,1,0:T(8,128)(2,1)} %get-tuple-element.65.refs_1_, bf16[2,512,1024]{2,1,0:T(8,128)(2,1)} %get-tuple-element.62.refs_2_, bf16[2,512,1024]{2,1,0:T(8,128)(2,1)} %get-tuple-element.63.refs_3_), custom_call_target="tpu_custom_call" | custom-call | flops 8589934592 | bytes 33554432 | tf_op jit(solution)/shard_map/expert_grad/pallas_call | solution.py:507
  556.8 16.4 %expert_grad.4 = bf16[4,2,2048,256]{3,2,1,0:T(8,128)(2,1)} custom-call(bf16[2,512,2048]{2,1,0:T(8,128)(2,1)} %get-tuple-element.64.refs_0_, bf16[2,512,2048]{2,1,0:T(8,128)(2,1)} %get-tuple-element.65.refs_1_, bf16[2,512,1024]{2,1,0:T(8,128)(2,1)} %get-tuple-element.66.refs_2_, bf16[2,512,1024]{2,1,0:T(8,128)(2,1)} %get-tuple-element.67.refs_3_), custom_call_target="tpu_custom_call" | custom-call | flops 8589934592 | bytes 33554432 | tf_op jit(solution)/shard_map/expert_grad/pallas_call | solution.py:507
  573.2 18.1 %expert_output.3 = bf16[4,256,2048]{2,1,0:T(8,128)(2,1)} custom-call(s32[2,4,256]{2,1,0:T(4,128)} %pad_add_fusion.1.refs_8_.slot_ref, bf16[2,512,1024]{2,1,0:T(8,128)(2,1)} %get-tuple-element.69.act_ref.refs_1_, bf16[4,2,256,2048]{3,2,1,0:T(8,128)(2,1)} %pad_maximum_fusion.2.refs_12_.wd_ref), custom_call_target="tpu_custom_call" | custom-call | flops 4294967296 | bytes 14680064 | tf_op jit(solution)/shard_map/expert_output/pallas_call | solution.py:459
  608.2 15.8 %expert_grad.5 = bf16[4,2,256,2048]{3,2,1,0:T(8,128)(2,1)} custom-call(bf16[2,512,1024]{2,1,0:T(8,128)(2,1)} %get-tuple-element.68.act_ref.refs_0_, bf16[2,512,1024]{2,1,0:T(8,128)(2,1)} %get-tuple-element.69.act_ref.refs_1_, bf16[2,512,2048]{2,1,0:T(8,128)(2,1)} %get-tuple-element.70.refs_2_, bf16[2,512,2048]{2,1,0:T(8,128)(2,1)} %get-tuple-element.71.refs_3_), custom_call_target="tpu_custom_call" | custom-call | flops 8589934592 | bytes 11534336 | tf_op jit(solution)/shard_map/expert_grad/pallas_call | solution.py:507
  629.1 18.1 %expert_output.2 = bf16[4,256,2048]{2,1,0:T(8,128)(2,1)} custom-call(s32[2,4,256]{2,1,0:T(4,128)} %pad_add_fusion.refs_8_.slot_ref, bf16[2,512,1024]{2,1,0:T(8,128)(2,1)} %get-tuple-element.68.act_ref.refs_0_, bf16[4,2,256,2048]{3,2,1,0:T(8,128)(2,1)} %pad_maximum_fusion.2.refs_12_.wd_ref), custom_call_target="tpu_custom_call" | custom-call | flops 4294967296 | bytes 14680064 | tf_op jit(solution)/shard_map/expert_output/pallas_call | solution.py:459
  660.4 14.5 %collective-permute-done.49 = bf16[256,2048]{1,0:T(8,128)(2,1)S(1)} collective-permute-done((bf16[256,2048]{1,0:T(8,128)(2,1)S(1)}, bf16[256,2048]{1,0:T(8,128)(2,1)S(1)}, u32[]{:S(2)}, u32[]{:S(2)}) %collective-permute-start.49) | collective-permute-done | bytes 1048608 | tf_op jit(solution)/shard_map/ppermute | solution.py:97
  686.8 16.8 %collective-permute-done.54 = bf16[256,2048]{1,0:T(8,128)(2,1)S(1)} collective-permute-done((bf16[256,2048]{1,0:T(8,128)(2,1)S(1)}, bf16[256,2048]{1,0:T(8,128)(2,1)S(1)}, u32[]{:S(2)}, u32[]{:S(2)}) %collective-permute-start.54) | collective-permute-done | bytes 1048608 | tf_op jit(solution)/shard_map/ppermute | solution.py:98
  707.6 15.8 %collective-permute-done.98 = bf16[2,2048,256]{2,1,0:T(8,128)(2,1)S(1)} collective-permute-done((bf16[2,2048,256]{2,1,0:T(8,128)(2,1)S(1)}, bf16[2,2048,256]{2,1,0:T(8,128)(2,1)S(1)}, u32[]{:S(2)}, u32[]{:S(2)}) %collective-permute-start.98) | collective-permute-done | bytes 2097184 | tf_op jit(solution)/shard_map/ppermute | solution.py:105
  728.9 39.5 %collective-permute-done.101 = bf16[2,2048,256]{2,1,0:T(8,128)(2,1)} collective-permute-done((bf16[2,2048,256]{2,1,0:T(8,128)(2,1)}, bf16[2,2048,256]{2,1,0:T(8,128)(2,1)}, u32[]{:S(2)}, u32[]{:S(2)}) %collective-permute-start.101) | collective-permute-done | bytes 2097184 | tf_op jit(solution)/shard_map/ppermute | solution.py:105
  772.0 62.5 %collective-permute-done.56 = bf16[256,2048]{1,0:T(8,128)(2,1)} collective-permute-done((bf16[256,2048]{1,0:T(8,128)(2,1)S(1)}, bf16[256,2048]{1,0:T(8,128)(2,1)}, u32[]{:S(2)}, u32[]{:S(2)}) %collective-permute-start.56) | collective-permute-done | bytes 1048608 | tf_op jit(solution)/shard_map/ppermute | solution.py:105
  851.7 31.8 %attention_back.1 = (bf16[1024,512]{1,0:T(8,128)(2,1)}, bf16[1024,512]{1,0:T(8,128)(2,1)}, bf16[1024,512]{1,0:T(8,128)(2,1)}, f32[2,128]{1,0:T(2,128)}) custom-call(f32[1024,1536]{1,0:T(8,128)} %fusion.42.q_ref.k_ref.v_ref, f32[1024,1536]{1,0:T(8,128)} %fusion.42.q_ref.k_ref.v_ref, f32[1024,1536]{1,0:T(8,128)} %fusion.42.q_ref.k_ref.v_ref, ...), custom_call_target="tpu_custom_call" | custom-call | flops 5368709120 | bytes 10485760 | tf_op jit(solution)/shard_map/attention_back/pallas_call | solution.py:238
  969.3 14.3 %collective-permute-done.85 = bf16[64,2048]{1,0:T(8,128)(2,1)S(1)} collective-permute-done((bf16[64,2048]{1,0:T(8,128)(2,1)S(1)}, bf16[64,2048]{1,0:T(8,128)(2,1)S(1)}, u32[]{:S(2)}, u32[]{:S(2)}) %collective-permute-start.85) | collective-permute-done | bytes 262176 | tf_op jit(solution)/shard_map/ppermute | solution.py:98
  1089.0 15.3 %collective-permute-done.72 = bf16[64,6144]{1,0:T(8,128)(2,1)S(1)} collective-permute-done((bf16[64,6144]{1,0:T(8,128)(2,1)S(1)}, bf16[64,6144]{1,0:T(8,128)(2,1)S(1)}, u32[]{:S(2)}, u32[]{:S(2)}) %collective-permute-start.72) | collective-permute-done | bytes 786464 | tf_op jit(solution)/shard_map/ppermute | solution.py:67
  1106.6 15.8 %collective-permute-done.74 = bf16[64,6144]{1,0:T(8,128)(2,1)S(1)} collective-permute-done((bf16[64,6144]{1,0:T(8,128)(2,1)S(1)}, bf16[64,6144]{1,0:T(8,128)(2,1)S(1)}, u32[]{:S(2)}, u32[]{:S(2)}) %collective-permute-start.74) | collective-permute-done | bytes 786464 | tf_op jit(solution)/shard_map/ppermute | solution.py:67
  1124.8 17.5 %collective-permute-done.77 = bf16[64,6144]{1,0:T(8,128)(2,1)S(1)} collective-permute-done((bf16[64,6144]{1,0:T(8,128)(2,1)S(1)}, bf16[64,6144]{1,0:T(8,128)(2,1)S(1)}, u32[]{:S(2)}, u32[]{:S(2)}) %collective-permute-start.77) | collective-permute-done | bytes 786464 | tf_op jit(solution)/shard_map/ppermute | solution.py:68
  (522 shorter events, 532.1 us)
Async XLA Ops:
  0.7 61.0 %collective-permute-start.1 = (bf16[256,2048]{1,0:T(8,128)(2,1)}, bf16[256,2048]{1,0:T(8,128)(2,1)}, u32[]{:S(2)}, u32[]{:S(2)}) collective-permute-start(bf16[256,2048]{1,0:T(8,128)(2,1)} %param.16), channel_id=1, source_target_pairs={{0,2},{1,3},{2,0},{3,1},{4,6},{5,7},{6,4},{7,5},{8,10},{9,11},{10,... | collective-permute-start | bytes 3145736 | tf_op jit(solution)/shard_map/ppermute | solution.py:105
  3.7 81.4 %collective-permute-start = (bf16[256,2048]{1,0:T(8,128)(2,1)}, bf16[256,2048]{1,0:T(8,128)(2,1)}, u32[]{:S(2)}, u32[]{:S(2)}) collective-permute-start(bf16[256,2048]{1,0:T(8,128)(2,1)} %param.16), channel_id=1, source_target_pairs={{0,1},{1,0},{2,3},{3,2},{4,5},{5,4},{6,7},{7,6},{8,9},{9,8},{10,11... | collective-permute-start | bytes 3145736 | tf_op jit(solution)/shard_map/ppermute | solution.py:105
  66.9 87.9 %collective-permute-start.21 = (bf16[2,2048,256]{2,1,0:T(8,128)(2,1)}, bf16[2,2048,256]{2,1,0:T(8,128)(2,1)}, u32[]{:S(2)}, u32[]{:S(2)}) collective-permute-start(bf16[2,2048,256]{2,1,0:T(8,128)(2,1)} %get-tuple-element.43), channel_id=1, source_target_pairs={{0,2},{1,3},{2,0},{3,1},{4,6},{5,7},{6,4},{7,5},{8,10},{9,11},{10,... | collective-permute-start | bytes 6291464 | tf_op jit(solution)/shard_map/ppermute | solution.py:105
  154.8 68.1 %collective-permute-start.24 = (bf16[2,2048,256]{2,1,0:T(8,128)(2,1)S(1)}, bf16[2,2048,256]{2,1,0:T(8,128)(2,1)S(1)}, u32[]{:S(2)}, u32[]{:S(2)}) collective-permute-start(bf16[2,2048,256]{2,1,0:T(8,128)(2,1)S(1)} %copy-done.14), channel_id=1, source_target_pairs={{0,2},{1,3},{2,0},{3,1},{4,6},{5,7},{6,4},{7,5},{8,10},{9,11},{10,... | collective-permute-start | bytes 6291464 | tf_op jit(solution)/shard_map/ppermute | solution.py:105
  175.1 51.9 %collective-permute-start.22 = (bf16[2,2048,256]{2,1,0:T(8,128)(2,1)}, bf16[2,2048,256]{2,1,0:T(8,128)(2,1)S(1)}, u32[]{:S(2)}, u32[]{:S(2)}) collective-permute-start(bf16[2,2048,256]{2,1,0:T(8,128)(2,1)} %collective-permute-done.21), channel_id=1, source_target_pairs={{0,1},{1,0},{2,3},{3,2},{4,5},{5,4},{6,7},{7,6},{8,9},{9,8},{10,11... | collective-permute-start | bytes 6291464 | tf_op jit(solution)/shard_map/ppermute | solution.py:105
  175.2 49.8 %collective-permute-start.34 = (bf16[256,2048]{1,0:T(8,128)(2,1)S(1)}, bf16[256,2048]{1,0:T(8,128)(2,1)}, u32[]{:S(2)}, u32[]{:S(2)}) collective-permute-start(bf16[256,2048]{1,0:T(8,128)(2,1)S(1)} %collective-permute-done.18.refs_6_), channel_id=1, source_target_pairs={{8,0},{16,8},{24,16},{28,24},{20,28},{12,20},{4,12},{0,4},{9,1},{1... | collective-permute-start | bytes 3145736 | tf_op jit(solution)/shard_map/ppermute | solution.py:68
  227.0 75.5 %collective-permute-start.27 = (bf16[2,256,2048]{2,1,0:T(8,128)(2,1)}, bf16[2,256,2048]{2,1,0:T(8,128)(2,1)}, u32[]{:S(2)}, u32[]{:S(2)}) collective-permute-start(bf16[2,256,2048]{2,1,0:T(8,128)(2,1)} %param.29), channel_id=1, source_target_pairs={{0,2},{1,3},{2,0},{3,1},{4,6},{5,7},{6,4},{7,5},{8,10},{9,11},{10,... | collective-permute-start | bytes 6291464 | tf_op jit(solution)/shard_map/ppermute | solution.py:105
  250.0 51.1 %all-to-all-start.2 = ((s32[8,256,8]{1,2,0:T(8,128)}), s32[8,256,8]{1,2,0:T(8,128)S(1)}, u32[]{:S(2)}, u32[]{:S(2)}) async-start(s32[8,256,8]{1,2,0:T(8,128)} %broadcast_in_dim.17), calls=%async_computation.2 | async-start | bytes 131072 | tf_op jit(solution)/shard_map/all_to_all | solution.py:593
  257.1 70.5 %collective-permute-start.23 = (bf16[2,2048,256]{2,1,0:T(8,128)(2,1)}, bf16[2,2048,256]{2,1,0:T(8,128)(2,1)}, u32[]{:S(2)}, u32[]{:S(2)}) collective-permute-start(bf16[2,2048,256]{2,1,0:T(8,128)(2,1)} %get-tuple-element.44), channel_id=1, source_target_pairs={{0,1},{1,0},{2,3},{3,2},{4,5},{5,4},{6,7},{7,6},{8,9},{9,8},{10,11... | collective-permute-start | bytes 6291464 | tf_op jit(solution)/shard_map/ppermute | solution.py:105
  271.6 57.8 %collective-permute-start.25 = (bf16[2,2048,256]{2,1,0:T(8,128)(2,1)}, bf16[2,2048,256]{2,1,0:T(8,128)(2,1)}, u32[]{:S(2)}, u32[]{:S(2)}) collective-permute-start(bf16[2,2048,256]{2,1,0:T(8,128)(2,1)} %copy-done.26), channel_id=1, source_target_pairs={{0,1},{1,0},{2,3},{3,2},{4,5},{5,4},{6,7},{7,6},{8,9},{9,8},{10,11... | collective-permute-start | bytes 6291464 | tf_op jit(solution)/shard_map/ppermute | solution.py:105
  425.3 74.4 %collective-permute-start.39 = (bf16[128,2048]{1,0:T(8,128)(2,1)}, bf16[128,2048]{1,0:T(8,128)(2,1)S(1)}, u32[]{:S(2)}, u32[]{:S(2)}) collective-permute-start(bf16[128,2048]{1,0:T(8,128)(2,1)} %get-tuple-element.179), channel_id=1, source_target_pairs={{8,0},{16,8},{24,16},{28,24},{20,28},{12,20},{4,12},{0,4},{9,1},{1... | collective-permute-start | bytes 1572872 | tf_op jit(solution)/shard_map/ppermute | solution.py:88
  434.7 65.0 %collective-permute-start.44 = (bf16[256,2048]{1,0:T(8,128)(2,1)S(1)}, bf16[256,2048]{1,0:T(8,128)(2,1)}, u32[]{:S(2)}, u32[]{:S(2)}) collective-permute-start(bf16[256,2048]{1,0:T(8,128)(2,1)S(1)} %fusion.21), channel_id=1, source_target_pairs={{0,8},{8,16},{16,24},{24,28},{28,20},{20,12},{12,4},{4,0},{1,9},{9... | collective-permute-start | bytes 3145736 | tf_op jit(solution)/shard_map/ppermute | solution.py:98
  536.3 116.6 %collective-permute-start.97 = (bf16[2,2048,256]{2,1,0:T(8,128)(2,1)}, bf16[2,2048,256]{2,1,0:T(8,128)(2,1)}, u32[]{:S(2)}, u32[]{:S(2)}) collective-permute-start(bf16[2,2048,256]{2,1,0:T(8,128)(2,1)} %get-tuple-element.152), channel_id=1, source_target_pairs={{0,1},{1,0},{2,3},{3,2},{4,5},{5,4},{6,7},{7,6},{8,9},{9,8},{10,11... | collective-permute-start | bytes 6291464 | tf_op jit(solution)/shard_map/ppermute | solution.py:105
  536.3 148.7 %collective-permute-start.96 = (bf16[2,2048,256]{2,1,0:T(8,128)(2,1)}, bf16[2,2048,256]{2,1,0:T(8,128)(2,1)}, u32[]{:S(2)}, u32[]{:S(2)}) collective-permute-start(bf16[2,2048,256]{2,1,0:T(8,128)(2,1)} %get-tuple-element.151), channel_id=1, source_target_pairs={{0,1},{1,0},{2,3},{3,2},{4,5},{5,4},{6,7},{7,6},{8,9},{9,8},{10,11... | collective-permute-start | bytes 6291464 | tf_op jit(solution)/shard_map/ppermute | solution.py:105
  601.6 54.5 %collective-permute-start.100 = (bf16[2,2048,256]{2,1,0:T(8,128)(2,1)}, bf16[2,2048,256]{2,1,0:T(8,128)(2,1)}, u32[]{:S(2)}, u32[]{:S(2)}) collective-permute-start(bf16[2,2048,256]{2,1,0:T(8,128)(2,1)} %get-tuple-element.154), channel_id=1, source_target_pairs={{0,1},{1,0},{2,3},{3,2},{4,5},{5,4},{6,7},{7,6},{8,9},{9,8},{10,11... | collective-permute-start | bytes 6291464 | tf_op jit(solution)/shard_map/ppermute | solution.py:105
  656.1 72.8 %collective-permute-start.99 = (bf16[2,2048,256]{2,1,0:T(8,128)(2,1)}, bf16[2,2048,256]{2,1,0:T(8,128)(2,1)}, u32[]{:S(2)}, u32[]{:S(2)}) collective-permute-start(bf16[2,2048,256]{2,1,0:T(8,128)(2,1)} %get-tuple-element.153), channel_id=1, source_target_pairs={{0,1},{1,0},{2,3},{3,2},{4,5},{5,4},{6,7},{7,6},{8,9},{9,8},{10,11... | collective-permute-start | bytes 6291464 | tf_op jit(solution)/shard_map/ppermute | solution.py:105
  685.1 83.4 %collective-permute-start.101 = (bf16[2,2048,256]{2,1,0:T(8,128)(2,1)}, bf16[2,2048,256]{2,1,0:T(8,128)(2,1)}, u32[]{:S(2)}, u32[]{:S(2)}) collective-permute-start(bf16[2,2048,256]{2,1,0:T(8,128)(2,1)} %fusion.7), channel_id=1, source_target_pairs={{0,2},{1,3},{2,0},{3,1},{4,6},{5,7},{6,4},{7,5},{8,10},{9,11},{10,... | collective-permute-start | bytes 6291464 | tf_op jit(solution)/shard_map/ppermute | solution.py:105
  703.6 135.5 %collective-permute-start.102 = (bf16[2,256,2048]{2,1,0:T(8,128)(2,1)}, bf16[2,256,2048]{2,1,0:T(8,128)(2,1)}, u32[]{:S(2)}, u32[]{:S(2)}) collective-permute-start(bf16[2,256,2048]{2,1,0:T(8,128)(2,1)} %get-tuple-element.149), channel_id=1, source_target_pairs={{0,1},{1,0},{2,3},{3,2},{4,5},{5,4},{6,7},{7,6},{8,9},{9,8},{10,11... | collective-permute-start | bytes 6291464 | tf_op jit(solution)/shard_map/ppermute | solution.py:105
  703.9 135.3 %collective-permute-start.104 = (bf16[2,256,2048]{2,1,0:T(8,128)(2,1)}, bf16[2,256,2048]{2,1,0:T(8,128)(2,1)}, u32[]{:S(2)}, u32[]{:S(2)}) collective-permute-start(bf16[2,256,2048]{2,1,0:T(8,128)(2,1)} %fusion.5), channel_id=1, source_target_pairs={{0,2},{1,3},{2,0},{3,1},{4,6},{5,7},{6,4},{7,5},{8,10},{9,11},{10,... | collective-permute-start | bytes 6291464 | tf_op jit(solution)/shard_map/ppermute | solution.py:105
  723.4 111.2 %collective-permute-start.56 = (bf16[256,2048]{1,0:T(8,128)(2,1)S(1)}, bf16[256,2048]{1,0:T(8,128)(2,1)}, u32[]{:S(2)}, u32[]{:S(2)}) collective-permute-start(bf16[256,2048]{1,0:T(8,128)(2,1)S(1)} %get-tuple-element.145), channel_id=1, source_target_pairs={{0,2},{1,3},{2,0},{3,1},{4,6},{5,7},{6,4},{7,5},{8,10},{9,11},{10,... | collective-permute-start | bytes 3145736 | tf_op jit(solution)/shard_map/ppermute | solution.py:105
  771.9 73.2 %collective-permute-start.55 = (bf16[256,2048]{1,0:T(8,128)(2,1)S(1)}, bf16[256,2048]{1,0:T(8,128)(2,1)S(1)}, u32[]{:S(2)}, u32[]{:S(2)}) collective-permute-start(bf16[256,2048]{1,0:T(8,128)(2,1)S(1)} %get-tuple-element.145), channel_id=1, source_target_pairs={{0,1},{1,0},{2,3},{3,2},{4,5},{5,4},{6,7},{7,6},{8,9},{9,8},{10,11... | collective-permute-start | bytes 3145736 | tf_op jit(solution)/shard_map/ppermute | solution.py:105
  910.0 74.6 %collective-permute-start.59 = (bf16[256,2048]{1,0:T(8,128)(2,1)}, bf16[256,2048]{1,0:T(8,128)(2,1)}, u32[]{:S(2)}, u32[]{:S(2)}) collective-permute-start(bf16[256,2048]{1,0:T(8,128)(2,1)} %get-tuple-element.167), channel_id=1, source_target_pairs={{0,1},{1,0},{2,3},{3,2},{4,5},{5,4},{6,7},{7,6},{8,9},{9,8},{10,11... | collective-permute-start | bytes 3145736 | tf_op jit(solution)/shard_map/ppermute | solution.py:105
  910.5 136.8 %collective-permute-start.58 = (bf16[256,2048]{1,0:T(8,128)(2,1)}, bf16[256,2048]{1,0:T(8,128)(2,1)}, u32[]{:S(2)}, u32[]{:S(2)}) collective-permute-start(bf16[256,2048]{1,0:T(8,128)(2,1)} %get-tuple-element.166), channel_id=1, source_target_pairs={{0,1},{1,0},{2,3},{3,2},{4,5},{5,4},{6,7},{7,6},{8,9},{9,8},{10,11... | collective-permute-start | bytes 3145736 | tf_op jit(solution)/shard_map/ppermute | solution.py:105
  992.4 55.3 %collective-permute-start.60 = (bf16[256,2048]{1,0:T(8,128)(2,1)S(1)}, bf16[256,2048]{1,0:T(8,128)(2,1)S(1)}, u32[]{:S(2)}, u32[]{:S(2)}) collective-permute-start(bf16[256,2048]{1,0:T(8,128)(2,1)S(1)} %add_convert_fusion), channel_id=1, source_target_pairs={{0,2},{1,3},{2,0},{3,1},{4,6},{5,7},{6,4},{7,5},{8,10},{9,11},{10,... | collective-permute-start | bytes 3145736 | tf_op jit(solution)/shard_map/ppermute | solution.py:105
  (147 other events, 3855.6 us)

commit v2 on v1

--- a/solution.py
+++ b/solution.py
@@ -51,7 +51,8 @@
     source = jnp.array(order, jnp.int32)[
         jnp.mod(mine - jnp.arange(size, dtype=jnp.int32), size)
     ]
-    return mine, source
+    behind = jnp.mod(mine - jnp.array(places, jnp.int32), size)
+    return source, behind
 
 
 def tied(value, *others):
@@ -59,11 +60,20 @@
 
 
 def ring_gather(block, size):
+    ahead, back = ring_perms(size)
+    first = (lax.ppermute(block, "expert", ahead), lax.ppermute(block, "expert", back))
+    return ring_rest(block, first, size, {})
+
+
+def ring_rest(block, first, size, gates):
     ahead, back = ring_perms(size)
     half = block.shape[0] // 2
     blocks = [block] * size
-    from_behind = from_ahead = block
-    for step in range(1, size // 2):
+    from_behind, from_ahead = first
+    blocks[1], blocks[size - 1] = first
+    for step in range(2, size // 2):
+        if step in gates:
+            from_behind, from_ahead = tied((from_behind, from_ahead), gates[step])
         from_behind = lax.ppermute(from_behind, "expert", ahead)
         from_ahead = lax.ppermute(from_ahead, "expert", back)
         blocks[step] = from_behind
@@ -115,6 +125,14 @@
     near = [swap(blocks[3].astype(BF16), 1), swap(blocks[1].astype(BF16), 1)]
     far = swap((blocks[2].astype(F32) + near[0].astype(F32)).astype(BF16), 2)
     return blocks[0].astype(F32) + near[1].astype(F32) + far.astype(F32)
+
+
+def shard_scatter_late(blocks, gate):
+    near = [swap(blocks[3].astype(BF16), 1), swap(blocks[1].astype(BF16), 1)]
+    sent = (blocks[2].astype(F32) + near[0].astype(F32)).astype(BF16)
+    sent, own = tied((sent, near[1]), gate)
+    far = swap(sent, 2)
+    return blocks[0].astype(F32) + own.astype(F32) + far.astype(F32), far
 
 
 def tree_sum(value, axis):
@@ -252,6 +270,15 @@
 
 
 GROUP = 4
+
+
+def block_groups(size):
+    if size == 8:
+        return [[0, 1, 7], [4, 3, 5], [2, 6]]
+    order = arrivals(size)
+    return [order[i : i + GROUP] for i in range(0, size, GROUP)]
+
+
 VMEM_BYTES = 60 * 1024 * 1024
 
 
@@ -549,7 +576,7 @@
     slots = rows * routes.shape[1] // expert_count
     shard_index = lax.axis_index("shard")
     expert_index = lax.axis_index("expert")
-    place, source = ring_place(n_expert)
+    source, behind = ring_place(n_expert)
     part_rows = w_qkv.shape[0]
     slice_rows = part_rows // n_expert
     relative = jnp.bitwise_xor(shard_index, jnp.arange(n_shard, dtype=jnp.int32))
@@ -574,9 +601,14 @@
     own_slice = lax.all_to_all(
         own_slice.reshape(n_shard, slice_rows, 3 * local_width), "shard", 0, 0, tiled=True
     )
-    w_blocks = ring_gather(
-        own_slice.reshape(n_shard * slice_rows, 3 * local_width), n_expert
-    )
+    own_slice = own_slice.reshape(n_shard * slice_rows, 3 * local_width)
+
+    ahead, back = ring_perms(n_expert)
+    dy_first = (
+        lax.ppermute(out_grad, "expert", ahead),
+        lax.ppermute(out_grad, "expert", back),
+    )
+    w_blocks = ring_gather(tied(own_slice, dy_first), n_expert)
     w_local = jnp.zeros((n_shard, n_expert, slice_rows, 3 * local_width), BF16)
     for r in arrivals(n_expert):
         w_local = lax.dynamic_update_slice(
@@ -586,17 +618,17 @@
         )
     w_local = w_local.reshape(width, 3 * local_width)
 
-    token_parts = shard_gather(tokens)
+    token_parts = shard_gather(tied(tokens, own_slice))
     token_blocks = jnp.concatenate(token_parts, axis=0)
 
-    dy_blocks = ring_gather(tied(out_grad, w_blocks[n_expert // 2]), n_expert)
     routes_all = lax.all_to_all(
         jnp.broadcast_to(routes[None], (n_expert,) + routes.shape), "expert", 0, 0, tiled=True
     )[source]
 
     gate_own, up_own = w_gate_up[:, 0], w_gate_up[:, 1]
-    gate_full = jnp.stack(shard_gather(tied(gate_own, token_parts[2])))
-    up_full = jnp.stack(shard_gather(tied(up_own, token_parts[2])))
+    gate_parts = shard_gather(tied(gate_own, token_parts[2]))
+    up_parts = shard_gather(tied(up_own, gate_parts[2]))
+    gate_full, up_full = jnp.stack(gate_parts), jnp.stack(up_parts)
 
     my_experts = expert_index * local_experts + jnp.arange(local_experts, dtype=jnp.int32)
     named = jnp.any(
@@ -632,7 +664,10 @@
     normed = (token_float * scale_one * gain_one).astype(BF16)
     qkv_pre = jnp.dot(normed, w_local, preferred_element_type=F32)
     mixed = attention(qkv_pre, tables, heads, size)
-    attended = jnp.dot(mixed, w_out, preferred_element_type=F32).astype(BF16)
+    dy_blocks = ring_rest(
+        out_grad, dy_first, n_expert, {2: w_blocks[n_expert // 2], 3: mixed}
+    )
+    attended = jnp.dot(tied(mixed, dy_blocks[2]), w_out, preferred_element_type=F32).astype(BF16)
     own_tokens = tokens.astype(F32)
     hidden = own_tokens + shard_scatter(list(attended.reshape(n_shard, rows, width)))
     scale_two = rms_scale(hidden)
@@ -640,15 +675,17 @@
     router = jax.nn.softmax(
         jnp.dot(ffn_low, full_router, preferred_element_type=F32), axis=-1
     )
-    down_full = jnp.stack(shard_gather(tied(w_down, ffn_low)))
-
-    ffn_blocks = ring_gather(ffn_low, n_expert)
-    arrival = arrivals(n_expert)
-    groups = [arrival[i : i + GROUP] for i in range(0, n_expert, GROUP)]
+    down_full = jnp.stack(shard_gather(tied(w_down, up_parts[2])))
+
+    ffn_blocks = ring_gather(tied(ffn_low, dy_blocks[3]), n_expert)
+    groups = block_groups(n_expert)
     base = (expert_index * local_experts).reshape(1).astype(jnp.int32)
     results, slot_groups = [], []
     for group in groups:
-        slot_groups.append(jnp.stack([slot_of[:, r] for r in group], axis=1))
+        slots_g = jnp.stack([slot_of[:, r] for r in group], axis=1)
+        if results:
+            slots_g = tied(slots_g, results[-1][-1])
+        slot_groups.append(slots_g)
         results.append(
             expert_group(
                 base,
@@ -669,18 +706,14 @@
         return lambda r: arrays[where_is[r][0]][where_is[r][1]]
 
     ffn_back, hops = ring_scatter(picker(terms), n_expert)
-    to_block = jnp.zeros((n_expert,), jnp.int32).at[source].set(
-        jnp.arange(n_expert, dtype=jnp.int32)
-    )
     back_to = jnp.stack(
         [router_terms[where_is[r][0]][:, where_is[r][1]] for r in range(n_expert)]
     )
     router_back = lax.all_to_all(
-        back_to[to_block], "expert", split_axis=0, concat_axis=0, tiled=True
+        back_to[behind], "expert", split_axis=0, concat_axis=0, tiled=True
     ).reshape(expert_count, rows).T
 
     gate_parts = expert_grad(rows_in, gate_back, n_shard)
-    gate_grads = shard_scatter(list(gate_parts))
     up_parts = expert_grad(tied(rows_in, hops[0]), up_back, n_shard)
     up_grads = shard_scatter(list(up_parts))
     down_parts = expert_grad(tied(act, hops[1]), rows_cot, n_shard)
@@ -688,8 +721,9 @@
         expert_output(slots_g, tied(act_g, hops[2]), down_full)
         for slots_g, act_g in zip(slot_groups, act)
     ]
-    out_terms[-1] = tied(out_terms[-1], ffn_back)
-    out_sum, _ = ring_scatter(picker(out_terms), n_expert)
+    farthest = where_is[n_expert // 2][0]
+    out_terms[farthest] = tied(out_terms[farthest], ffn_back)
+    out_sum, out_hops = ring_scatter(picker(out_terms), n_expert)
     layer_out = (hidden + out_sum).astype(BF16)
 
     logit_back = (
@@ -701,7 +735,9 @@
     hidden_back = out_grad.astype(F32) + norm_back(ffn_back, hidden, scale_two, gain_two)
 
     mix_back = jnp.concatenate(shard_gather(hidden_back.astype(BF16)), axis=0)
-    down_grad = shard_scatter(list(tied(down_parts, mix_back)))
+    gate_grads, far = shard_scatter_late(list(gate_parts), mix_back)
+    up_grads, far = shard_scatter_late(list(up_parts), far)
+    down_grad, far = shard_scatter_late(list(down_parts), far)
     head_back = dot_f32(mix_back, w_out, ((1,), (1,))).astype(BF16)
     out_part = dot_f32(mixed, mix_back, ((0,), (0,))).astype(BF16)
     query_back, key_back, value_back, head_gains = attention_back(

time: 1160 us -> 1050 us (0.905)
  waiting for transfers between devices: 489 us -> 339 us
  Pallas kernels: 262 us -> 279 us
  other arithmetic: 112 us -> 126 us
    ppermute x30, waiting for transfers between devices: 158 us -> 101 us  [swap(): return lax.ppermute(value, 'shard', [(i, i ^ bit) for i in range(size)])]
    ppermute x40, waiting for transfers between devices: 216 us -> 173 us  [the longest x10 62.2 us: ring_rest(): from_ahead = lax.ppermute(from_ahead, 'expert', back)]
    ppermute x12, waiting for transfers between devices: 48.5 us -> 23.8 us  [ring_scatter(): up = lax.ppermute((own_up + up.astype(F32)).astype(BF16), 'expert', ahead)]
    ppermute x12, waiting for transfers between devices: 24.2 us -> 8.65 us  [ring_scatter(): lax.ppermute((own_down + down.astype(F32)).astype(BF16), 'expert', back)]
    convert_element_type x0 -> x3, other arithmetic: none -> 12.9 us  [shard_scatter_late(): sent = (blocks[2].astype(F32) + near[0].astype(F32)).astype(BF16)]
    pallas_call x2 -> x3, Pallas kernels: 36.2 us -> 43.1 us  [expert_output(): pl.pallas_call(functools.partial(output_kernel, count), grid=(experts, pa...]
    pallas_call x2 -> x3, Pallas kernels: 127 us -> 133 us  [expert_group(): pl.pallas_call(functools.partial(expert_kernel, count), grid=(experts, pa...]
  transfers between devices with their start and end apart: 111 -> 111, of which waited for: 46 -> 39; matrix products, arithmetic and copies ran while one was open for 17% -> 21% of each run, Pallas kernels for 14% -> 19%
where the time goes in v2:
time: 1050 us; the launch traced here: 1040 us
  waiting for transfers between devices  339 us (32%)
  Pallas kernels  279 us (27%)
  starting transfers between devices  128 us (12%)
  other arithmetic  126 us (12%)
  local copies, waits for them, and re-layouts  89.5 us (9%)
  matrix products  52.6 us (5%)
  between operations  22.9 us (2%)
    pallas_call x3, Pallas kernels, expert_group(): pl.pallas_call(functools.partial(expert_kernel, count), grid=(experts, pa...  133 us
    ppermute x30, waiting for transfers between devices, swap(): return lax.ppermute(value, 'shard', [(i, i ^ bit) for i in range(size)])  101 us
    ppermute x10, waiting for transfers between devices, ring_rest(): from_ahead = lax.ppermute(from_ahead, 'expert', back)  62.2 us
    pallas_call x3, Pallas kernels, expert_grad(): pl.pallas_call(functools.partial(grad_kernel, len(lefts)), grid=(experts,...  52.9 us
    ppermute x10, waiting for transfers between devices, ring_rest(): from_behind = lax.ppermute(from_behind, 'expert', ahead)  49.4 us
    pallas_call x3, Pallas kernels, expert_output(): pl.pallas_call(functools.partial(output_kernel, count), grid=(experts, pa...  43.1 us
    dot_general x6, matrix products, dot_f32(): lax.dot_general(left, right, (dims, ((), ())), preferred_element_type=F32)  36.2 us
    pallas_call x1, Pallas kernels, attention_back(): pl.pallas_call(functools.partial(attention_back_kernel, size ** (-0.5), m...  31.7 us
  transfers between devices with their start and end apart: 111, of which 39 were waited for; matrix products, arithmetic and copies ran while one was open for 21% of the time, Pallas kernels for 19%

profile of v2, /device:TPU:0, one launch (start us, length us, event | category | flops | bytes accessed | tf_op | source)
XLA Modules:
  0.0 1037.5 jit_solution(9240107368255089791)
XLA Ops:
  94.8 13.6 %collective-permute-done.22 = bf16[2,2048,256]{2,1,0:T(8,128)(2,1)} collective-permute-done((bf16[2,2048,256]{2,1,0:T(8,128)(2,1)}, bf16[2,2048,256]{2,1,0:T(8,128)(2,1)}, u32[]{:S(2)}, u32[]{:S(2)}) %collective-permute-start.22) | collective-permute-done | bytes 2097184 | tf_op jit(solution)/shard_map/ppermute | solution.py:115
  122.6 18.8 %attention.1 = bf16[1024,512]{1,0:T(8,128)(2,1)} custom-call(f32[1024,1536]{1,0:T(8,128)} %fusion.42.q_ref.k_ref.v_ref, f32[1024,1536]{1,0:T(8,128)} %fusion.42.q_ref.k_ref.v_ref, f32[1024,1536]{1,0:T(8,128)} %fusion.42.q_ref.k_ref.v_ref, f32[1024,128]{1,0:T(8,128)} %get-tuple-element.282.cos_ref, f32[1024,128]{1,0:T(8,128)} %get-tuple-element.283.sin_ref, ...), custom_call_target="tpu_custom_call" | custom-call | flops 2147483648 | bytes 7340032 | tf_op jit(solution)/shard_map/attention/pallas_call | solution.py:237
  157.8 13.7 %collective-permute-done.37.refs_5_ = bf16[256,2048]{1,0:T(8,128)(2,1)} collective-permute-done((bf16[256,2048]{1,0:T(8,128)(2,1)}, bf16[256,2048]{1,0:T(8,128)(2,1)}, u32[]{:S(2)}, u32[]{:S(2)}) %collective-permute-start.37) | collective-permute-done | bytes 1048608 | tf_op jit(solution)/shard_map/ppermute | solution.py:78
  184.9 11.8 %collective-permute-done.18.refs_4_ = bf16[256,2048]{1,0:T(8,128)(2,1)} collective-permute-done((bf16[256,2048]{1,0:T(8,128)(2,1)}, bf16[256,2048]{1,0:T(8,128)(2,1)}, u32[]{:S(2)}, u32[]{:S(2)}) %collective-permute-start.18) | collective-permute-done | bytes 1048608 | tf_op jit(solution)/shard_map/ppermute | solution.py:77
  214.9 20.0 %collective-permute-done.36 = bf16[128,2048]{1,0:T(8,128)(2,1)S(1)} collective-permute-done((bf16[128,2048]{1,0:T(8,128)(2,1)S(1)}, bf16[128,2048]{1,0:T(8,128)(2,1)S(1)}, u32[]{:S(2)}, u32[]{:S(2)}) %collective-permute-start.36) | collective-permute-done | bytes 524320 | tf_op jit(solution)/shard_map/ppermute | solution.py:81
  248.1 13.4 %collective-permute-done.31.refs_1_ = bf16[256,2048]{1,0:T(8,128)(2,1)S(1)} collective-permute-done((bf16[256,2048]{1,0:T(8,128)(2,1)}, bf16[256,2048]{1,0:T(8,128)(2,1)S(1)}, u32[]{:S(2)}, u32[]{:S(2)}) %collective-permute-start.31) | collective-permute-done | bytes 1048608 | tf_op jit(solution)/shard_map/ppermute | solution.py:78
  288.3 48.9 %experts.3 = (bf16[2,384,2048]{2,1,0:T(8,128)(2,1)}, bf16[2,384,2048]{2,1,0:T(8,128)(2,1)}, bf16[2,384,1024]{2,1,0:T(8,128)(2,1)}, bf16[2,384,1024]{2,1,0:T(8,12...) custom-call(s32[1]{0:T(128)} %bitcast.25.base_ref, ...), custom_call_target="tpu_custom_call" | custom-call | flops 16106127360 | bytes 25165824 | tf_op jit(solution)/shard_map/experts/pallas_call | solution.py:401
  339.6 49.1 %experts.4 = (bf16[2,384,2048]{2,1,0:T(8,128)(2,1)}, bf16[2,384,2048]{2,1,0:T(8,128)(2,1)}, bf16[2,384,1024]{2,1,0:T(8,128)(2,1)}, bf16[2,384,1024]{2,1,0:T(8,12...) custom-call(s32[1]{0:T(128)} %bitcast.25.base_ref, ...), custom_call_target="tpu_custom_call" | custom-call | flops 16106127360 | bytes 25165824 | tf_op jit(solution)/shard_map/experts/pallas_call | solution.py:401
  406.0 34.9 %experts.5 = (bf16[2,256,2048]{2,1,0:T(8,128)(2,1)}, bf16[2,256,2048]{2,1,0:T(8,128)(2,1)}, bf16[2,256,1024]{2,1,0:T(8,128)(2,1)}, bf16[2,256,1024]{2,1,0:T(8,12...) custom-call(s32[1]{0:T(128)} %bitcast.25.base_ref, ...), custom_call_target="tpu_custom_call" | custom-call | flops 10737418240 | bytes 25165824 | tf_op jit(solution)/shard_map/experts/pallas_call | solution.py:401
  453.8 17.6 %expert_grad.3 = bf16[4,2,2048,256]{3,2,1,0:T(8,128)(2,1)} custom-call(bf16[2,384,2048]{2,1,0:T(8,128)(2,1)} %get-tuple-element.105.refs_0_, bf16[2,384,2048]{2,1,0:T(8,128)(2,1)} %get-tuple-element.106.refs_1_, bf16[2,256,2048]{2,1,0:T(8,128)(2,1)} %get-tuple-element.107.refs_2_, bf16[2,384,1024]{2,1,0:T(8,128)(2,1)} %get-tuple-element.100.refs_3_, ...), custom_call_target="tpu_custom_call" | custom-call | flops 8589934592 | bytes 33554432 | tf_op jit(solution)/shard_map/expert_grad/pallas_call | solution.py:534
  482.9 17.7 %expert_grad.4 = bf16[4,2,2048,256]{3,2,1,0:T(8,128)(2,1)} custom-call(bf16[2,384,2048]{2,1,0:T(8,128)(2,1)} %get-tuple-element.105.refs_0_, bf16[2,384,2048]{2,1,0:T(8,128)(2,1)} %get-tuple-element.106.refs_1_, bf16[2,256,2048]{2,1,0:T(8,128)(2,1)} %get-tuple-element.107.refs_2_, bf16[2,384,1024]{2,1,0:T(8,128)(2,1)} %get-tuple-element.108.refs_3_, ...), custom_call_target="tpu_custom_call" | custom-call | flops 8589934592 | bytes 33554432 | tf_op jit(solution)/shard_map/expert_grad/pallas_call | solution.py:534
  505.1 15.3 %expert_output.5 = bf16[3,256,2048]{2,1,0:T(8,128)(2,1)} custom-call(s32[2,3,256]{2,1,0:T(4,128)} %pad_add_fusion.1.refs_6_.slot_ref, bf16[2,384,1024]{2,1,0:T(8,128)(2,1)} %get-tuple-element.114.act_ref.refs_1_, bf16[4,2,256,2048]{3,2,1,0:T(8,128)(2,1)} %pad_maximum_fusion.2.refs_10_.refs_8_.wd_ref), custom_call_target="tpu_custom_call" | custom-call | flops 3221225472 | bytes 13107200 | tf_op jit(solution)/shard_map/expert_output/pallas_call | solution.py:486
  528.4 17.6 %expert_grad.5 = bf16[4,2,256,2048]{3,2,1,0:T(8,128)(2,1)} custom-call(bf16[2,384,1024]{2,1,0:T(8,128)(2,1)} %get-tuple-element.113.act_ref.refs_0_, bf16[2,384,1024]{2,1,0:T(8,128)(2,1)} %get-tuple-element.114.act_ref.refs_1_, bf16[2,256,1024]{2,1,0:T(8,128)(2,1)} %get-tuple-element.115.act_ref.refs_2_, bf16[2,384,2048]{2,1,0:T(8,128)(2,1)} %get-tuple-element.116.refs_3_, ...), custom_call_target="tpu_custom_call" | custom-call | flops 8589934592 | bytes 11534336 | tf_op jit(solution)/shard_map/expert_grad/pallas_call | solution.py:534
  560.1 12.4 %expert_output.4 = bf16[2,256,2048]{2,1,0:T(8,128)(2,1)} custom-call(s32[2,2,256]{2,1,0:T(2,128)} %pad_add_fusion.2.refs_4_.slot_ref, bf16[2,256,1024]{2,1,0:T(8,128)(2,1)} %get-tuple-element.115.act_ref.refs_2_, bf16[4,2,256,2048]{3,2,1,0:T(8,128)(2,1)} %pad_maximum_fusion.2.refs_10_.refs_8_.wd_ref), custom_call_target="tpu_custom_call" | custom-call | flops 2147483648 | bytes 11534336 | tf_op jit(solution)/shard_map/expert_output/pallas_call | solution.py:486
  592.3 11.5 %collective-permute-done.98 = bf16[2,2048,256]{2,1,0:T(8,128)(2,1)} collective-permute-done((bf16[2,2048,256]{2,1,0:T(8,128)(2,1)}, bf16[2,2048,256]{2,1,0:T(8,128)(2,1)}, u32[]{:S(2)}, u32[]{:S(2)}) %collective-permute-start.98) | collective-permute-done | bytes 2097184 | tf_op jit(solution)/shard_map/ppermute | solution.py:115
  605.5 15.3 %expert_output.3 = bf16[3,256,2048]{2,1,0:T(8,128)(2,1)} custom-call(s32[2,3,256]{2,1,0:T(4,128)} %pad_add_fusion.refs_6_.slot_ref, bf16[2,384,1024]{2,1,0:T(8,128)(2,1)} %get-tuple-element.113.act_ref.refs_0_, bf16[4,2,256,2048]{3,2,1,0:T(8,128)(2,1)} %pad_maximum_fusion.2.refs_10_.refs_8_.wd_ref), custom_call_target="tpu_custom_call" | custom-call | flops 3221225472 | bytes 13107200 | tf_op jit(solution)/shard_map/expert_output/pallas_call | solution.py:486
  634.5 16.3 %collective-permute-done.101 = bf16[2,2048,256]{2,1,0:T(8,128)(2,1)} collective-permute-done((bf16[2,2048,256]{2,1,0:T(8,128)(2,1)}, bf16[2,2048,256]{2,1,0:T(8,128)(2,1)}, u32[]{:S(2)}, u32[]{:S(2)}) %collective-permute-start.101) | collective-permute-done | bytes 2097184 | tf_op jit(solution)/shard_map/ppermute | solution.py:115
  666.1 53.3 %collective-permute-done.56 = bf16[256,2048]{1,0:T(8,128)(2,1)} collective-permute-done((bf16[256,2048]{1,0:T(8,128)(2,1)S(1)}, bf16[256,2048]{1,0:T(8,128)(2,1)}, u32[]{:S(2)}, u32[]{:S(2)}) %collective-permute-start.56) | collective-permute-done | bytes 1048608 | tf_op jit(solution)/shard_map/ppermute | solution.py:115
  734.6 31.7 %attention_back.1 = (bf16[1024,512]{1,0:T(8,128)(2,1)}, bf16[1024,512]{1,0:T(8,128)(2,1)}, bf16[1024,512]{1,0:T(8,128)(2,1)}, f32[2,128]{1,0:T(2,128)}) custom-call(f32[1024,1536]{1,0:T(8,128)} %fusion.42.q_ref.k_ref.v_ref, f32[1024,1536]{1,0:T(8,128)} %fusion.42.q_ref.k_ref.v_ref, f32[1024,1536]{1,0:T(8,128)} %fusion.42.q_ref.k_ref.v_ref, ...), custom_call_target="tpu_custom_call" | custom-call | flops 5368709120 | bytes 10485760 | tf_op jit(solution)/shard_map/attention_back/pallas_call | solution.py:256
  854.0 14.2 %collective-permute-done.85 = bf16[64,2048]{1,0:T(8,128)(2,1)S(1)} collective-permute-done((bf16[64,2048]{1,0:T(8,128)(2,1)S(1)}, bf16[64,2048]{1,0:T(8,128)(2,1)S(1)}, u32[]{:S(2)}, u32[]{:S(2)}) %collective-permute-start.85) | collective-permute-done | bytes 262176 | tf_op jit(solution)/shard_map/ppermute | solution.py:108
  905.3 12.5 %collective-permute-done.89 = bf16[64,2048]{1,0:T(8,128)(2,1)S(1)} collective-permute-done((bf16[64,2048]{1,0:T(8,128)(2,1)S(1)}, bf16[64,2048]{1,0:T(8,128)(2,1)S(1)}, u32[]{:S(2)}, u32[]{:S(2)}) %collective-permute-start.89) | collective-permute-done | bytes 262176 | tf_op jit(solution)/shard_map/ppermute | solution.py:64
  972.0 14.5 %collective-permute-done.72 = bf16[64,6144]{1,0:T(8,128)(2,1)S(1)} collective-permute-done((bf16[64,6144]{1,0:T(8,128)(2,1)S(1)}, bf16[64,6144]{1,0:T(8,128)(2,1)S(1)}, u32[]{:S(2)}, u32[]{:S(2)}) %collective-permute-start.72) | collective-permute-done | bytes 786464 | tf_op jit(solution)/shard_map/ppermute | solution.py:64
  988.8 15.5 %collective-permute-done.74 = bf16[64,6144]{1,0:T(8,128)(2,1)S(1)} collective-permute-done((bf16[64,6144]{1,0:T(8,128)(2,1)S(1)}, bf16[64,6144]{1,0:T(8,128)(2,1)S(1)}, u32[]{:S(2)}, u32[]{:S(2)}) %collective-permute-start.74) | collective-permute-done | bytes 786464 | tf_op jit(solution)/shard_map/ppermute | solution.py:77
  1006.6 17.5 %collective-permute-done.77 = bf16[64,6144]{1,0:T(8,128)(2,1)S(1)} collective-permute-done((bf16[64,6144]{1,0:T(8,128)(2,1)S(1)}, bf16[64,6144]{1,0:T(8,128)(2,1)S(1)}, u32[]{:S(2)}, u32[]{:S(2)}) %collective-permute-start.77) | collective-permute-done | bytes 786464 | tf_op jit(solution)/shard_map/ppermute | solution.py:78
  (510 shorter events, 507.4 us)
Async XLA Ops:
  60.5 47.9 %collective-permute-start.22 = (bf16[2,2048,256]{2,1,0:T(8,128)(2,1)}, bf16[2,2048,256]{2,1,0:T(8,128)(2,1)}, u32[]{:S(2)}, u32[]{:S(2)}) collective-permute-start(bf16[2,2048,256]{2,1,0:T(8,128)(2,1)} %get-tuple-element.73), channel_id=1, source_target_pairs={{0,2},{1,3},{2,0},{3,1},{4,6},{5,7},{6,4},{7,5},{8,10},{9,11},{10,... | collective-permute-start | bytes 6291464 | tf_op jit(solution)/shard_map/ppermute | solution.py:115
  108.4 48.8 %collective-permute-start.25 = (bf16[2,2048,256]{2,1,0:T(8,128)(2,1)}, bf16[2,2048,256]{2,1,0:T(8,128)(2,1)}, u32[]{:S(2)}, u32[]{:S(2)}) collective-permute-start(bf16[2,2048,256]{2,1,0:T(8,128)(2,1)} %get-tuple-element.74), channel_id=1, source_target_pairs={{0,2},{1,3},{2,0},{3,1},{4,6},{5,7},{6,4},{7,5},{8,10},{9,11},{10,... | collective-permute-start | bytes 6291464 | tf_op jit(solution)/shard_map/ppermute | solution.py:115
  151.0 48.3 %collective-permute-start.21 = (bf16[2,2048,256]{2,1,0:T(8,128)(2,1)}, bf16[2,2048,256]{2,1,0:T(8,128)(2,1)}, u32[]{:S(2)}, u32[]{:S(2)}) collective-permute-start(bf16[2,2048,256]{2,1,0:T(8,128)(2,1)} %get-tuple-element.73), channel_id=1, source_target_pairs={{0,1},{1,0},{2,3},{3,2},{4,5},{5,4},{6,7},{7,6},{8,9},{9,8},{10,11... | collective-permute-start | bytes 6291464 | tf_op jit(solution)/shard_map/ppermute | solution.py:115
  157.2 44.0 %collective-permute-start.23 = (bf16[2,2048,256]{2,1,0:T(8,128)(2,1)}, bf16[2,2048,256]{2,1,0:T(8,128)(2,1)}, u32[]{:S(2)}, u32[]{:S(2)}) collective-permute-start(bf16[2,2048,256]{2,1,0:T(8,128)(2,1)} %collective-permute-done.22), channel_id=1, source_target_pairs={{0,1},{1,0},{2,3},{3,2},{4,5},{5,4},{6,7},{7,6},{8,9},{9,8},{10,11... | collective-permute-start | bytes 6291464 | tf_op jit(solution)/shard_map/ppermute | solution.py:115
  157.2 51.3 %collective-permute-start.24 = (bf16[2,2048,256]{2,1,0:T(8,128)(2,1)}, bf16[2,2048,256]{2,1,0:T(8,128)(2,1)}, u32[]{:S(2)}, u32[]{:S(2)}) collective-permute-start(bf16[2,2048,256]{2,1,0:T(8,128)(2,1)} %get-tuple-element.74), channel_id=1, source_target_pairs={{0,1},{1,0},{2,3},{3,2},{4,5},{5,4},{6,7},{7,6},{8,9},{9,8},{10,11... | collective-permute-start | bytes 6291464 | tf_op jit(solution)/shard_map/ppermute | solution.py:115
  180.6 54.4 %collective-permute-start.28 = (bf16[2,256,2048]{2,1,0:T(8,128)(2,1)}, bf16[2,256,2048]{2,1,0:T(8,128)(2,1)}, u32[]{:S(2)}, u32[]{:S(2)}) collective-permute-start(bf16[2,256,2048]{2,1,0:T(8,128)(2,1)} %param.30), channel_id=1, source_target_pairs={{0,2},{1,3},{2,0},{3,1},{4,6},{5,7},{6,4},{7,5},{8,10},{9,11},{10,... | collective-permute-start | bytes 6291464 | tf_op jit(solution)/shard_map/ppermute | solution.py:115
  208.6 54.9 %collective-permute-start.26 = (bf16[2,2048,256]{2,1,0:T(8,128)(2,1)}, bf16[2,2048,256]{2,1,0:T(8,128)(2,1)S(1)}, u32[]{:S(2)}, u32[]{:S(2)}) collective-permute-start(bf16[2,2048,256]{2,1,0:T(8,128)(2,1)} %collective-permute-done.25), channel_id=1, source_target_pairs={{0,1},{1,0},{2,3},{3,2},{4,5},{5,4},{6,7},{7,6},{8,9},{9,8},{10,11... | collective-permute-start | bytes 6291464 | tf_op jit(solution)/shard_map/ppermute | solution.py:115
  285.7 51.5 %collective-permute-start.35 = (bf16[128,2048]{1,0:T(8,128)(2,1)S(1)}, bf16[128,2048]{1,0:T(8,128)(2,1)}, u32[]{:S(2)}, u32[]{:S(2)}) collective-permute-start(bf16[128,2048]{1,0:T(8,128)(2,1)S(1)} %slice.401), channel_id=1, source_target_pairs={{8,0},{16,8},{24,16},{28,24},{20,28},{12,20},{4,12},{0,4},{9,1},{1... | collective-permute-start | bytes 1572872 | tf_op jit(solution)/shard_map/ppermute | solution.py:82
  287.4 49.8 %collective-permute-start.33 = (bf16[128,2048]{1,0:T(8,128)(2,1)S(1)}, bf16[128,2048]{1,0:T(8,128)(2,1)}, u32[]{:S(2)}, u32[]{:S(2)}) collective-permute-start(bf16[128,2048]{1,0:T(8,128)(2,1)S(1)} %slice.400), channel_id=1, source_target_pairs={{0,8},{8,16},{16,24},{24,28},{28,20},{20,12},{12,4},{4,0},{1,9},{9... | collective-permute-start | bytes 1572872 | tf_op jit(solution)/shard_map/ppermute | solution.py:81
  404.0 43.3 %collective-permute-start.44 = (bf16[256,2048]{1,0:T(8,128)(2,1)}, bf16[256,2048]{1,0:T(8,128)(2,1)}, u32[]{:S(2)}, u32[]{:S(2)}) collective-permute-start(bf16[256,2048]{1,0:T(8,128)(2,1)} %get-tuple-element.228), channel_id=1, source_target_pairs={{0,8},{8,16},{16,24},{24,28},{28,20},{20,12},{12,4},{4,0},{1,9},{9... | collective-permute-start | bytes 3145736 | tf_op jit(solution)/shard_map/ppermute | solution.py:108
  475.8 75.8 %collective-permute-start.96 = (bf16[2,2048,256]{2,1,0:T(8,128)(2,1)}, bf16[2,2048,256]{2,1,0:T(8,128)(2,1)}, u32[]{:S(2)}, u32[]{:S(2)}) collective-permute-start(bf16[2,2048,256]{2,1,0:T(8,128)(2,1)} %get-tuple-element.200), channel_id=1, source_target_pairs={{0,1},{1,0},{2,3},{3,2},{4,5},{5,4},{6,7},{7,6},{8,9},{9,8},{10,11... | collective-permute-start | bytes 6291464 | tf_op jit(solution)/shard_map/ppermute | solution.py:115
  475.8 80.1 %collective-permute-start.97 = (bf16[2,2048,256]{2,1,0:T(8,128)(2,1)}, bf16[2,2048,256]{2,1,0:T(8,128)(2,1)}, u32[]{:S(2)}, u32[]{:S(2)}) collective-permute-start(bf16[2,2048,256]{2,1,0:T(8,128)(2,1)} %get-tuple-element.199), channel_id=1, source_target_pairs={{0,1},{1,0},{2,3},{3,2},{4,5},{5,4},{6,7},{7,6},{8,9},{9,8},{10,11... | collective-permute-start | bytes 6291464 | tf_op jit(solution)/shard_map/ppermute | solution.py:115
  505.1 77.9 %collective-permute-start.99 = (bf16[2,2048,256]{2,1,0:T(8,128)(2,1)}, bf16[2,2048,256]{2,1,0:T(8,128)(2,1)}, u32[]{:S(2)}, u32[]{:S(2)}) collective-permute-start(bf16[2,2048,256]{2,1,0:T(8,128)(2,1)} %get-tuple-element.202), channel_id=1, source_target_pairs={{0,1},{1,0},{2,3},{3,2},{4,5},{5,4},{6,7},{7,6},{8,9},{9,8},{10,11... | collective-permute-start | bytes 6291464 | tf_op jit(solution)/shard_map/ppermute | solution.py:115
  546.0 46.3 %collective-permute-start.100 = (bf16[2,2048,256]{2,1,0:T(8,128)(2,1)}, bf16[2,2048,256]{2,1,0:T(8,128)(2,1)}, u32[]{:S(2)}, u32[]{:S(2)}) collective-permute-start(bf16[2,2048,256]{2,1,0:T(8,128)(2,1)} %get-tuple-element.201), channel_id=1, source_target_pairs={{0,1},{1,0},{2,3},{3,2},{4,5},{5,4},{6,7},{7,6},{8,9},{9,8},{10,11... | collective-permute-start | bytes 6291464 | tf_op jit(solution)/shard_map/ppermute | solution.py:115
  555.9 47.9 %collective-permute-start.98 = (bf16[2,2048,256]{2,1,0:T(8,128)(2,1)}, bf16[2,2048,256]{2,1,0:T(8,128)(2,1)}, u32[]{:S(2)}, u32[]{:S(2)}) collective-permute-start(bf16[2,2048,256]{2,1,0:T(8,128)(2,1)} %fusion.10), channel_id=1, source_target_pairs={{0,2},{1,3},{2,0},{3,1},{4,6},{5,7},{6,4},{7,5},{8,10},{9,11},{10,... | collective-permute-start | bytes 6291464 | tf_op jit(solution)/shard_map/ppermute | solution.py:115
  575.7 51.9 %collective-permute-start.102 = (bf16[2,256,2048]{2,1,0:T(8,128)(2,1)}, bf16[2,256,2048]{2,1,0:T(8,128)(2,1)}, u32[]{:S(2)}, u32[]{:S(2)}) collective-permute-start(bf16[2,256,2048]{2,1,0:T(8,128)(2,1)} %get-tuple-element.198), channel_id=1, source_target_pairs={{0,1},{1,0},{2,3},{3,2},{4,5},{5,4},{6,7},{7,6},{8,9},{9,8},{10,11... | collective-permute-start | bytes 6291464 | tf_op jit(solution)/shard_map/ppermute | solution.py:115
  603.8 47.0 %collective-permute-start.101 = (bf16[2,2048,256]{2,1,0:T(8,128)(2,1)}, bf16[2,2048,256]{2,1,0:T(8,128)(2,1)}, u32[]{:S(2)}, u32[]{:S(2)}) collective-permute-start(bf16[2,2048,256]{2,1,0:T(8,128)(2,1)} %fusion.7), channel_id=1, source_target_pairs={{0,2},{1,3},{2,0},{3,1},{4,6},{5,7},{6,4},{7,5},{8,10},{9,11},{10,... | collective-permute-start | bytes 6291464 | tf_op jit(solution)/shard_map/ppermute | solution.py:115
  650.8 73.2 %collective-permute-start.104 = (bf16[2,256,2048]{2,1,0:T(8,128)(2,1)}, bf16[2,256,2048]{2,1,0:T(8,128)(2,1)S(1)}, u32[]{:S(2)}, u32[]{:S(2)}) collective-permute-start(bf16[2,256,2048]{2,1,0:T(8,128)(2,1)} %fusion.5), channel_id=1, source_target_pairs={{0,2},{1,3},{2,0},{3,1},{4,6},{5,7},{6,4},{7,5},{8,10},{9,11},{10,... | collective-permute-start | bytes 6291464 | tf_op jit(solution)/shard_map/ppermute | solution.py:115
  658.6 60.8 %collective-permute-start.56 = (bf16[256,2048]{1,0:T(8,128)(2,1)S(1)}, bf16[256,2048]{1,0:T(8,128)(2,1)}, u32[]{:S(2)}, u32[]{:S(2)}) collective-permute-start(bf16[256,2048]{1,0:T(8,128)(2,1)S(1)} %get-tuple-element.193), channel_id=1, source_target_pairs={{0,2},{1,3},{2,0},{3,1},{4,6},{5,7},{6,4},{7,5},{8,10},{9,11},{10,... | collective-permute-start | bytes 3145736 | tf_op jit(solution)/shard_map/ppermute | solution.py:115
  666.0 63.3 %collective-permute-start.55 = (bf16[256,2048]{1,0:T(8,128)(2,1)S(1)}, bf16[256,2048]{1,0:T(8,128)(2,1)}, u32[]{:S(2)}, u32[]{:S(2)}) collective-permute-start(bf16[256,2048]{1,0:T(8,128)(2,1)S(1)} %get-tuple-element.193), channel_id=1, source_target_pairs={{0,1},{1,0},{2,3},{3,2},{4,5},{5,4},{6,7},{7,6},{8,9},{9,8},{10,11... | collective-permute-start | bytes 3145736 | tf_op jit(solution)/shard_map/ppermute | solution.py:115
  794.7 74.5 %collective-permute-start.59 = (bf16[256,2048]{1,0:T(8,128)(2,1)}, bf16[256,2048]{1,0:T(8,128)(2,1)}, u32[]{:S(2)}, u32[]{:S(2)}) collective-permute-start(bf16[256,2048]{1,0:T(8,128)(2,1)} %get-tuple-element.215), channel_id=1, source_target_pairs={{0,1},{1,0},{2,3},{3,2},{4,5},{5,4},{6,7},{7,6},{8,9},{9,8},{10,11... | collective-permute-start | bytes 3145736 | tf_op jit(solution)/shard_map/ppermute | solution.py:115
  795.2 136.3 %collective-permute-start.58 = (bf16[256,2048]{1,0:T(8,128)(2,1)}, bf16[256,2048]{1,0:T(8,128)(2,1)}, u32[]{:S(2)}, u32[]{:S(2)}) collective-permute-start(bf16[256,2048]{1,0:T(8,128)(2,1)} %get-tuple-element.214), channel_id=1, source_target_pairs={{0,1},{1,0},{2,3},{3,2},{4,5},{5,4},{6,7},{7,6},{8,9},{9,8},{10,11... | collective-permute-start | bytes 3145736 | tf_op jit(solution)/shard_map/ppermute | solution.py:115
  851.9 44.6 %collective-permute-start.65 = (bf16[256,1536]{1,0:T(8,128)(2,1)S(1)}, bf16[256,1536]{1,0:T(8,128)(2,1)S(1)}, u32[]{:S(2)}, u32[]{:S(2)}) collective-permute-start(bf16[256,1536]{1,0:T(8,128)(2,1)S(1)} %fusion.36), channel_id=1, source_target_pairs={{8,0},{16,8},{24,16},{28,24},{20,28},{12,20},{4,12},{0,4},{9,1},{1... | collective-permute-start | bytes 2359304 | tf_op jit(solution)/shard_map/ppermute | solution.py:107
  876.8 54.9 %collective-permute-start.60 = (bf16[256,2048]{1,0:T(8,128)(2,1)S(1)}, bf16[256,2048]{1,0:T(8,128)(2,1)S(1)}, u32[]{:S(2)}, u32[]{:S(2)}) collective-permute-start(bf16[256,2048]{1,0:T(8,128)(2,1)S(1)} %add_convert_fusion), channel_id=1, source_target_pairs={{0,2},{1,3},{2,0},{3,1},{4,6},{5,7},{6,4},{7,5},{8,10},{9,11},{10,... | collective-permute-start | bytes 3145736 | tf_op jit(solution)/shard_map/ppermute | solution.py:115
  (141 other events, 2911.5 us)

commit v3 on v2

--- a/solution.py
+++ b/solution.py
@@ -59,15 +59,25 @@
     return lax.optimization_barrier((value, others))[0]
 
 
-def ring_gather(block, size):
+def zero_of(*others):
+    total = jnp.zeros((), F32)
+    for other in jax.tree.leaves(others):
+        total = total + jnp.minimum(jnp.abs(other[(0,) * other.ndim].astype(F32)), 0.0)
+    return total
+
+
+def held(value, *others):
+    return value + zero_of(*others).astype(value.dtype)
+
+
+def ring_gather(block, size, whole=True):
     ahead, back = ring_perms(size)
     first = (lax.ppermute(block, "expert", ahead), lax.ppermute(block, "expert", back))
-    return ring_rest(block, first, size, {})
-
-
-def ring_rest(block, first, size, gates):
+    return ring_rest(block, first, size, {}, whole)
+
+
+def ring_rest(block, first, size, gates, whole=True):
     ahead, back = ring_perms(size)
-    half = block.shape[0] // 2
     blocks = [block] * size
     from_behind, from_ahead = first
     blocks[1], blocks[size - 1] = first
@@ -78,10 +88,20 @@
         from_ahead = lax.ppermute(from_ahead, "expert", back)
         blocks[step] = from_behind
         blocks[size - step] = from_ahead
-    top = lax.ppermute(from_behind[:half], "expert", ahead)
-    bottom = lax.ppermute(from_ahead[half:], "expert", back)
-    blocks[size // 2] = jnp.concatenate([top, bottom], axis=0)
+    if whole:
+        ring_last(blocks, size)
     return blocks
+
+
+def ring_last(blocks, size, after=()):
+    ahead, back = ring_perms(size)
+    half = blocks[0].shape[0] // 2
+    top, bottom = blocks[size // 2 - 1][:half], blocks[size // 2 + 1][half:]
+    if after:
+        top, bottom = held(top, after), held(bottom, after)
+    blocks[size // 2] = jnp.concatenate(
+        [lax.ppermute(top, "expert", ahead), lax.ppermute(bottom, "expert", back)], axis=0
+    )
 
 
 def arrivals(size):
@@ -91,21 +111,27 @@
     return order + [size // 2]
 
 
-def ring_scatter(pick, size):
+def ring_scatter(pick, size, after=(), brought=None):
     ahead, back = ring_perms(size)
     first = pick(size // 2)
+    if after:
+        first = held(first, after)
     half = first.shape[0] // 2
     down = lax.ppermute(first[:half].astype(BF16), "expert", back)
     up = lax.ppermute(first[half:].astype(BF16), "expert", ahead)
-    hops = [down]
+    hops = [] if brought is None else brought
+    hops.append(down)
     for step in range(size // 2 - 1, 0, -1):
         own_down, own_up = pick(step).astype(F32), pick(size - step).astype(F32)
         if step == size // 2 - 1:
             zeros = jnp.zeros_like(down)
             down = jnp.concatenate([down, zeros], axis=0)
             up = jnp.concatenate([zeros, up], axis=0)
-        down = lax.ppermute((own_down + down.astype(F32)).astype(BF16), "expert", back)
-        up = lax.ppermute((own_up + up.astype(F32)).astype(BF16), "expert", ahead)
+        both = zero_of(down, up)
+        down, up = (
+            lax.ppermute((own_down + down.astype(F32) + both).astype(BF16), "expert", back),
+            lax.ppermute((own_up + up.astype(F32) + both).astype(BF16), "expert", ahead),
+        )
         hops.append(down)
     return pick(0).astype(F32) + down.astype(F32) + up.astype(F32), hops
 
@@ -125,14 +151,6 @@
     near = [swap(blocks[3].astype(BF16), 1), swap(blocks[1].astype(BF16), 1)]
     far = swap((blocks[2].astype(F32) + near[0].astype(F32)).astype(BF16), 2)
     return blocks[0].astype(F32) + near[1].astype(F32) + far.astype(F32)
-
-
-def shard_scatter_late(blocks, gate):
-    near = [swap(blocks[3].astype(BF16), 1), swap(blocks[1].astype(BF16), 1)]
-    sent = (blocks[2].astype(F32) + near[0].astype(F32)).astype(BF16)
-    sent, own = tied((sent, near[1]), gate)
-    far = swap(sent, 2)
-    return blocks[0].astype(F32) + own.astype(F32) + far.astype(F32), far
 
 
 def tree_sum(value, axis):
@@ -212,9 +230,9 @@
         out[...] = norm_back(grad, pre, pre_scale, gain).astype(BF16)
 
 
-def attention_specs(length, size, heads):
+def attention_specs(length, size, heads, first=0):
     def column(part):
-        return pl.BlockSpec((length, size), lambda h: (0, part * heads + h))
+        return pl.BlockSpec((length, size), lambda h: (0, part * heads + first + h))
 
     def whole(*shape):
         return pl.BlockSpec(shape, lambda h: (0, 0))
@@ -249,20 +267,21 @@
     )(qkv_pre, qkv_pre, qkv_pre, *tables)
 
 
-def attention_back(qkv_pre, head_back, tables, heads, size):
+def attention_back(qkv_pre, head_back, tables, heads, size, first, count):
     length = qkv_pre.shape[0]
-    own, pre, rest = attention_specs(length, size, heads)
-    shape = jax.ShapeDtypeStruct((length, heads * size), BF16)
+    given, pre, rest = attention_specs(length, size, heads, first)
+    own = pl.BlockSpec((length, size), lambda h: (0, h))
+    shape = jax.ShapeDtypeStruct((length, count * size), BF16)
     return pl.pallas_call(
         functools.partial(attention_back_kernel, size**-0.5, min(256, length)),
-        grid=(heads,),
-        in_specs=pre + [own] + rest,
+        grid=(count,),
+        in_specs=pre + [given] + rest,
         out_specs=[own, own, own, pl.BlockSpec((2, size), lambda h: (0, 0))],
         out_shape=[shape, shape, shape, jax.ShapeDtypeStruct((2, size), F32)],
         scratch_shapes=[pltpu.VMEM((length, size), F32)] * 3,
         cost_estimate=pl.CostEstimate(
-            flops=10 * heads * length * length * size,
-            bytes_accessed=qkv_pre.size * 4 + 4 * length * heads * size * 2,
+            flops=10 * count * length * length * size,
+            bytes_accessed=qkv_pre.size * 4 + 4 * length * count * size * 2,
             transcendentals=heads * length * length,
         ),
         name="attention_back",
@@ -270,11 +289,12 @@
 
 
 GROUP = 4
+ATTENTION_PARTS = 1
 
 
 def block_groups(size):
     if size == 8:
-        return [[0, 1, 7], [4, 3, 5], [2, 6]]
+        return [[0, 1, 7], [2, 6], [4, 3, 5]]
     order = arrivals(size)
     return [order[i : i + GROUP] for i in range(0, size, GROUP)]
 
@@ -282,13 +302,14 @@
 VMEM_BYTES = 60 * 1024 * 1024
 
 
-def expert_kernel(count, base_ref, *refs):
+def expert_kernel(count, extras, base_ref, *refs):
+    refs = refs[extras:]
     x_refs, dy_refs = refs[:count], refs[count : 2 * count]
     slot_ref, router_ref, wg_ref, wu_ref, wd_ref = refs[2 * count : 2 * count + 5]
-    rin_ref, rcot_ref, act_ref, gb_ref, ub_ref, terms_ref, rback_ref = refs[
-        2 * count + 5 : 2 * count + 12
+    rin_ref, rcot_ref, act_ref, gb_ref, ub_ref, rback_ref = refs[
+        2 * count + 5 : 2 * count + 11
     ]
-    acc_ref, sum_ref, weight_ref, gg_ref = refs[2 * count + 12 :]
+    weight_ref, gg_ref = refs[2 * count + 11 :]
     expert, part = pl.program_id(0), pl.program_id(1)
     tokens = x_refs[0].shape[0]
     slots = rin_ref.shape[1] // count
@@ -322,7 +343,7 @@
             )
 
     rows_in, rows_cot = rin_ref[0], rcot_ref[0]
-    w_gate, w_up, w_back = wg_ref[0, 0], wu_ref[0, 0], wd_ref[0, 0]
+    w_gate, w_up, w_back = wg_ref[0, 0, 0], wu_ref[0, 0, 0], wd_ref[0, 0]
     weight = weight_ref[...]
     pre_gate = dot_f32(rows_in, w_gate, ((1,), (0,)))
     pre_up = dot_f32(rows_in, w_up, ((1,), (0,)))
@@ -335,22 +356,17 @@
     for lane in range(128, share.shape[1], 128):
         folded = folded + share[:, lane : lane + 128]
     act_back = weight * cot_down
-    gate_back = (act_back * pre_up * (sigmoid + silu * (1.0 - sigmoid))).astype(BF16)
-    up_back = (act_back * silu).astype(BF16)
     act_ref[0] = (weight * act).astype(BF16)
-    gb_ref[0] = gate_back
-    ub_ref[0] = up_back
-    back = dot_f32(gate_back, w_gate, ((1,), (1,))) + dot_f32(up_back, w_up, ((1,), (1,)))
+    gb_ref[0] = (act_back * pre_up * (sigmoid + silu * (1.0 - sigmoid))).astype(BF16)
+    ub_ref[0] = (act_back * silu).astype(BF16)
 
     @pl.when(part == 0)
     def _():
         gg_ref[...] = folded
-        acc_ref[...] = back
 
     @pl.when(part > 0)
     def _():
         gg_ref[...] += folded
-        acc_ref[...] += back
 
     @pl.when(part == pl.num_programs(1) - 1)
     def _():
@@ -361,26 +377,15 @@
             rback_ref[0, block : block + 1, :] = jnp.sum(
                 jnp.where(pick, share, 0.0), axis=0, keepdims=True
             )
-            term = dot_f32(low(pick), acc_ref[rows, :].astype(BF16), ((0,), (0,)))
-
-            @pl.when(expert == 0)
-            def _():
-                sum_ref[block] = term
-
-            @pl.when(expert > 0)
-            def _():
-                sum_ref[block] += term
-
-            @pl.when(expert == pl.num_programs(0) - 1)
-            def _():
-                terms_ref[block] = sum_ref[block].astype(BF16)
-
-
-def weight_spec(shape):
-    return pl.BlockSpec((1, 1) + shape[2:], lambda e, j: (j, e, 0, 0))
-
-
-def expert_group(base, x_blocks, dy_blocks, slot_of, router_rows, w_gate, w_up, w_down, slots):
+
+
+def weight_spec(shape, which=None):
+    if which is None:
+        return pl.BlockSpec((1, 1) + shape[2:], lambda e, j: (j, e, 0, 0))
+    return pl.BlockSpec((1, 1, 1) + shape[3:], lambda e, j: (j, e, which, 0, 0))
+
+
+def expert_group(base, x_blocks, dy_blocks, slot_of, router_rows, w_gate_up, w_down, slots, after):
     count = len(x_blocks)
     tokens, width = x_blocks[0].shape
     parts, experts, hidden = w_down.shape[:3]
@@ -397,17 +402,18 @@
     part = pl.BlockSpec((1, rows, hidden), lambda e, j: (e, 0, j))
     wide = jax.ShapeDtypeStruct((experts, rows, width), BF16)
     deep = jax.ShapeDtypeStruct((experts, rows, parts * hidden), BF16)
-    flops = 10 * rows * width * parts * hidden * experts
+    flops = 6 * rows * width * parts * hidden * experts
     return pl.pallas_call(
-        functools.partial(expert_kernel, count),
+        functools.partial(expert_kernel, count, len(after)),
         grid=(experts, parts),
         in_specs=[pl.BlockSpec(memory_space=pltpu.SMEM)]
+        + [pl.BlockSpec(memory_space=pl.ANY)] * len(after)
         + [still((tokens, width))] * (2 * count)
         + [
             per_expert(count, tokens),
             still(router_rows.shape),
-            weight_spec(w_gate.shape),
-            weight_spec(w_up.shape),
+            weight_spec(w_gate_up.shape, 0),
+            weight_spec(w_gate_up.shape, 1),
             weight_spec(w_down.shape),
         ],
         out_specs=[
@@ -416,9 +422,6 @@
             part,
             part,
             part,
-            pl.BlockSpec(
-                (count, tokens, width), lambda e, j: (0, 0, 0), pipeline_mode=pl.Buffered(1)
-            ),
             per_expert(count, tokens),
         ],
         out_shape=[
@@ -427,28 +430,31 @@
             deep,
             deep,
             deep,
-            jax.ShapeDtypeStruct((count, tokens, width), BF16),
             jax.ShapeDtypeStruct((experts, count, tokens), F32),
         ],
         scratch_shapes=[
-            pltpu.VMEM((rows, width), F32),
-            pltpu.VMEM((count, tokens, width), F32),
             pltpu.VMEM((rows, 1), F32),
             pltpu.VMEM((rows, 128), F32),
         ],
         compiler_params=pltpu.CompilerParams(vmem_limit_bytes=VMEM_BYTES),
         cost_estimate=pl.CostEstimate(
-            flops=flops, bytes_accessed=6 * w_gate.size, transcendentals=rows * parts * hidden
+            flops=flops, bytes_accessed=3 * w_gate_up.size, transcendentals=rows * parts * hidden
         ),
         name="experts",
-    )(base, *x_blocks, *dy_blocks, slot_of, router_rows, w_gate, w_up, w_down)
-
-
-def output_kernel(count, slot_ref, act_ref, wd_ref, terms_ref, acc_ref, sum_ref):
+    )(base, *after, *x_blocks, *dy_blocks, slot_of, router_rows, w_gate_up, w_gate_up, w_down)
+
+
+def combine_kernel(count, pairs, dim, slot_ref, *refs):
+    lefts, weights = refs[:pairs], refs[pairs : 2 * pairs]
+    terms_ref, acc_ref, sum_ref = refs[-3:]
     expert, part = pl.program_id(0), pl.program_id(1)
     tokens = terms_ref.shape[1]
-    slots = act_ref.shape[1] // count
-    out = dot_f32(act_ref[0], wd_ref[0, 0], ((1,), (0,)))
+    slots = acc_ref.shape[0] // count
+    out = None
+    for left, weight in zip(lefts, weights):
+        matrix = weight[(0,) * (len(weight.shape) - 2)]
+        product = dot_f32(left[0], matrix, ((1,), (dim,)))
+        out = product if out is None else out + product
 
     @pl.when(part == 0)
     def _():
@@ -479,18 +485,20 @@
                 terms_ref[block] = sum_ref[block].astype(BF16)
 
 
-def expert_output(slot_of, act, w_down):
+def expert_combine(slot_of, lefts, weight, dim, after):
     experts, count, tokens = slot_of.shape
-    parts, _, hidden, width = w_down.shape
-    rows = act.shape[1]
+    parts = weight.shape[0]
+    hidden, width = weight.shape[-2:] if dim == 0 else weight.shape[-1:-3:-1]
+    rows = lefts[0].shape[1]
+    pairs = len(lefts)
+    which = range(pairs) if pairs > 1 else [None]
     return pl.pallas_call(
-        functools.partial(output_kernel, count),
+        functools.partial(combine_kernel, count, pairs, dim),
         grid=(experts, parts),
-        in_specs=[
-            pl.BlockSpec((1, count, tokens), lambda e, j: (e, 0, 0)),
-            pl.BlockSpec((1, rows, hidden), lambda e, j: (e, 0, j)),
-            weight_spec(w_down.shape),
-        ],
+        in_specs=[pl.BlockSpec((1, count, tokens), lambda e, j: (e, 0, 0))]
+        + [pl.BlockSpec((1, rows, hidden), lambda e, j: (e, 0, j))] * pairs
+        + [weight_spec(weight.shape, place) for place in which]
+        + [pl.BlockSpec(memory_space=pl.ANY)] * len(after),
         out_specs=pl.BlockSpec((count, tokens, width), lambda e, j: (0, 0, 0)),
         out_shape=jax.ShapeDtypeStruct((count, tokens, width), BF16),
         scratch_shapes=[
@@ -499,12 +507,12 @@
         ],
         compiler_params=pltpu.CompilerParams(vmem_limit_bytes=VMEM_BYTES),
         cost_estimate=pl.CostEstimate(
-            flops=2 * rows * width * parts * hidden * experts,
-            bytes_accessed=2 * (w_down.size + act.size + count * tokens * width),
+            flops=2 * pairs * rows * width * parts * hidden * experts,
+            bytes_accessed=2 * (weight.size + pairs * lefts[0].size + count * tokens * width),
             transcendentals=0,
         ),
-        name="expert_output",
-    )(slot_of, act, w_down)
+        name="expert_combine",
+    )(slot_of, *lefts, *[weight] * pairs, *after)
 
 
 def grad_kernel(groups, *refs):
@@ -515,7 +523,7 @@
     refs[-1][0, 0] = total.astype(BF16)
 
 
-def expert_grad(lefts, rights, parts):
+def expert_grad(lefts, rights, parts, after):
     experts = lefts[0].shape[0]
     hidden = min(lefts[0].shape[2], rights[0].shape[2]) // parts
 
@@ -535,7 +543,8 @@
         functools.partial(grad_kernel, len(lefts)),
         grid=(experts, parts),
         in_specs=[spec(left, cut_left) for left in lefts]
-        + [spec(right, not cut_left) for right in rights],
+        + [spec(right, not cut_left) for right in rights]
+        + [pl.BlockSpec(memory_space=pl.ANY)] * len(after),
         out_specs=pl.BlockSpec((1, 1) + shape, lambda e, j: (j, e, 0, 0)),
         out_shape=jax.ShapeDtypeStruct((parts, experts) + shape, BF16),
         compiler_params=pltpu.CompilerParams(vmem_limit_bytes=VMEM_BYTES),
@@ -545,7 +554,7 @@
             transcendentals=0,
         ),
         name="expert_grad",
-    )(*lefts, *rights)
+    )(*lefts, *rights, *after)
 
 
 def on_device(
@@ -625,10 +634,8 @@
         jnp.broadcast_to(routes[None], (n_expert,) + routes.shape), "expert", 0, 0, tiled=True
     )[source]
 
-    gate_own, up_own = w_gate_up[:, 0], w_gate_up[:, 1]
-    gate_parts = shard_gather(tied(gate_own, token_parts[2]))
-    up_parts = shard_gather(tied(up_own, gate_parts[2]))
-    gate_full, up_full = jnp.stack(gate_parts), jnp.stack(up_parts)
+    gate_up_full = lax.all_gather(w_gate_up, "shard")
+    down_full = lax.all_gather(w_down, "shard")
 
     my_experts = expert_index * local_experts + jnp.arange(local_experts, dtype=jnp.int32)
     named = jnp.any(
@@ -671,20 +678,22 @@
     own_tokens = tokens.astype(F32)
     hidden = own_tokens + shard_scatter(list(attended.reshape(n_shard, rows, width)))
     scale_two = rms_scale(hidden)
-    ffn_low = (hidden * scale_two * gain_two).astype(BF16)
+    ffn_low = (
+        hidden * scale_two * gain_two
+        + zero_of(dy_blocks[n_expert // 2 - 1], dy_blocks[n_expert // 2 + 1])
+    ).astype(BF16)
     router = jax.nn.softmax(
         jnp.dot(ffn_low, full_router, preferred_element_type=F32), axis=-1
     )
-    down_full = jnp.stack(shard_gather(tied(w_down, up_parts[2])))
-
-    ffn_blocks = ring_gather(tied(ffn_low, dy_blocks[3]), n_expert)
+
+    ffn_blocks = ring_gather(tied(ffn_low, dy_blocks[3]), n_expert, whole=False)
     groups = block_groups(n_expert)
     base = (expert_index * local_experts).reshape(1).astype(jnp.int32)
     results, slot_groups = [], []
     for group in groups:
         slots_g = jnp.stack([slot_of[:, r] for r in group], axis=1)
-        if results:
-            slots_g = tied(slots_g, results[-1][-1])
+        if n_expert // 2 in group:
+            ring_last(ffn_blocks, n_expert, [results[0][-1]] if results else ())
         slot_groups.append(slots_g)
         results.append(
             expert_group(
@@ -693,19 +702,46 @@
                 [dy_blocks[r] for r in group],
                 slot_groups[-1],
                 router_rows,
-                gate_full,
-                up_full,
+                gate_up_full,
                 down_full,
                 slots,
+                [results[-1][-1]] if results else [],
             )
         )
-    rows_in, rows_cot, act, gate_back, up_back, terms, router_terms = map(list, zip(*results))
+    rows_in, rows_cot, act, gate_back, up_back, router_terms = map(list, zip(*results))
     where_is = {r: (g, i) for g, group in enumerate(groups) for i, r in enumerate(group)}
 
     def picker(arrays):
         return lambda r: arrays[where_is[r][0]][where_is[r][1]]
 
-    ffn_back, hops = ring_scatter(picker(terms), n_expert)
+    out_terms, terms = [None] * len(groups), [None] * len(groups)
+    latest = router_terms[-1]
+    last = len(groups) - 1
+    out_hops = []
+
+    def pick_out(r):
+        g, place_in = where_is[r]
+        if out_terms[g] is None:
+            after = [out_terms[g + 1]] if g < last else [router_terms[-1]]
+            after += out_hops[:1] if g == 0 else []
+            out_terms[g] = expert_combine(slot_groups[g], [act[g]], down_full, 0, after)
+        return out_terms[g][place_in]
+
+    for g in range(last, 0, -1):
+        pick_out(groups[g][0])
+    out_sum, _ = ring_scatter(pick_out, n_expert, brought=out_hops)
+    layer_out = (hidden + out_sum).astype(BF16)
+    latest = out_terms[0]
+    for g in range(last, -1, -1):
+        latest = terms[g] = expert_combine(
+            slot_groups[g],
+            [gate_back[g], up_back[g]],
+            gate_up_full,
+            1,
+            [latest] + (out_hops[1:2] if g == last - 1 else []),
+        )
+    back_hops = []
+    ffn_back, _ = ring_scatter(picker(terms), n_expert, after=out_hops[2:3], brought=back_hops)
     back_to = jnp.stack(
         [router_terms[where_is[r][0]][:, where_is[r][1]] for r in range(n_expert)]
     )
@@ -713,18 +749,9 @@
         back_to[behind], "expert", split_axis=0, concat_axis=0, tiled=True
     ).reshape(expert_count, rows).T
 
-    gate_parts = expert_grad(rows_in, gate_back, n_shard)
-    up_parts = expert_grad(tied(rows_in, hops[0]), up_back, n_shard)
-    up_grads = shard_scatter(list(up_parts))
-    down_parts = expert_grad(tied(act, hops[1]), rows_cot, n_shard)
-    out_terms = [
-        expert_output(slots_g, tied(act_g, hops[2]), down_full)
-        for slots_g, act_g in zip(slot_groups, act)
-    ]
-    farthest = where_is[n_expert // 2][0]
-    out_terms[farthest] = tied(out_terms[farthest], ffn_back)
-    out_sum, out_hops = ring_scatter(picker(out_terms), n_expert)
-    layer_out = (hidden + out_sum).astype(BF16)
+    gate_parts = expert_grad(rows_in, gate_back, n_shard, [latest] + out_hops[2:3])
+    up_parts = expert_grad(rows_in, up_back, n_shard, [gate_parts] + back_hops[:1])
+    ffn_back = ffn_back + zero_of(up_parts)
 
     logit_back = (
         router * (router_back - jnp.sum(router * router_back, axis=-1, keepdims=True))
@@ -734,20 +761,47 @@
     gain_two_part = jnp.sum(ffn_back * hidden * scale_two, axis=0)
     hidden_back = out_grad.astype(F32) + norm_back(ffn_back, hidden, scale_two, gain_two)
 
-    mix_back = jnp.concatenate(shard_gather(hidden_back.astype(BF16)), axis=0)
-    gate_grads, far = shard_scatter_late(list(gate_parts), mix_back)
-    up_grads, far = shard_scatter_late(list(up_parts), far)
-    down_grad, far = shard_scatter_late(list(down_parts), far)
+    hidden_low = hidden_back.astype(BF16)
+    mix_parts = shard_gather(hidden_low)
+    mix_back = jnp.concatenate(mix_parts, axis=0)
+
+    def to_owners(parts):
+        return lax.psum_scatter(
+            parts.reshape((n_shard * local_experts,) + parts.shape[2:]),
+            "shard",
+            scatter_dimension=0,
+            tiled=True,
+        )
+
+    gate_grads, up_grads = to_owners(gate_parts), to_owners(up_parts)
+
     head_back = dot_f32(mix_back, w_out, ((1,), (1,))).astype(BF16)
-    out_part = dot_f32(mixed, mix_back, ((0,), (0,))).astype(BF16)
-    query_back, key_back, value_back, head_gains = attention_back(
-        qkv_pre, head_back, tables, heads, size
-    )
-    qkv_back = jnp.concatenate([query_back, key_back, value_back], axis=1)
+    out_part = held(dot_f32(mixed, mix_back, ((0,), (0,))), up_grads).astype(BF16)
+    out_total = lax.psum(out_part, "expert")
+    down_parts = expert_grad(act, rows_cot, n_shard, [out_total])
+    down_grads = to_owners(down_parts)
+    backs, head_gains, count = [], 0.0, heads // ATTENTION_PARTS
+    for part in range(ATTENTION_PARTS):
+        *back, gains = attention_back(
+            qkv_pre, head_back, tables, heads, size, part * count, count
+        )
+        backs.append(back)
+        head_gains = head_gains + gains
+    qkv_back = jnp.concatenate([back[i] for i in range(3) for back in backs], axis=1)
     qkv_part = dot_f32(normed, qkv_back, ((0,), (0,))).astype(BF16)
-    normed_back = dot_f32(tied(qkv_back, qkv_part), w_local, ((1,), (1,)))
+    qkv_terms = qkv_part.reshape(n_shard, n_expert, slice_rows, 3 * local_width)
+    qkv_mine, qkv_hops = ring_scatter(
+        lambda r: lax.dynamic_index_in_dim(qkv_terms, source[r], 1, keepdims=False).reshape(
+            n_shard * slice_rows, 3 * local_width
+        ),
+        n_expert,
+        after=[gate_grads],
+    )
+    normed_back = dot_f32(held(qkv_back, qkv_hops[2], out_total), w_local, ((1,), (1,)))
     gain_one_part = jnp.sum(normed_back * token_float * scale_one, axis=0)
-    own_back = shard_scatter(list(normed_back.astype(BF16).reshape(n_shard, rows, width)))
+    own_back = shard_scatter(
+        list(normed_back.astype(BF16).reshape(n_shard, rows, width))
+    )
     tokens_grad = hidden_back + norm_back(own_back, own_tokens, scale_one[:rows], gain_one)
 
     def placed_blocks(blocks):
@@ -758,18 +812,6 @@
             )
         return total
 
-    out_terms_w = out_part.reshape(n_expert, slice_rows, width)
-    out_mine, _ = ring_scatter(
-        lambda r: lax.dynamic_index_in_dim(out_terms_w, source[r], 0, keepdims=False), n_expert
-    )
-    out_total = placed_blocks(ring_gather(out_mine.astype(BF16), n_expert))
-    qkv_terms = qkv_part.reshape(n_shard, n_expert, slice_rows, 3 * local_width)
-    qkv_mine, _ = ring_scatter(
-        lambda r: lax.dynamic_index_in_dim(qkv_terms, source[r], 1, keepdims=False).reshape(
-            n_shard * slice_rows, 3 * local_width
-        ),
-        n_expert,
-    )
     qkv_mine = lax.all_to_all(
         qkv_mine.astype(BF16), "shard", split_axis=0, concat_axis=0, tiled=True
     )
@@ -790,9 +832,10 @@
         ],
         axis=1,
     )
+    small = held(small, qkv_hops[1])
     small = lax.all_to_all(small, "shard", split_axis=0, concat_axis=0, tiled=True)
     small = tree_sum(jnp.sum(small, axis=0).reshape(1, -1), "expert")[0]
-    gate_up_grad = jnp.stack([gate_grads, up_grads], axis=1)
+    gate_up_grad = jnp.stack([gate_grads, up_grads], axis=1).astype(F32)
     return (
         layer_out,
         tokens_grad,
@@ -800,11 +843,11 @@
         qkv_total,
         small[cuts[1] : cuts[2]],
         small[cuts[2] : cuts[3]],
-        out_total,
+        out_total.astype(F32),
         small[cuts[0] : cuts[1]],
         small[cuts[3] :].reshape(part_rows, expert_count),
         gate_up_grad,
-        down_grad,
+        down_grads.astype(F32),
     )
 
 

time: 1050 us -> 1080 us (1.029)
  waiting for transfers between devices: 339 us -> 426 us
  other arithmetic: 126 us -> 88.8 us
  starting transfers between devices: 128 us -> 93.8 us
  between operations: 22.9 us -> 50.8 us
  Pallas kernels: 279 us -> 267 us
    psum x0 -> x1, waiting for transfers between devices: none -> 60.8 us  [on_device(): out_total = lax.psum(out_part, 'expert')]
    ppermute x34 -> x26, waiting for transfers between devices: 60 us -> 112 us  [the longest x9 60.1 us: ring_scatter(): lax.ppermute((own_down + down.astype(F32) + both).astype(BF16), 'expert',...]
    ppermute x10 -> x8, waiting for transfers between devices: 62.2 us -> 25.6 us  [ring_rest(): from_ahead = lax.ppermute(from_ahead, 'expert', back)]
    ppermute x30 -> x12, waiting for transfers between devices: 101 us -> 72.1 us  [swap(): return lax.ppermute(value, 'shard', [(i, i ^ bit) for i in range(size)])]
    all_to_all x1, waiting for transfers between devices: 0.01 us -> 27.8 us  [on_device(): lax.all_to_all(back_to[behind], 'expert', split_axis=0, concat_axis=0, ti...]
    another operation x6 -> x0, other arithmetic: 27.4 us -> none  [the longest x2 14 us: on_device(): gate_full, up_full = (jnp.stack(gate_parts), jnp.stack(up_parts))]
    ppermute x4 -> x3, waiting for transfers between devices: 0.15 us -> 21 us  [ring_scatter(): down = lax.ppermute(first[:half].astype(BF16), 'expert', back)]
    slice x10 -> x28, local copies, waits for them, and re-layouts: 3.15 us -> 23.2 us  [the longest x22 21 us: zero_of(): other[(0,) * other.ndim].astype(F32)]
  transfers between devices with their start and end apart: 111 -> 83, of which waited for: 39 -> 37; matrix products, arithmetic and copies ran while one was open for 21% -> 19% of each run, Pallas kernels for 19% -> 18%
where the time goes in v3:
time: 1080 us; the launch traced here: 1070 us
  waiting for transfers between devices  426 us (39%)
  Pallas kernels  267 us (25%)
  starting transfers between devices  93.8 us (9%)
  local copies, waits for them, and re-layouts  92.4 us (9%)
  other arithmetic  88.8 us (8%)
  between operations  50.8 us (5%)
  matrix products  50.6 us (5%)
    pallas_call x6, Pallas kernels, expert_combine(): pl.pallas_call(functools.partial(combine_kernel, count, pairs, dim), grid...  96.6 us
    ppermute x12, waiting for transfers between devices, swap(): return lax.ppermute(value, 'shard', [(i, i ^ bit) for i in range(size)])  72.1 us
    pallas_call x3, Pallas kernels, expert_group(): pl.pallas_call(functools.partial(expert_kernel, count, len(after)), grid=...  67 us
    psum x1, waiting for transfers between devices, on_device(): out_total = lax.psum(out_part, 'expert')  60.8 us
    ppermute x9, waiting for transfers between devices, ring_scatter(): lax.ppermute((own_down + down.astype(F32) + both).astype(BF16), 'expert',...  60.1 us
    pallas_call x3, Pallas kernels, expert_grad(): pl.pallas_call(functools.partial(grad_kernel, len(lefts)), grid=(experts,...  53.1 us
    ppermute x8, waiting for transfers between devices, ring_rest(): from_behind = lax.ppermute(from_behind, 'expert', ahead)  36.3 us
    dot_general x6, matrix products, dot_f32(): lax.dot_general(left, right, (dims, ((), ())), preferred_element_type=F32)  35.4 us
  transfers between devices with their start and end apart: 83, of which 37 were waited for; matrix products, arithmetic and copies ran while one was open for 19% of the time, Pallas kernels for 18%

profile of v3, /device:TPU:0, one launch (start us, length us, event | category | flops | bytes accessed | tf_op | source)
XLA Modules:
  0.0 1069.8 jit_solution(16761296423438893215)
XLA Ops:
  75.4 20.9 %collective-permute-done.1 = bf16[256,2048]{1,0:T(8,128)(2,1)} collective-permute-done((bf16[256,2048]{1,0:T(8,128)(2,1)S(1)}, bf16[256,2048]{1,0:T(8,128)(2,1)}, u32[]{:S(2)}, u32[]{:S(2)}) %collective-permute-start.1) | collective-permute-done | bytes 1048608 | tf_op jit(solution)/shard_map/ppermute | solution.py:141
  147.1 18.9 %attention.1 = bf16[1024,512]{1,0:T(8,128)(2,1)} custom-call(f32[1024,1536]{1,0:T(8,128)} %fusion.57.q_ref.k_ref.v_ref, f32[1024,1536]{1,0:T(8,128)} %fusion.57.q_ref.k_ref.v_ref, f32[1024,1536]{1,0:T(8,128)} %fusion.57.q_ref.k_ref.v_ref, f32[1024,128]{1,0:T(8,128)} %get-tuple-element.218.cos_ref, f32[1024,128]{1,0:T(8,128)} %get-tuple-element.219.sin_ref, ...), custom_call_target="tpu_custom_call" | custom-call | flops 2147483648 | bytes 7340032 | tf_op jit(solution)/shard_map/attention/pallas_call | solution.py:255
  173.1 22.5 %collective-permute-done.18.refs_5_ = bf16[256,2048]{1,0:T(8,128)(2,1)S(1)} collective-permute-done((bf16[256,2048]{1,0:T(8,128)(2,1)}, bf16[256,2048]{1,0:T(8,128)(2,1)S(1)}, u32[]{:S(2)}, u32[]{:S(2)}) %collective-permute-start.18) | collective-permute-done | bytes 1048608 | tf_op jit(solution)/shard_map/ppermute | solution.py:87
  198.1 23.1 %collective-permute-done.16 = bf16[256,2048]{1,0:T(8,128)(2,1)S(1)} collective-permute-done((bf16[256,2048]{1,0:T(8,128)(2,1)S(1)}, bf16[256,2048]{1,0:T(8,128)(2,1)S(1)}, u32[]{:S(2)}, u32[]{:S(2)}) %collective-permute-start.16) | collective-permute-done | bytes 1048608 | tf_op jit(solution)/shard_map/ppermute | solution.py:141
  231.4 17.2 %collective-permute-done.20.refs_1_ = bf16[256,2048]{1,0:T(8,128)(2,1)} collective-permute-done((bf16[256,2048]{1,0:T(8,128)(2,1)S(1)}, bf16[256,2048]{1,0:T(8,128)(2,1)}, u32[]{:S(2)}, u32[]{:S(2)}) %collective-permute-start.20) | collective-permute-done | bytes 1048608 | tf_op jit(solution)/shard_map/ppermute | solution.py:75
  261.3 13.7 %collective-permute-done.22.refs_1_ = bf16[256,2048]{1,0:T(8,128)(2,1)} collective-permute-done((bf16[256,2048]{1,0:T(8,128)(2,1)}, bf16[256,2048]{1,0:T(8,128)(2,1)}, u32[]{:S(2)}, u32[]{:S(2)}) %collective-permute-start.22) | collective-permute-done | bytes 1048608 | tf_op jit(solution)/shard_map/ppermute | solution.py:87
  290.7 23.8 %experts.3 = (bf16[2,384,2048]{2,1,0:T(8,128)(2,1)}, bf16[2,384,2048]{2,1,0:T(8,128)(2,1)}, bf16[2,384,1024]{2,1,0:T(8,128)(2,1)}, bf16[2,384,1024]{2,1,0:T(8,12...) custom-call(s32[1]{0:T(128)} %bitcast.25.base_ref, bf16[256,2048]{1,0:T(8,128)(2,1)} %copy-done.6, ...), custom_call_target="tpu_custom_call" | custom-call | flops 9663676416 | bytes 25165824 | tf_op jit(solution)/shard_map/experts/pallas_call | solution.py:406
  320.4 19.4 %experts.4 = (bf16[2,256,2048]{2,1,0:T(8,128)(2,1)}, bf16[2,256,2048]{2,1,0:T(8,128)(2,1)}, bf16[2,256,1024]{2,1,0:T(8,128)(2,1)}, bf16[2,256,1024]{2,1,0:T(8,12...) custom-call(s32[1]{0:T(128)} %bitcast.25.base_ref, f32[2,3,256]{2,1,0:T(4,128)} %get-tuple-element.50.refs_0_, ...), custom_call_target="tpu_custom_call" | custom-call | flops 6442450944 | bytes 25165824 | tf_op jit(solution)/shard_map/experts/pallas_call | solution.py:406
  342.1 23.8 %experts.5 = (bf16[2,384,2048]{2,1,0:T(8,128)(2,1)}, bf16[2,384,2048]{2,1,0:T(8,128)(2,1)}, bf16[2,384,1024]{2,1,0:T(8,128)(2,1)}, bf16[2,384,1024]{2,1,0:T(8,12...) custom-call(s32[1]{0:T(128)} %bitcast.25.base_ref, f32[2,2,256]{2,1,0:T(2,128)} %get-tuple-element.52.refs_0_, ...), custom_call_target="tpu_custom_call" | custom-call | flops 9663676416 | bytes 25165824 | tf_op jit(solution)/shard_map/experts/pallas_call | solution.py:406
  365.9 15.4 %expert_combine.6.refs_2_ = bf16[3,256,2048]{2,1,0:T(8,128)(2,1)} custom-call(s32[2,3,256]{2,1,0:T(4,128)} %pad_add_fusion.1.refs_7_.slot_ref, bf16[2,384,1024]{2,1,0:T(8,128)(2,1)} %get-tuple-element.53.refs_0_.refs_2_, bf16[4,2,256,2048]{3,2,1,0:T(8,128)(2,1)} %bitcast.261, f32[2,3,256]{2,1,0:T(4,128)} %get-tuple-element.54.refs_2_), custom_call_target="tpu_custom_call" | custom-call | flops 3221225472 | bytes 13107200 | tf_op jit(solution)/shard_map/expert_combine/pallas_call | solution.py:495
  412.2 15.3 %expert_combine.8.refs_4_ = bf16[3,256,2048]{2,1,0:T(8,128)(2,1)} custom-call(s32[2,3,256]{2,1,0:T(4,128)} %pad_add_fusion.refs_6_.slot_ref, bf16[2,384,1024]{2,1,0:T(8,128)(2,1)} %get-tuple-element.49.refs_0_, bf16[4,2,256,2048]{3,2,1,0:T(8,128)(2,1)} %bitcast.263, bf16[2,256,2048]{2,1,0:T(8,128)(2,1)} %expert_combine.7.refs_2_, bf16[128,2048]{1,0:T(8,128)(2,1)} %copy-done.24), custom_call_target="tpu_custom_call" | custom-call | flops 3221225472 | bytes 13107200 | tf_op jit(solution)/shard_map/expert_combine/pallas_call | solution.py:495
  436.7 19.1 %expert_combine.9.refs_4_ = bf16[3,256,2048]{2,1,0:T(8,128)(2,1)} custom-call(s32[2,3,256]{2,1,0:T(4,128)} %pad_add_fusion.1.refs_7_.slot_ref, bf16[2,384,1024]{2,1,0:T(8,128)(2,1)} %get-tuple-element.59.refs_0_.refs_5_, bf16[2,384,1024]{2,1,0:T(8,128)(2,1)} %get-tuple-element.60.refs_1_.refs_5_, bf16[4,2,2,2048,256]{4,3,2,1,0:T(8,128)(2,1)} %bitcast.252, ...), custom_call_target="tpu_custom_call" | custom-call | flops 6442450944 | bytes 23068672 | tf_op jit(solution)/shard_map/expert_combine/pallas_call | solution.py:495
  455.7 15.5 %expert_combine.10.refs_4_ = bf16[2,256,2048]{2,1,0:T(8,128)(2,1)} custom-call(s32[2,2,256]{2,1,0:T(2,128)} %pad_add_fusion.2.refs_5_.slot_ref, bf16[2,256,1024]{2,1,0:T(8,128)(2,1)} %get-tuple-element.57.refs_0_.refs_4_, bf16[2,256,1024]{2,1,0:T(8,128)(2,1)} %get-tuple-element.58.refs_1_.refs_4_, bf16[4,2,2,2048,256]{4,3,2,1,0:T(8,128)(2,1)} %bitcast.254, ...), custom_call_target="tpu_custom_call" | custom-call | flops 4294967296 | bytes 20971520 | tf_op jit(solution)/shard_map/expert_combine/pallas_call | solution.py:495
  471.2 19.1 %expert_combine.11.refs_6_ = bf16[3,256,2048]{2,1,0:T(8,128)(2,1)} custom-call(s32[2,3,256]{2,1,0:T(4,128)} %pad_add_fusion.refs_6_.slot_ref, bf16[2,384,1024]{2,1,0:T(8,128)(2,1)} %get-tuple-element.55.refs_0_.refs_3_, bf16[2,384,1024]{2,1,0:T(8,128)(2,1)} %get-tuple-element.56.refs_1_.refs_3_, bf16[4,2,2,2048,256]{4,3,2,1,0:T(8,128)(2,1)} %bitcast.256, ...), custom_call_target="tpu_custom_call" | custom-call | flops 6442450944 | bytes 23068672 | tf_op jit(solution)/shard_map/expert_combine/pallas_call | solution.py:495
  491.3 17.5 %expert_grad.3.refs_6_ = bf16[4,2,2048,256]{3,2,1,0:T(8,128)(2,1)} custom-call(bf16[2,384,2048]{2,1,0:T(8,128)(2,1)} %get-tuple-element.61.refs_0_, bf16[2,256,2048]{2,1,0:T(8,128)(2,1)} %get-tuple-element.62.refs_1_, bf16[2,384,2048]{2,1,0:T(8,128)(2,1)} %get-tuple-element.63.refs_2_, bf16[2,384,1024]{2,1,0:T(8,128)(2,1)} %get-tuple-element.55.refs_0_.refs_3_, ...), custom_call_target="tpu_custom_call" | custom-call | flops 8589934592 | bytes 33554432 | tf_op jit(solution)/shard_map/expert_grad/pallas_call | solution.py:542
  522.6 18.0 %expert_grad.4 = bf16[4,2,2048,256]{3,2,1,0:T(8,128)(2,1)} custom-call(bf16[2,384,2048]{2,1,0:T(8,128)(2,1)} %get-tuple-element.61.refs_0_, bf16[2,256,2048]{2,1,0:T(8,128)(2,1)} %get-tuple-element.62.refs_1_, bf16[2,384,2048]{2,1,0:T(8,128)(2,1)} %get-tuple-element.63.refs_2_, bf16[2,384,1024]{2,1,0:T(8,128)(2,1)} %get-tuple-element.56.refs_1_.refs_3_, ...), custom_call_target="tpu_custom_call" | custom-call | flops 8589934592 | bytes 33554432 | tf_op jit(solution)/shard_map/expert_grad/pallas_call | solution.py:542
  555.7 15.5 %collective-permute-done.39 = bf16[256,2048]{1,0:T(8,128)(2,1)S(1)} collective-permute-done((bf16[256,2048]{1,0:T(8,128)(2,1)S(1)}, bf16[256,2048]{1,0:T(8,128)(2,1)S(1)}, u32[]{:S(2)}, u32[]{:S(2)}) %collective-permute-start.39) | collective-permute-done | bytes 1048608 | tf_op jit(solution)/shard_map/ppermute | solution.py:132
  592.3 27.8 %all-to-all-done.3 = f32[8,2,256]{2,1,0:T(2,128)S(1)} async-done(((f32[8,2,256]{2,1,0:T(2,128)}), f32[8,2,256]{2,1,0:T(2,128)S(1)}, u32[]{:S(2)}, u32[]{:S(2)}) %all-to-all-start.3) | async-done | bytes 16416 | tf_op jit(solution)/shard_map/all_to_all | solution.py:748
  637.7 17.4 %collective-permute-done.44 = bf16[256,2048]{1,0:T(8,128)(2,1)S(1)} collective-permute-done((bf16[256,2048]{1,0:T(8,128)(2,1)S(1)}, bf16[256,2048]{1,0:T(8,128)(2,1)S(1)}, u32[]{:S(2)}, u32[]{:S(2)}) %collective-permute-start.44) | collective-permute-done | bytes 1048608 | tf_op jit(solution)/shard_map/ppermute | solution.py:132
  672.6 15.9 %collective-permute-done.47 = bf16[256,2048]{1,0:T(8,128)(2,1)} collective-permute-done((bf16[256,2048]{1,0:T(8,128)(2,1)}, bf16[256,2048]{1,0:T(8,128)(2,1)}, u32[]{:S(2)}, u32[]{:S(2)}) %collective-permute-start.47) | collective-permute-done | bytes 1048608 | tf_op jit(solution)/shard_map/ppermute | solution.py:141
  699.2 31.7 %attention_back.1 = (bf16[1024,512]{1,0:T(8,128)(2,1)}, bf16[1024,512]{1,0:T(8,128)(2,1)}, bf16[1024,512]{1,0:T(8,128)(2,1)}, f32[2,128]{1,0:T(2,128)}) custom-call(f32[1024,1536]{1,0:T(8,128)} %fusion.57.q_ref.k_ref.v_ref, f32[1024,1536]{1,0:T(8,128)} %fusion.57.q_ref.k_ref.v_ref, f32[1024,1536]{1,0:T(8,128)} %fusion.57.q_ref.k_ref.v_ref, ...), custom_call_target="tpu_custom_call" | custom-call | flops 5368709120 | bytes 10485760 | tf_op jit(solution)/shard_map/attention_back/pallas_call | solution.py:275
  827.7 60.8 %all-reduce.8.cloned.1.call-done.refs_6_ = bf16[512,2048]{1,0:T(8,128)(2,1)} async-done(((bf16[512,2048]{1,0:T(8,128)(2,1)}), bf16[512,2048]{1,0:T(8,128)(2,1)}) %all-reduce.8.cloned.1.call-update) | async-done | bytes 2097168 | tf_op jit(solution)/shard_map/psum | solution.py:780
  890.4 17.6 %expert_grad.5 = bf16[4,2,256,2048]{3,2,1,0:T(8,128)(2,1)} custom-call(bf16[2,384,1024]{2,1,0:T(8,128)(2,1)} %get-tuple-element.49.refs_0_, bf16[2,256,1024]{2,1,0:T(8,128)(2,1)} %get-tuple-element.51.refs_0_.refs_1_, bf16[2,384,1024]{2,1,0:T(8,128)(2,1)} %get-tuple-element.53.refs_0_.refs_2_, bf16[2,384,2048]{2,1,0:T(8,128)(2,1)} %get-tuple-element.68.refs_3_, ...), custom_call_target="tpu_custom_call" | custom-call | flops 8589934592 | bytes 11534336 | tf_op jit(solution)/shard_map/expert_grad/pallas_call | solution.py:542
  1034.4 13.2 %collective-permute-done.68 = bf16[64,6144]{1,0:T(8,128)(2,1)S(1)} collective-permute-done((bf16[64,6144]{1,0:T(8,128)(2,1)S(1)}, bf16[64,6144]{1,0:T(8,128)(2,1)S(1)}, u32[]{:S(2)}, u32[]{:S(2)}) %collective-permute-start.68) | collective-permute-done | bytes 786464 | tf_op jit(solution)/shard_map/ppermute | solution.py:88
  (457 shorter events, 516.1 us)
Async XLA Ops:
  7.2 283.5 %all-gather.7.cloned.1.call-start = ((), (), s32[]{:S(2)}) async-start(), calls=%async_computation.14 | async-start | bytes 10485760 | tf_op jit(solution)/shard_map/all_gather | solution.py:638
  7.9 282.8 %all-gather.5.cloned.1.call-start = ((), (), s32[]{:S(2)}) async-start(), calls=%async_computation.13 | async-start | bytes 20971520 | tf_op jit(solution)/shard_map/all_gather | solution.py:637
  8.7 40.1 %collective-permute-start.4 = (bf16[256,2048]{1,0:T(8,128)(2,1)}, bf16[256,2048]{1,0:T(8,128)(2,1)}, u32[]{:S(2)}, u32[]{:S(2)}) collective-permute-start(bf16[256,2048]{1,0:T(8,128)(2,1)} %refs_3_.1), channel_id=1, source_target_pairs={{8,0},{16,8},{24,16},{28,24},{20,28},{12,20},{4,12},{0,4},{9,1},{1... | collective-permute-start | bytes 3145736 | tf_op jit(solution)/shard_map/ppermute | solution.py:618
  11.7 37.1 %collective-permute-start.3 = (bf16[256,2048]{1,0:T(8,128)(2,1)}, bf16[256,2048]{1,0:T(8,128)(2,1)}, u32[]{:S(2)}, u32[]{:S(2)}) collective-permute-start(bf16[256,2048]{1,0:T(8,128)(2,1)} %refs_3_.1), channel_id=1, source_target_pairs={{0,8},{8,16},{16,24},{24,28},{28,20},{20,12},{12,4},{4,0},{1,9},{9... | collective-permute-start | bytes 3145736 | tf_op jit(solution)/shard_map/ppermute | solution.py:617
  46.1 50.2 %collective-permute-start.1 = (bf16[256,2048]{1,0:T(8,128)(2,1)S(1)}, bf16[256,2048]{1,0:T(8,128)(2,1)}, u32[]{:S(2)}, u32[]{:S(2)}) collective-permute-start(bf16[256,2048]{1,0:T(8,128)(2,1)S(1)} %copy-done.8), channel_id=1, source_target_pairs={{0,2},{1,3},{2,0},{3,1},{4,6},{5,7},{6,4},{7,5},{8,10},{9,11},{10,... | collective-permute-start | bytes 3145736 | tf_op jit(solution)/shard_map/ppermute | solution.py:141
  133.6 32.3 %collective-permute-start.13 = (bf16[256,2048]{1,0:T(8,128)(2,1)}, bf16[256,2048]{1,0:T(8,128)(2,1)}, u32[]{:S(2)}, u32[]{:S(2)}) collective-permute-start(bf16[256,2048]{1,0:T(8,128)(2,1)} %collective-permute-done.3.refs_4_), channel_id=1, source_target_pairs={{0,8},{8,16},{16,24},{24,28},{28,20},{20,12},{12,4},{4,0},{1,9},{9... | collective-permute-start | bytes 3145736 | tf_op jit(solution)/shard_map/ppermute | solution.py:87
  134.4 35.5 %collective-permute-start.17 = (bf16[256,2048]{1,0:T(8,128)(2,1)}, bf16[256,2048]{1,0:T(8,128)(2,1)}, u32[]{:S(2)}, u32[]{:S(2)}) collective-permute-start(bf16[256,2048]{1,0:T(8,128)(2,1)} %collective-permute-done.4.refs_5_), channel_id=1, source_target_pairs={{8,0},{16,8},{24,16},{28,24},{20,28},{12,20},{4,12},{0,4},{9,1},{1... | collective-permute-start | bytes 3145736 | tf_op jit(solution)/shard_map/ppermute | solution.py:88
  172.9 48.3 %collective-permute-start.16 = (bf16[256,2048]{1,0:T(8,128)(2,1)S(1)}, bf16[256,2048]{1,0:T(8,128)(2,1)S(1)}, u32[]{:S(2)}, u32[]{:S(2)}) collective-permute-start(bf16[256,2048]{1,0:T(8,128)(2,1)S(1)} %add_convert_fusion.3), channel_id=1, source_target_pairs={{0,2},{1,3},{2,0},{3,1},{4,6},{5,7},{6,4},{7,5},{8,10},{9,11},{10,... | collective-permute-start | bytes 3145736 | tf_op jit(solution)/shard_map/ppermute | solution.py:141
  231.3 514.3 %reduce-scatter.4.cloned.1.call-start = ((), (), s32[]{:S(2)}) async-start(), calls=%async_computation.9 | async-start | bytes 10485760 | tf_op jit(solution)/shard_map/reduce_scatter | solution.py:769
  253.4 35.9 %collective-permute-start.23 = (bf16[256,2048]{1,0:T(8,128)(2,1)}, bf16[256,2048]{1,0:T(8,128)(2,1)}, u32[]{:S(2)}, u32[]{:S(2)}) collective-permute-start(bf16[256,2048]{1,0:T(8,128)(2,1)} %collective-permute-done.21.refs_2_), channel_id=1, source_target_pairs={{8,0},{16,8},{24,16},{28,24},{20,28},{12,20},{4,12},{0,4},{9,1},{1... | collective-permute-start | bytes 3145736 | tf_op jit(solution)/shard_map/ppermute | solution.py:88
  275.0 41.3 %collective-permute-start.24 = (bf16[256,2048]{1,0:T(8,128)(2,1)}, bf16[256,2048]{1,0:T(8,128)(2,1)S(1)}, u32[]{:S(2)}, u32[]{:S(2)}) collective-permute-start(bf16[256,2048]{1,0:T(8,128)(2,1)} %collective-permute-done.22.refs_1_), channel_id=1, source_target_pairs={{0,8},{8,16},{16,24},{24,28},{28,20},{20,12},{12,4},{4,0},{1,9},{9... | collective-permute-start | bytes 3145736 | tf_op jit(solution)/shard_map/ppermute | solution.py:87
  435.0 55.2 %collective-permute-start.34 = (bf16[256,2048]{1,0:T(8,128)(2,1)}, bf16[256,2048]{1,0:T(8,128)(2,1)S(1)}, u32[]{:S(2)}, u32[]{:S(2)}) collective-permute-start(bf16[256,2048]{1,0:T(8,128)(2,1)} %get-tuple-element.172), channel_id=1, source_target_pairs={{8,0},{16,8},{24,16},{28,24},{20,28},{12,20},{4,12},{0,4},{9,1},{1... | collective-permute-start | bytes 3145736 | tf_op jit(solution)/shard_map/ppermute | solution.py:132
  508.8 257.2 %reduce-scatter.6.cloned.1.call-start = ((), (), s32[]{:S(2)}) async-start(), calls=%async_computation.10 | async-start | bytes 10485760 | tf_op jit(solution)/shard_map/reduce_scatter | solution.py:769
  554.8 65.4 %collective-permute-start.35 = (bf16[256,2048]{1,0:T(8,128)(2,1)}, bf16[256,2048]{1,0:T(8,128)(2,1)}, u32[]{:S(2)}, u32[]{:S(2)}) collective-permute-start(bf16[256,2048]{1,0:T(8,128)(2,1)} %get-tuple-element.173), channel_id=1, source_target_pairs={{0,8},{8,16},{16,24},{24,28},{28,20},{20,12},{12,4},{4,0},{1,9},{9... | collective-permute-start | bytes 3145736 | tf_op jit(solution)/shard_map/ppermute | solution.py:133
  584.1 37.9 %collective-permute-start.42 = (bf16[256,2048]{1,0:T(8,128)(2,1)}, bf16[256,2048]{1,0:T(8,128)(2,1)}, u32[]{:S(2)}, u32[]{:S(2)}) collective-permute-start(bf16[256,2048]{1,0:T(8,128)(2,1)} %get-tuple-element.170), channel_id=1, source_target_pairs={{8,0},{16,8},{24,16},{28,24},{20,28},{12,20},{4,12},{0,4},{9,1},{1... | collective-permute-start | bytes 3145736 | tf_op jit(solution)/shard_map/ppermute | solution.py:132
  585.6 38.2 %collective-permute-start.43 = (bf16[256,2048]{1,0:T(8,128)(2,1)}, bf16[256,2048]{1,0:T(8,128)(2,1)}, u32[]{:S(2)}, u32[]{:S(2)}) collective-permute-start(bf16[256,2048]{1,0:T(8,128)(2,1)} %get-tuple-element.171), channel_id=1, source_target_pairs={{0,8},{8,16},{16,24},{24,28},{28,20},{20,12},{12,4},{4,0},{1,9},{9... | collective-permute-start | bytes 3145736 | tf_op jit(solution)/shard_map/ppermute | solution.py:133
  587.9 32.1 %all-to-all-start.3 = ((f32[8,2,256]{2,1,0:T(2,128)}), f32[8,2,256]{2,1,0:T(2,128)S(1)}, u32[]{:S(2)}, u32[]{:S(2)}) async-start(f32[8,2,256]{2,1,0:T(2,128)} %gather_fusion.3), calls=%async_computation.3 | async-start | bytes 32768 | tf_op jit(solution)/shard_map/all_to_all | solution.py:748
  592.2 296.3 %all-reduce.8.cloned.1.call-start = ((), (), s32[]{:S(2)}) async-start(), calls=%async_computation.11 | async-start | bytes 4194304 | tf_op jit(solution)/shard_map/psum | solution.py:780
  633.3 34.9 %collective-permute-start.36 = (bf16[256,2048]{1,0:T(8,128)(2,1)S(1)}, bf16[256,2048]{1,0:T(8,128)(2,1)S(1)}, u32[]{:S(2)}, u32[]{:S(2)}) collective-permute-start(bf16[256,2048]{1,0:T(8,128)(2,1)S(1)} %get-tuple-element.163), channel_id=1, source_target_pairs={{8,0},{16,8},{24,16},{28,24},{20,28},{12,20},{4,12},{0,4},{9,1},{1... | collective-permute-start | bytes 3145736 | tf_op jit(solution)/shard_map/ppermute | solution.py:132
  634.1 34.3 %collective-permute-start.37 = (bf16[256,2048]{1,0:T(8,128)(2,1)S(1)}, bf16[256,2048]{1,0:T(8,128)(2,1)S(1)}, u32[]{:S(2)}, u32[]{:S(2)}) collective-permute-start(bf16[256,2048]{1,0:T(8,128)(2,1)S(1)} %get-tuple-element.164), channel_id=1, source_target_pairs={{0,8},{8,16},{16,24},{24,28},{28,20},{20,12},{12,4},{4,0},{1,9},{9... | collective-permute-start | bytes 3145736 | tf_op jit(solution)/shard_map/ppermute | solution.py:133
  765.2 33.4 %collective-permute-start.50 = (bf16[256,1536]{1,0:T(8,128)(2,1)}, bf16[256,1536]{1,0:T(8,128)(2,1)}, u32[]{:S(2)}, u32[]{:S(2)}) collective-permute-start(bf16[256,1536]{1,0:T(8,128)(2,1)} %fusion.52), channel_id=1, source_target_pairs={{8,0},{16,8},{24,16},{28,24},{20,28},{12,20},{4,12},{0,4},{9,1},{1... | collective-permute-start | bytes 2359304 | tf_op jit(solution)/shard_map/ppermute | solution.py:132
  774.1 284.3 %reduce-scatter.8.cloned.1.call-start = ((), (), s32[]{:S(2)}) async-start(), calls=%async_computation.12 | async-start | bytes 10485760 | tf_op jit(solution)/shard_map/reduce_scatter | solution.py:769
  964.5 48.5 %collective-permute-start.54 = (bf16[256,2048]{1,0:T(8,128)(2,1)}, bf16[256,2048]{1,0:T(8,128)(2,1)}, u32[]{:S(2)}, u32[]{:S(2)}) collective-permute-start(bf16[256,2048]{1,0:T(8,128)(2,1)} %get-tuple-element.155), channel_id=1, source_target_pairs={{0,1},{1,0},{2,3},{3,2},{4,5},{5,4},{6,7},{7,6},{8,9},{9,8},{10,11... | collective-permute-start | bytes 3145736 | tf_op jit(solution)/shard_map/ppermute | solution.py:141
  964.6 34.1 %collective-permute-start.55 = (bf16[256,2048]{1,0:T(8,128)(2,1)}, bf16[256,2048]{1,0:T(8,128)(2,1)}, u32[]{:S(2)}, u32[]{:S(2)}) collective-permute-start(bf16[256,2048]{1,0:T(8,128)(2,1)} %get-tuple-element.156), channel_id=1, source_target_pairs={{0,1},{1,0},{2,3},{3,2},{4,5},{5,4},{6,7},{7,6},{8,9},{9,8},{10,11... | collective-permute-start | bytes 3145736 | tf_op jit(solution)/shard_map/ppermute | solution.py:141
  (112 other events, 1920.5 us)
Sparse Core Ops, SparseCore 0:
  9.6 92.6 all-gather.6
  103.8 128.3 all-gather.4
  509.0 70.0 reduce-scatter.3
  582.0 71.4 reduce-scatter.5
  774.2 114.2 all-reduce.7
  908.1 79.1 reduce-scatter.7

commit v4 on v3

--- a/solution.py
+++ b/solution.py
@@ -751,7 +751,8 @@
 
     gate_parts = expert_grad(rows_in, gate_back, n_shard, [latest] + out_hops[2:3])
     up_parts = expert_grad(rows_in, up_back, n_shard, [gate_parts] + back_hops[:1])
-    ffn_back = ffn_back + zero_of(up_parts)
+    down_parts = expert_grad(act, rows_cot, n_shard, [up_parts] + back_hops[1:2])
+    ffn_back = ffn_back + zero_of(down_parts)
 
     logit_back = (
         router * (router_back - jnp.sum(router * router_back, axis=-1, keepdims=True))
@@ -765,21 +766,18 @@
     mix_parts = shard_gather(hidden_low)
     mix_back = jnp.concatenate(mix_parts, axis=0)
 
-    def to_owners(parts):
-        return lax.psum_scatter(
+    gate_grads, up_grads, down_grads = (
+        lax.psum_scatter(
             parts.reshape((n_shard * local_experts,) + parts.shape[2:]),
             "shard",
             scatter_dimension=0,
             tiled=True,
-        )
-
-    gate_grads, up_grads = to_owners(gate_parts), to_owners(up_parts)
+        ).astype(F32)
+        for parts in (gate_parts, up_parts, down_parts)
+    )
 
     head_back = dot_f32(mix_back, w_out, ((1,), (1,))).astype(BF16)
-    out_part = held(dot_f32(mixed, mix_back, ((0,), (0,))), up_grads).astype(BF16)
-    out_total = lax.psum(out_part, "expert")
-    down_parts = expert_grad(act, rows_cot, n_shard, [out_total])
-    down_grads = to_owners(down_parts)
+    out_part = dot_f32(mixed, mix_back, ((0,), (0,))).astype(BF16)
     backs, head_gains, count = [], 0.0, heads // ATTENTION_PARTS
     for part in range(ATTENTION_PARTS):
         *back, gains = attention_back(
@@ -795,9 +793,8 @@
             n_shard * slice_rows, 3 * local_width
         ),
         n_expert,
-        after=[gate_grads],
-    )
-    normed_back = dot_f32(held(qkv_back, qkv_hops[2], out_total), w_local, ((1,), (1,)))
+    )
+    normed_back = dot_f32(held(qkv_back, qkv_hops[1]), w_local, ((1,), (1,)))
     gain_one_part = jnp.sum(normed_back * token_float * scale_one, axis=0)
     own_back = shard_scatter(
         list(normed_back.astype(BF16).reshape(n_shard, rows, width))
@@ -812,6 +809,7 @@
             )
         return total
 
+    out_total = lax.psum(out_part, "expert").astype(F32)
     qkv_mine = lax.all_to_all(
         qkv_mine.astype(BF16), "shard", split_axis=0, concat_axis=0, tiled=True
     )
@@ -835,7 +833,7 @@
     small = held(small, qkv_hops[1])
     small = lax.all_to_all(small, "shard", split_axis=0, concat_axis=0, tiled=True)
     small = tree_sum(jnp.sum(small, axis=0).reshape(1, -1), "expert")[0]
-    gate_up_grad = jnp.stack([gate_grads, up_grads], axis=1).astype(F32)
+    gate_up_grad = jnp.stack([gate_grads, up_grads], axis=1)
     return (
         layer_out,
         tokens_grad,
@@ -843,11 +841,11 @@
         qkv_total,
         small[cuts[1] : cuts[2]],
         small[cuts[2] : cuts[3]],
-        out_total.astype(F32),
+        out_total,
         small[cuts[0] : cuts[1]],
         small[cuts[3] :].reshape(part_rows, expert_count),
         gate_up_grad,
-        down_grads.astype(F32),
+        down_grads,
     )
 
 

time: 1080 us -> 1010 us (0.935)
  waiting for transfers between devices: 426 us -> 358 us
  other arithmetic: 88.8 us -> 105 us
  local copies, waits for them, and re-layouts: 92.4 us -> 79 us
    psum x1, waiting for transfers between devices: 60.8 us -> 0.01 us  [on_device(): out_total = lax.psum(out_part, 'expert').astype(F32)]
    reduce_scatter x3, waiting for transfers between devices: 0.01 us -> 50.6 us  [on_device(): lax.psum_scatter(parts.reshape((n_shard * local_experts,) + parts.shape[2...]
    ppermute x9, waiting for transfers between devices: 60.1 us -> 25.2 us  [ring_scatter(): lax.ppermute((own_down + down.astype(F32) + both).astype(BF16), 'expert',...]
    all_to_all x1, waiting for transfers between devices: 27.8 us -> 6.63 us  [on_device(): lax.all_to_all(back_to[behind], 'expert', split_axis=0, concat_axis=0, ti...]
    ppermute x8, waiting for transfers between devices: 25.6 us -> 38.8 us  [ring_rest(): from_ahead = lax.ppermute(from_ahead, 'expert', back)]
    convert_element_type x9 -> x8, other arithmetic: 24.1 us -> 27 us  [ring_scatter(): (own_down + down.astype(F32) + both).astype(BF16)]
  transfers between devices with their start and end apart: 83 -> 83, of which waited for: 37 -> 35; matrix products, arithmetic and copies ran while one was open for 19% -> 19% of each run, Pallas kernels for 18% -> 23%
where the time goes in v4:
time: 1010 us; the launch traced here: 997 us
  waiting for transfers between devices  358 us (35%)
  Pallas kernels  267 us (26%)
  other arithmetic  105 us (10%)
  starting transfers between devices  90.6 us (9%)
  local copies, waits for them, and re-layouts  79 us (8%)
  matrix products  48.7 us (5%)
  between operations  48.4 us (5%)
    pallas_call x6, Pallas kernels, expert_combine(): pl.pallas_call(functools.partial(combine_kernel, count, pairs, dim), grid...  96.8 us
    ppermute x12, waiting for transfers between devices, swap(): return lax.ppermute(value, 'shard', [(i, i ^ bit) for i in range(size)])  74.6 us
    pallas_call x3, Pallas kernels, expert_group(): pl.pallas_call(functools.partial(expert_kernel, count, len(after)), grid=...  67 us
    pallas_call x3, Pallas kernels, expert_grad(): pl.pallas_call(functools.partial(grad_kernel, len(lefts)), grid=(experts,...  52.7 us
    reduce_scatter x3, waiting for transfers between devices, on_device(): lax.psum_scatter(parts.reshape((n_shard * local_experts,) + parts.shape[2...  50.6 us
    ppermute x8, waiting for transfers between devices, ring_rest(): from_ahead = lax.ppermute(from_ahead, 'expert', back)  38.8 us
    ppermute x8, waiting for transfers between devices, ring_rest(): from_behind = lax.ppermute(from_behind, 'expert', ahead)  37 us
    dot_general x6, matrix products, dot_f32(): lax.dot_general(left, right, (dims, ((), ())), preferred_element_type=F32)  33.4 us
  transfers between devices with their start and end apart: 83, of which 35 were waited for; matrix products, arithmetic and copies ran while one was open for 19% of the time, Pallas kernels for 23%

profile of v4, /device:TPU:0, one launch (start us, length us, event | category | flops | bytes accessed | tf_op | source)
XLA Modules:
  0.0 996.9 jit_solution(12718693328298401768)
XLA Ops:
  74.6 21.8 %collective-permute-done.1 = bf16[256,2048]{1,0:T(8,128)(2,1)} collective-permute-done((bf16[256,2048]{1,0:T(8,128)(2,1)S(1)}, bf16[256,2048]{1,0:T(8,128)(2,1)}, u32[]{:S(2)}, u32[]{:S(2)}) %collective-permute-start.1) | collective-permute-done | bytes 1048608 | tf_op jit(solution)/shard_map/ppermute | solution.py:141
  147.2 18.8 %attention.1 = bf16[1024,512]{1,0:T(8,128)(2,1)} custom-call(f32[1024,1536]{1,0:T(8,128)} %fusion.57.q_ref.k_ref.v_ref, f32[1024,1536]{1,0:T(8,128)} %fusion.57.q_ref.k_ref.v_ref, f32[1024,1536]{1,0:T(8,128)} %fusion.57.q_ref.k_ref.v_ref, f32[1024,128]{1,0:T(8,128)} %get-tuple-element.207.cos_ref, f32[1024,128]{1,0:T(8,128)} %get-tuple-element.208.sin_ref, ...), custom_call_target="tpu_custom_call" | custom-call | flops 2147483648 | bytes 7340032 | tf_op jit(solution)/shard_map/attention/pallas_call | solution.py:255
  173.3 22.5 %collective-permute-done.18.refs_5_ = bf16[256,2048]{1,0:T(8,128)(2,1)S(1)} collective-permute-done((bf16[256,2048]{1,0:T(8,128)(2,1)}, bf16[256,2048]{1,0:T(8,128)(2,1)S(1)}, u32[]{:S(2)}, u32[]{:S(2)}) %collective-permute-start.18) | collective-permute-done | bytes 1048608 | tf_op jit(solution)/shard_map/ppermute | solution.py:87
  198.2 23.1 %collective-permute-done.16 = bf16[256,2048]{1,0:T(8,128)(2,1)S(1)} collective-permute-done((bf16[256,2048]{1,0:T(8,128)(2,1)S(1)}, bf16[256,2048]{1,0:T(8,128)(2,1)S(1)}, u32[]{:S(2)}, u32[]{:S(2)}) %collective-permute-start.16) | collective-permute-done | bytes 1048608 | tf_op jit(solution)/shard_map/ppermute | solution.py:141
  231.4 17.3 %collective-permute-done.20.refs_1_ = bf16[256,2048]{1,0:T(8,128)(2,1)} collective-permute-done((bf16[256,2048]{1,0:T(8,128)(2,1)S(1)}, bf16[256,2048]{1,0:T(8,128)(2,1)}, u32[]{:S(2)}, u32[]{:S(2)}) %collective-permute-start.20) | collective-permute-done | bytes 1048608 | tf_op jit(solution)/shard_map/ppermute | solution.py:75
  261.4 13.7 %collective-permute-done.22.refs_1_ = bf16[256,2048]{1,0:T(8,128)(2,1)} collective-permute-done((bf16[256,2048]{1,0:T(8,128)(2,1)}, bf16[256,2048]{1,0:T(8,128)(2,1)}, u32[]{:S(2)}, u32[]{:S(2)}) %collective-permute-start.22) | collective-permute-done | bytes 1048608 | tf_op jit(solution)/shard_map/ppermute | solution.py:87
  290.8 23.8 %experts.3 = (bf16[2,384,2048]{2,1,0:T(8,128)(2,1)}, bf16[2,384,2048]{2,1,0:T(8,128)(2,1)}, bf16[2,384,1024]{2,1,0:T(8,128)(2,1)}, bf16[2,384,1024]{2,1,0:T(8,12...) custom-call(s32[1]{0:T(128)} %bitcast.25.base_ref, bf16[256,2048]{1,0:T(8,128)(2,1)} %copy-done.5, ...), custom_call_target="tpu_custom_call" | custom-call | flops 9663676416 | bytes 25165824 | tf_op jit(solution)/shard_map/experts/pallas_call | solution.py:406
  320.5 19.4 %experts.4 = (bf16[2,256,2048]{2,1,0:T(8,128)(2,1)}, bf16[2,256,2048]{2,1,0:T(8,128)(2,1)}, bf16[2,256,1024]{2,1,0:T(8,128)(2,1)}, bf16[2,256,1024]{2,1,0:T(8,12...) custom-call(s32[1]{0:T(128)} %bitcast.25.base_ref, f32[2,3,256]{2,1,0:T(4,128)} %get-tuple-element.50.refs_0_, ...), custom_call_target="tpu_custom_call" | custom-call | flops 6442450944 | bytes 25165824 | tf_op jit(solution)/shard_map/experts/pallas_call | solution.py:406
  342.2 23.8 %experts.5 = (bf16[2,384,2048]{2,1,0:T(8,128)(2,1)}, bf16[2,384,2048]{2,1,0:T(8,128)(2,1)}, bf16[2,384,1024]{2,1,0:T(8,128)(2,1)}, bf16[2,384,1024]{2,1,0:T(8,12...) custom-call(s32[1]{0:T(128)} %bitcast.25.base_ref, f32[2,2,256]{2,1,0:T(2,128)} %get-tuple-element.52.refs_0_, ...), custom_call_target="tpu_custom_call" | custom-call | flops 9663676416 | bytes 25165824 | tf_op jit(solution)/shard_map/experts/pallas_call | solution.py:406
  366.0 15.4 %expert_combine.6.refs_2_ = bf16[3,256,2048]{2,1,0:T(8,128)(2,1)} custom-call(s32[2,3,256]{2,1,0:T(4,128)} %pad_add_fusion.1.refs_7_.slot_ref, bf16[2,384,1024]{2,1,0:T(8,128)(2,1)} %get-tuple-element.53.refs_0_.refs_2_, bf16[4,2,256,2048]{3,2,1,0:T(8,128)(2,1)} %bitcast.261, f32[2,3,256]{2,1,0:T(4,128)} %get-tuple-element.54.refs_2_), custom_call_target="tpu_custom_call" | custom-call | flops 3221225472 | bytes 13107200 | tf_op jit(solution)/shard_map/expert_combine/pallas_call | solution.py:495
  428.5 15.3 %expert_combine.8.refs_4_ = bf16[3,256,2048]{2,1,0:T(8,128)(2,1)} custom-call(s32[2,3,256]{2,1,0:T(4,128)} %pad_add_fusion.refs_6_.slot_ref, bf16[2,384,1024]{2,1,0:T(8,128)(2,1)} %get-tuple-element.49.refs_0_, bf16[4,2,256,2048]{3,2,1,0:T(8,128)(2,1)} %bitcast.263, bf16[2,256,2048]{2,1,0:T(8,128)(2,1)} %expert_combine.7.refs_2_, bf16[128,2048]{1,0:T(8,128)(2,1)} %copy-done.20), custom_call_target="tpu_custom_call" | custom-call | flops 3221225472 | bytes 13107200 | tf_op jit(solution)/shard_map/expert_combine/pallas_call | solution.py:495
  443.8 19.1 %expert_combine.9.refs_4_ = bf16[3,256,2048]{2,1,0:T(8,128)(2,1)} custom-call(s32[2,3,256]{2,1,0:T(4,128)} %pad_add_fusion.1.refs_7_.slot_ref, bf16[2,384,1024]{2,1,0:T(8,128)(2,1)} %get-tuple-element.59.refs_0_.refs_5_, bf16[2,384,1024]{2,1,0:T(8,128)(2,1)} %get-tuple-element.60.refs_1_.refs_5_, bf16[4,2,2,2048,256]{4,3,2,1,0:T(8,128)(2,1)} %bitcast.252, ...), custom_call_target="tpu_custom_call" | custom-call | flops 6442450944 | bytes 23068672 | tf_op jit(solution)/shard_map/expert_combine/pallas_call | solution.py:495
  491.6 15.5 %expert_combine.10.refs_4_ = bf16[2,256,2048]{2,1,0:T(8,128)(2,1)} custom-call(s32[2,2,256]{2,1,0:T(2,128)} %pad_add_fusion.2.refs_5_.slot_ref, bf16[2,256,1024]{2,1,0:T(8,128)(2,1)} %get-tuple-element.57.refs_0_.refs_4_, bf16[2,256,1024]{2,1,0:T(8,128)(2,1)} %get-tuple-element.58.refs_1_.refs_4_, bf16[4,2,2,2048,256]{4,3,2,1,0:T(8,128)(2,1)} %bitcast.254, ...), custom_call_target="tpu_custom_call" | custom-call | flops 4294967296 | bytes 20971520 | tf_op jit(solution)/shard_map/expert_combine/pallas_call | solution.py:495
  507.1 19.1 %expert_combine.11.refs_6_ = bf16[3,256,2048]{2,1,0:T(8,128)(2,1)} custom-call(s32[2,3,256]{2,1,0:T(4,128)} %pad_add_fusion.refs_6_.slot_ref, bf16[2,384,1024]{2,1,0:T(8,128)(2,1)} %get-tuple-element.55.refs_0_.refs_3_, bf16[2,384,1024]{2,1,0:T(8,128)(2,1)} %get-tuple-element.56.refs_1_.refs_3_, bf16[4,2,2,2048,256]{4,3,2,1,0:T(8,128)(2,1)} %bitcast.256, ...), custom_call_target="tpu_custom_call" | custom-call | flops 6442450944 | bytes 23068672 | tf_op jit(solution)/shard_map/expert_combine/pallas_call | solution.py:495
  544.2 17.5 %expert_grad.3.refs_6_ = bf16[4,2,2048,256]{3,2,1,0:T(8,128)(2,1)} custom-call(bf16[2,384,2048]{2,1,0:T(8,128)(2,1)} %get-tuple-element.64.refs_0_, bf16[2,256,2048]{2,1,0:T(8,128)(2,1)} %get-tuple-element.65.refs_1_, bf16[2,384,2048]{2,1,0:T(8,128)(2,1)} %get-tuple-element.66.refs_2_, bf16[2,384,1024]{2,1,0:T(8,128)(2,1)} %get-tuple-element.55.refs_0_.refs_3_, ...), custom_call_target="tpu_custom_call" | custom-call | flops 8589934592 | bytes 33554432 | tf_op jit(solution)/shard_map/expert_grad/pallas_call | solution.py:542
  573.3 17.5 %expert_grad.4.refs_6_ = bf16[4,2,2048,256]{3,2,1,0:T(8,128)(2,1)} custom-call(bf16[2,384,2048]{2,1,0:T(8,128)(2,1)} %get-tuple-element.64.refs_0_, bf16[2,256,2048]{2,1,0:T(8,128)(2,1)} %get-tuple-element.65.refs_1_, bf16[2,384,2048]{2,1,0:T(8,128)(2,1)} %get-tuple-element.66.refs_2_, bf16[2,384,1024]{2,1,0:T(8,128)(2,1)} %get-tuple-element.56.refs_1_.refs_3_, ...), custom_call_target="tpu_custom_call" | custom-call | flops 8589934592 | bytes 33554432 | tf_op jit(solution)/shard_map/expert_grad/pallas_call | solution.py:542
  590.8 17.6 %expert_grad.5 = bf16[4,2,256,2048]{3,2,1,0:T(8,128)(2,1)} custom-call(bf16[2,384,1024]{2,1,0:T(8,128)(2,1)} %get-tuple-element.49.refs_0_, bf16[2,256,1024]{2,1,0:T(8,128)(2,1)} %get-tuple-element.51.refs_0_.refs_1_, bf16[2,384,1024]{2,1,0:T(8,128)(2,1)} %get-tuple-element.53.refs_0_.refs_2_, bf16[2,384,2048]{2,1,0:T(8,128)(2,1)} %get-tuple-element.61.refs_3_, ...), custom_call_target="tpu_custom_call" | custom-call | flops 8589934592 | bytes 11534336 | tf_op jit(solution)/shard_map/expert_grad/pallas_call | solution.py:542
  620.2 14.5 %collective-permute-done.47 = bf16[256,2048]{1,0:T(8,128)(2,1)S(1)} collective-permute-done((bf16[256,2048]{1,0:T(8,128)(2,1)S(1)}, bf16[256,2048]{1,0:T(8,128)(2,1)S(1)}, u32[]{:S(2)}, u32[]{:S(2)}) %collective-permute-start.47) | collective-permute-done | bytes 1048608 | tf_op jit(solution)/shard_map/ppermute | solution.py:141
  649.1 31.7 %attention_back.1 = (bf16[1024,512]{1,0:T(8,128)(2,1)}, bf16[1024,512]{1,0:T(8,128)(2,1)}, bf16[1024,512]{1,0:T(8,128)(2,1)}, f32[2,128]{1,0:T(2,128)}) custom-call(f32[1024,1536]{1,0:T(8,128)} %fusion.57.q_ref.k_ref.v_ref, f32[1024,1536]{1,0:T(8,128)} %fusion.57.q_ref.k_ref.v_ref, f32[1024,1536]{1,0:T(8,128)} %fusion.57.q_ref.k_ref.v_ref, ...), custom_call_target="tpu_custom_call" | custom-call | flops 5368709120 | bytes 10485760 | tf_op jit(solution)/shard_map/attention_back/pallas_call | solution.py:275
  723.9 14.6 %collective-permute-done.58 = bf16[256,1536]{1,0:T(8,128)(2,1)} collective-permute-done((bf16[256,1536]{1,0:T(8,128)(2,1)}, bf16[256,1536]{1,0:T(8,128)(2,1)}, u32[]{:S(2)}, u32[]{:S(2)}) %collective-permute-start.58) | collective-permute-done | bytes 786464 | tf_op jit(solution)/shard_map/ppermute | solution.py:133
  778.5 14.3 %collective-permute-done.54 = f32[1,9280]{1,0:T(1,128)S(1)} collective-permute-done((f32[1,9280]{1,0:T(1,128)S(1)}, f32[1,9280]{1,0:T(1,128)S(1)}, u32[]{:S(2)}, u32[]{:S(2)}) %collective-permute-start.54) | collective-permute-done | bytes 37152 | tf_op jit(solution)/shard_map/ppermute | solution.py:160
  886.7 13.3 %collective-permute-done.66 = bf16[64,6144]{1,0:T(8,128)(2,1)S(1)} collective-permute-done((bf16[64,6144]{1,0:T(8,128)(2,1)S(1)}, bf16[64,6144]{1,0:T(8,128)(2,1)S(1)}, u32[]{:S(2)}, u32[]{:S(2)}) %collective-permute-start.66) | collective-permute-done | bytes 786464 | tf_op jit(solution)/shard_map/ppermute | solution.py:88
  904.6 13.0 %collective-permute-done.68 = bf16[64,6144]{1,0:T(8,128)(2,1)S(1)} collective-permute-done((bf16[64,6144]{1,0:T(8,128)(2,1)S(1)}, bf16[64,6144]{1,0:T(8,128)(2,1)S(1)}, u32[]{:S(2)}, u32[]{:S(2)}) %collective-permute-start.68) | collective-permute-done | bytes 786464 | tf_op jit(solution)/shard_map/ppermute | solution.py:88
  934.9 50.6 %reduce-scatter.8.cloned.1.call-done = bf16[2,256,2048]{2,1,0:T(8,128)(2,1)} async-done(((bf16[8,256,2048]{2,1,0:T(8,128)(2,1)}), bf16[2,256,2048]{2,1,0:T(8,128)(2,1)}) %reduce-scatter.8.cloned.1.call-update) | async-done | bytes 2097168 | tf_op jit(solution)/shard_map/reduce_scatter | solution.py:770
  (450 shorter events, 475.2 us)
Async XLA Ops:
  7.2 283.6 %all-gather.7.cloned.1.call-start = ((), (), s32[]{:S(2)}) async-start(), calls=%async_computation.14 | async-start | bytes 10485760 | tf_op jit(solution)/shard_map/all_gather | solution.py:638
  7.9 282.9 %all-gather.5.cloned.1.call-start = ((), (), s32[]{:S(2)}) async-start(), calls=%async_computation.13 | async-start | bytes 20971520 | tf_op jit(solution)/shard_map/all_gather | solution.py:637
  8.7 40.1 %collective-permute-start.4 = (bf16[256,2048]{1,0:T(8,128)(2,1)}, bf16[256,2048]{1,0:T(8,128)(2,1)}, u32[]{:S(2)}, u32[]{:S(2)}) collective-permute-start(bf16[256,2048]{1,0:T(8,128)(2,1)} %refs_3_.1), channel_id=1, source_target_pairs={{8,0},{16,8},{24,16},{28,24},{20,28},{12,20},{4,12},{0,4},{9,1},{1... | collective-permute-start | bytes 3145736 | tf_op jit(solution)/shard_map/ppermute | solution.py:618
  11.7 37.1 %collective-permute-start.3 = (bf16[256,2048]{1,0:T(8,128)(2,1)}, bf16[256,2048]{1,0:T(8,128)(2,1)}, u32[]{:S(2)}, u32[]{:S(2)}) collective-permute-start(bf16[256,2048]{1,0:T(8,128)(2,1)} %refs_3_.1), channel_id=1, source_target_pairs={{0,8},{8,16},{16,24},{24,28},{28,20},{20,12},{12,4},{4,0},{1,9},{9... | collective-permute-start | bytes 3145736 | tf_op jit(solution)/shard_map/ppermute | solution.py:617
  46.1 50.2 %collective-permute-start.1 = (bf16[256,2048]{1,0:T(8,128)(2,1)S(1)}, bf16[256,2048]{1,0:T(8,128)(2,1)}, u32[]{:S(2)}, u32[]{:S(2)}) collective-permute-start(bf16[256,2048]{1,0:T(8,128)(2,1)S(1)} %copy-done.7), channel_id=1, source_target_pairs={{0,2},{1,3},{2,0},{3,1},{4,6},{5,7},{6,4},{7,5},{8,10},{9,11},{10,... | collective-permute-start | bytes 3145736 | tf_op jit(solution)/shard_map/ppermute | solution.py:141
  134.4 35.6 %collective-permute-start.17 = (bf16[256,2048]{1,0:T(8,128)(2,1)}, bf16[256,2048]{1,0:T(8,128)(2,1)}, u32[]{:S(2)}, u32[]{:S(2)}) collective-permute-start(bf16[256,2048]{1,0:T(8,128)(2,1)} %collective-permute-done.4.refs_5_), channel_id=1, source_target_pairs={{8,0},{16,8},{24,16},{28,24},{20,28},{12,20},{4,12},{0,4},{9,1},{1... | collective-permute-start | bytes 3145736 | tf_op jit(solution)/shard_map/ppermute | solution.py:88
  173.0 48.3 %collective-permute-start.16 = (bf16[256,2048]{1,0:T(8,128)(2,1)S(1)}, bf16[256,2048]{1,0:T(8,128)(2,1)S(1)}, u32[]{:S(2)}, u32[]{:S(2)}) collective-permute-start(bf16[256,2048]{1,0:T(8,128)(2,1)S(1)} %add_convert_fusion.2), channel_id=1, source_target_pairs={{0,2},{1,3},{2,0},{3,1},{4,6},{5,7},{6,4},{7,5},{8,10},{9,11},{10,... | collective-permute-start | bytes 3145736 | tf_op jit(solution)/shard_map/ppermute | solution.py:141
  253.4 36.0 %collective-permute-start.23 = (bf16[256,2048]{1,0:T(8,128)(2,1)}, bf16[256,2048]{1,0:T(8,128)(2,1)}, u32[]{:S(2)}, u32[]{:S(2)}) collective-permute-start(bf16[256,2048]{1,0:T(8,128)(2,1)} %collective-permute-done.21.refs_2_), channel_id=1, source_target_pairs={{8,0},{16,8},{24,16},{28,24},{20,28},{12,20},{4,12},{0,4},{9,1},{1... | collective-permute-start | bytes 3145736 | tf_op jit(solution)/shard_map/ppermute | solution.py:88
  275.1 41.3 %collective-permute-start.24 = (bf16[256,2048]{1,0:T(8,128)(2,1)}, bf16[256,2048]{1,0:T(8,128)(2,1)S(1)}, u32[]{:S(2)}, u32[]{:S(2)}) collective-permute-start(bf16[256,2048]{1,0:T(8,128)(2,1)} %collective-permute-done.22.refs_1_), channel_id=1, source_target_pairs={{0,8},{8,16},{16,24},{24,28},{28,20},{20,12},{12,4},{4,0},{1,9},{9... | collective-permute-start | bytes 3145736 | tf_op jit(solution)/shard_map/ppermute | solution.py:87
  427.2 35.7 %collective-permute-start.34 = (bf16[256,2048]{1,0:T(8,128)(2,1)}, bf16[256,2048]{1,0:T(8,128)(2,1)}, u32[]{:S(2)}, u32[]{:S(2)}) collective-permute-start(bf16[256,2048]{1,0:T(8,128)(2,1)} %get-tuple-element.163), channel_id=1, source_target_pairs={{8,0},{16,8},{24,16},{28,24},{20,28},{12,20},{4,12},{0,4},{9,1},{1... | collective-permute-start | bytes 3145736 | tf_op jit(solution)/shard_map/ppermute | solution.py:132
  474.6 342.8 %all-reduce.8.cloned.1.call-start = ((), (), s32[]{:S(2)}) async-start(), calls=%async_computation.9 | async-start | bytes 4194304 | tf_op jit(solution)/shard_map/psum | solution.py:812
  481.4 44.8 %collective-permute-start.35 = (bf16[256,2048]{1,0:T(8,128)(2,1)}, bf16[256,2048]{1,0:T(8,128)(2,1)}, u32[]{:S(2)}, u32[]{:S(2)}) collective-permute-start(bf16[256,2048]{1,0:T(8,128)(2,1)} %get-tuple-element.164), channel_id=1, source_target_pairs={{0,8},{8,16},{16,24},{24,28},{28,20},{20,12},{12,4},{4,0},{1,9},{9... | collective-permute-start | bytes 3145736 | tf_op jit(solution)/shard_map/ppermute | solution.py:133
  487.6 40.4 %collective-permute-start.41 = (bf16[256,2048]{1,0:T(8,128)(2,1)}, bf16[256,2048]{1,0:T(8,128)(2,1)}, u32[]{:S(2)}, u32[]{:S(2)}) collective-permute-start(bf16[256,2048]{1,0:T(8,128)(2,1)} %get-tuple-element.152), channel_id=1, source_target_pairs={{0,8},{8,16},{16,24},{24,28},{28,20},{20,12},{12,4},{4,0},{1,9},{9... | collective-permute-start | bytes 3145736 | tf_op jit(solution)/shard_map/ppermute | solution.py:133
  488.3 41.6 %collective-permute-start.39 = (bf16[256,2048]{1,0:T(8,128)(2,1)}, bf16[256,2048]{1,0:T(8,128)(2,1)}, u32[]{:S(2)}, u32[]{:S(2)}) collective-permute-start(bf16[256,2048]{1,0:T(8,128)(2,1)} %get-tuple-element.153), channel_id=1, source_target_pairs={{8,0},{16,8},{24,16},{28,24},{20,28},{12,20},{4,12},{0,4},{9,1},{1... | collective-permute-start | bytes 3145736 | tf_op jit(solution)/shard_map/ppermute | solution.py:132
  542.2 72.6 %collective-permute-start.36 = (bf16[256,2048]{1,0:T(8,128)(2,1)}, bf16[256,2048]{1,0:T(8,128)(2,1)}, u32[]{:S(2)}, u32[]{:S(2)}) collective-permute-start(bf16[256,2048]{1,0:T(8,128)(2,1)} %get-tuple-element.154), channel_id=1, source_target_pairs={{8,0},{16,8},{24,16},{28,24},{20,28},{12,20},{4,12},{0,4},{9,1},{1... | collective-permute-start | bytes 3145736 | tf_op jit(solution)/shard_map/ppermute | solution.py:132
  543.8 71.0 %collective-permute-start.37 = (bf16[256,2048]{1,0:T(8,128)(2,1)}, bf16[256,2048]{1,0:T(8,128)(2,1)}, u32[]{:S(2)}, u32[]{:S(2)}) collective-permute-start(bf16[256,2048]{1,0:T(8,128)(2,1)} %get-tuple-element.155), channel_id=1, source_target_pairs={{0,8},{8,16},{16,24},{24,28},{28,20},{20,12},{12,4},{4,0},{1,9},{9... | collective-permute-start | bytes 3145736 | tf_op jit(solution)/shard_map/ppermute | solution.py:133
  570.9 39.4 %collective-permute-start.44 = (bf16[256,2048]{1,0:T(8,128)(2,1)}, bf16[256,2048]{1,0:T(8,128)(2,1)}, u32[]{:S(2)}, u32[]{:S(2)}) collective-permute-start(bf16[256,2048]{1,0:T(8,128)(2,1)} %get-tuple-element.150), channel_id=1, source_target_pairs={{8,0},{16,8},{24,16},{28,24},{20,28},{12,20},{4,12},{0,4},{9,1},{1... | collective-permute-start | bytes 3145736 | tf_op jit(solution)/shard_map/ppermute | solution.py:132
  572.5 37.7 %collective-permute-start.45 = (bf16[256,2048]{1,0:T(8,128)(2,1)}, bf16[256,2048]{1,0:T(8,128)(2,1)}, u32[]{:S(2)}, u32[]{:S(2)}) collective-permute-start(bf16[256,2048]{1,0:T(8,128)(2,1)} %get-tuple-element.151), channel_id=1, source_target_pairs={{0,8},{8,16},{16,24},{24,28},{28,20},{20,12},{12,4},{4,0},{1,9},{9... | collective-permute-start | bytes 3145736 | tf_op jit(solution)/shard_map/ppermute | solution.py:133
  642.0 286.7 %reduce-scatter.4.cloned.1.call-start = ((), (), s32[]{:S(2)}) async-start(), calls=%async_computation.10 | async-start | bytes 10485760 | tf_op jit(solution)/shard_map/reduce_scatter | solution.py:770
  642.5 286.1 %reduce-scatter.6.cloned.1.call-start = ((), (), s32[]{:S(2)}) async-start(), calls=%async_computation.11 | async-start | bytes 10485760 | tf_op jit(solution)/shard_map/reduce_scatter | solution.py:770
  643.1 342.4 %reduce-scatter.8.cloned.1.call-start = ((), (), s32[]{:S(2)}) async-start(), calls=%async_computation.12 | async-start | bytes 10485760 | tf_op jit(solution)/shard_map/reduce_scatter | solution.py:770
  712.6 40.5 %collective-permute-start.50 = (bf16[256,1536]{1,0:T(8,128)(2,1)}, bf16[256,1536]{1,0:T(8,128)(2,1)}, u32[]{:S(2)}, u32[]{:S(2)}) collective-permute-start(bf16[256,1536]{1,0:T(8,128)(2,1)} %fusion.54), channel_id=1, source_target_pairs={{8,0},{16,8},{24,16},{28,24},{20,28},{12,20},{4,12},{0,4},{9,1},{1... | collective-permute-start | bytes 2359304 | tf_op jit(solution)/shard_map/ppermute | solution.py:132
  801.2 35.3 %collective-permute-start.51 = (bf16[256,2048]{1,0:T(8,128)(2,1)}, bf16[256,2048]{1,0:T(8,128)(2,1)}, u32[]{:S(2)}, u32[]{:S(2)}) collective-permute-start(bf16[256,2048]{1,0:T(8,128)(2,1)} %get-tuple-element.146), channel_id=1, source_target_pairs={{0,1},{1,0},{2,3},{3,2},{4,5},{5,4},{6,7},{7,6},{8,9},{9,8},{10,11... | collective-permute-start | bytes 3145736 | tf_op jit(solution)/shard_map/ppermute | solution.py:141
  813.6 34.9 %collective-permute-start.53 = (bf16[256,2048]{1,0:T(8,128)(2,1)}, bf16[256,2048]{1,0:T(8,128)(2,1)}, u32[]{:S(2)}, u32[]{:S(2)}) collective-permute-start(bf16[256,2048]{1,0:T(8,128)(2,1)} %add_convert_fusion), channel_id=1, source_target_pairs={{0,2},{1,3},{2,0},{3,1},{4,6},{5,7},{6,4},{7,5},{8,10},{9,11},{10,... | collective-permute-start | bytes 3145736 | tf_op jit(solution)/shard_map/ppermute | solution.py:141
  (111 other events, 1927.4 us)
Sparse Core Ops, SparseCore 0:
  9.6 92.6 all-gather.6
  103.8 128.3 all-gather.4
  642.1 111.1 all-reduce.7
  756.3 80.0 reduce-scatter.3
  838.8 72.8 reduce-scatter.5
  914.1 71.4 reduce-scatter.7

commit v5 on v4

--- a/solution.py
+++ b/solution.py
@@ -766,14 +766,20 @@
     mix_parts = shard_gather(hidden_low)
     mix_back = jnp.concatenate(mix_parts, axis=0)
 
-    gate_grads, up_grads, down_grads = (
+    gate_grads = shard_scatter(
+        [
+            lax.dynamic_index_in_dim(gate_parts, relative[r], 0, keepdims=False)
+            for r in range(n_shard)
+        ]
+    )
+    up_grads, down_grads = (
         lax.psum_scatter(
             parts.reshape((n_shard * local_experts,) + parts.shape[2:]),
             "shard",
             scatter_dimension=0,
             tiled=True,
         ).astype(F32)
-        for parts in (gate_parts, up_parts, down_parts)
+        for parts in (up_parts, down_parts)
     )
 
     head_back = dot_f32(mix_back, w_out, ((1,), (1,))).astype(BF16)

time: 1010 us -> 999 us (0.989)
  waiting for transfers between devices: 358 us -> 319 us
  starting transfers between devices: 90.6 us -> 102 us
  local copies, waits for them, and re-layouts: 79 us -> 90.3 us
    reduce_scatter x3 -> x2, waiting for transfers between devices: 50.6 us -> 0.01 us  [on_device(): lax.psum_scatter(parts.reshape((n_shard * local_experts,) + parts.shape[2...]
    all_to_all x1, waiting for transfers between devices: 1.48 us -> 20.6 us  [on_device(): lax.all_to_all(small, 'shard', split_axis=0, concat_axis=0, tiled=True)]
    ppermute x9, waiting for transfers between devices: 25.2 us -> 12.5 us  [ring_scatter(): lax.ppermute((own_down + down.astype(F32) + both).astype(BF16), 'expert',...]
    ppermute x8, waiting for transfers between devices: 37 us -> 25.9 us  [ring_rest(): from_behind = lax.ppermute(from_behind, 'expert', ahead)]
    ppermute x12 -> x15, waiting for transfers between devices: 74.6 us -> 67.6 us  [swap(): return lax.ppermute(value, 'shard', [(i, i ^ bit) for i in range(size)])]
  transfers between devices with their start and end apart: 83 -> 85, of which waited for: 35 -> 32; matrix products, arithmetic and copies ran while one was open for 19% -> 21% of each run, Pallas kernels for 23% -> 23%
where the time goes in v5:
time: 999 us; the launch traced here: 993 us
  waiting for transfers between devices  319 us (32%)
  Pallas kernels  267 us (27%)
  other arithmetic  108 us (11%)
  starting transfers between devices  102 us (10%)
  local copies, waits for them, and re-layouts  90.3 us (9%)
  between operations  56.2 us (6%)
  matrix products  51.1 us (5%)
    pallas_call x6, Pallas kernels, expert_combine(): pl.pallas_call(functools.partial(combine_kernel, count, pairs, dim), grid...  96.8 us
    ppermute x15, waiting for transfers between devices, swap(): return lax.ppermute(value, 'shard', [(i, i ^ bit) for i in range(size)])  67.6 us
    pallas_call x3, Pallas kernels, expert_group(): pl.pallas_call(functools.partial(expert_kernel, count, len(after)), grid=...  67 us
    pallas_call x3, Pallas kernels, expert_grad(): pl.pallas_call(functools.partial(grad_kernel, len(lefts)), grid=(experts,...  52.7 us
    ppermute x8, waiting for transfers between devices, ring_rest(): from_ahead = lax.ppermute(from_ahead, 'expert', back)  38.9 us
    dot_general x6, matrix products, dot_f32(): lax.dot_general(left, right, (dims, ((), ())), preferred_element_type=F32)  35.8 us
    pallas_call x1, Pallas kernels, attention_back(): pl.pallas_call(functools.partial(attention_back_kernel, size ** (-0.5), m...  31.6 us
    convert_element_type x8, other arithmetic, ring_scatter(): (own_down + down.astype(F32) + both).astype(BF16)  26.9 us
  transfers between devices with their start and end apart: 85, of which 32 were waited for; matrix products, arithmetic and copies ran while one was open for 21% of the time, Pallas kernels for 23%

profile of v5, /device:TPU:0, one launch (start us, length us, event | category | flops | bytes accessed | tf_op | source)
XLA Modules:
  0.0 993.0 jit_solution(7093175855079712164)
XLA Ops:
  30.9 15.2 %all-to-all-done = bf16[4,64,1536]{2,1,0:T(8,128)(2,1)} async-done(((bf16[4,64,1536]{2,1,0:T(8,128)(2,1)}), bf16[4,64,1536]{2,1,0:T(8,128)(2,1)}, u32[]{:S(2)}, u32[]{:S(2)}) %all-to-all-start) | async-done | bytes 786464 | tf_op jit(solution)/shard_map/all_to_all | solution.py:610
  78.6 21.0 %collective-permute-done.1 = bf16[256,2048]{1,0:T(8,128)(2,1)} collective-permute-done((bf16[256,2048]{1,0:T(8,128)(2,1)S(1)}, bf16[256,2048]{1,0:T(8,128)(2,1)}, u32[]{:S(2)}, u32[]{:S(2)}) %collective-permute-start.1) | collective-permute-done | bytes 1048608 | tf_op jit(solution)/shard_map/ppermute | solution.py:141
  150.4 18.8 %attention.1 = bf16[1024,512]{1,0:T(8,128)(2,1)} custom-call(f32[1024,1536]{1,0:T(8,128)} %fusion.60.q_ref.k_ref.v_ref, f32[1024,1536]{1,0:T(8,128)} %fusion.60.q_ref.k_ref.v_ref, f32[1024,1536]{1,0:T(8,128)} %fusion.60.q_ref.k_ref.v_ref, f32[1024,128]{1,0:T(8,128)} %pad_maximum_fusion.7.cos_ref, f32[1024,128]{1,0:T(8,128)} %pad_maximum_fusion.8.sin_ref, ...), custom_call_target="tpu_custom_call" | custom-call | flops 2147483648 | bytes 7340032 | tf_op jit(solution)/shard_map/attention/pallas_call | solution.py:255
  177.0 21.9 %collective-permute-done.18.refs_5_ = bf16[256,2048]{1,0:T(8,128)(2,1)S(1)} collective-permute-done((bf16[256,2048]{1,0:T(8,128)(2,1)}, bf16[256,2048]{1,0:T(8,128)(2,1)S(1)}, u32[]{:S(2)}, u32[]{:S(2)}) %collective-permute-start.18) | collective-permute-done | bytes 1048608 | tf_op jit(solution)/shard_map/ppermute | solution.py:87
  201.3 23.9 %collective-permute-done.16 = bf16[256,2048]{1,0:T(8,128)(2,1)S(1)} collective-permute-done((bf16[256,2048]{1,0:T(8,128)(2,1)S(1)}, bf16[256,2048]{1,0:T(8,128)(2,1)S(1)}, u32[]{:S(2)}, u32[]{:S(2)}) %collective-permute-start.16) | collective-permute-done | bytes 1048608 | tf_op jit(solution)/shard_map/ppermute | solution.py:141
  235.2 17.4 %collective-permute-done.20.refs_1_ = bf16[256,2048]{1,0:T(8,128)(2,1)} collective-permute-done((bf16[256,2048]{1,0:T(8,128)(2,1)S(1)}, bf16[256,2048]{1,0:T(8,128)(2,1)}, u32[]{:S(2)}, u32[]{:S(2)}) %collective-permute-start.20) | collective-permute-done | bytes 1048608 | tf_op jit(solution)/shard_map/ppermute | solution.py:75
  304.4 23.8 %experts.3 = (bf16[2,384,2048]{2,1,0:T(8,128)(2,1)}, bf16[2,384,2048]{2,1,0:T(8,128)(2,1)}, bf16[2,384,1024]{2,1,0:T(8,128)(2,1)}, bf16[2,384,1024]{2,1,0:T(8,12...) custom-call(s32[1]{0:T(128)} %bitcast.25.base_ref, bf16[256,2048]{1,0:T(8,128)(2,1)} %copy-done.5, ...), custom_call_target="tpu_custom_call" | custom-call | flops 9663676416 | bytes 25165824 | tf_op jit(solution)/shard_map/experts/pallas_call | solution.py:406
  334.1 19.4 %experts.4 = (bf16[2,256,2048]{2,1,0:T(8,128)(2,1)}, bf16[2,256,2048]{2,1,0:T(8,128)(2,1)}, bf16[2,256,1024]{2,1,0:T(8,128)(2,1)}, bf16[2,256,1024]{2,1,0:T(8,12...) custom-call(s32[1]{0:T(128)} %bitcast.25.base_ref, f32[2,3,256]{2,1,0:T(4,128)} %get-tuple-element.50.refs_0_, ...), custom_call_target="tpu_custom_call" | custom-call | flops 6442450944 | bytes 25165824 | tf_op jit(solution)/shard_map/experts/pallas_call | solution.py:406
  355.8 23.8 %experts.5 = (bf16[2,384,2048]{2,1,0:T(8,128)(2,1)}, bf16[2,384,2048]{2,1,0:T(8,128)(2,1)}, bf16[2,384,1024]{2,1,0:T(8,128)(2,1)}, bf16[2,384,1024]{2,1,0:T(8,12...) custom-call(s32[1]{0:T(128)} %bitcast.25.base_ref, f32[2,2,256]{2,1,0:T(2,128)} %get-tuple-element.52.refs_0_, ...), custom_call_target="tpu_custom_call" | custom-call | flops 9663676416 | bytes 25165824 | tf_op jit(solution)/shard_map/experts/pallas_call | solution.py:406
  379.6 15.3 %expert_combine.6.refs_2_ = bf16[3,256,2048]{2,1,0:T(8,128)(2,1)} custom-call(s32[2,3,256]{2,1,0:T(4,128)} %pad_add_fusion.1.refs_7_.slot_ref, bf16[2,384,1024]{2,1,0:T(8,128)(2,1)} %get-tuple-element.53.refs_0_.refs_2_, bf16[4,2,256,2048]{3,2,1,0:T(8,128)(2,1)} %bitcast.277, f32[2,3,256]{2,1,0:T(4,128)} %get-tuple-element.54.refs_2_), custom_call_target="tpu_custom_call" | custom-call | flops 3221225472 | bytes 13107200 | tf_op jit(solution)/shard_map/expert_combine/pallas_call | solution.py:495
  442.0 15.3 %expert_combine.8.refs_4_ = bf16[3,256,2048]{2,1,0:T(8,128)(2,1)} custom-call(s32[2,3,256]{2,1,0:T(4,128)} %pad_add_fusion.refs_6_.slot_ref, bf16[2,384,1024]{2,1,0:T(8,128)(2,1)} %get-tuple-element.49.refs_0_, bf16[4,2,256,2048]{3,2,1,0:T(8,128)(2,1)} %bitcast.279, bf16[2,256,2048]{2,1,0:T(8,128)(2,1)} %expert_combine.7.refs_2_, bf16[128,2048]{1,0:T(8,128)(2,1)} %copy-done.22), custom_call_target="tpu_custom_call" | custom-call | flops 3221225472 | bytes 13107200 | tf_op jit(solution)/shard_map/expert_combine/pallas_call | solution.py:495
  457.3 19.1 %expert_combine.9.refs_4_ = bf16[3,256,2048]{2,1,0:T(8,128)(2,1)} custom-call(s32[2,3,256]{2,1,0:T(4,128)} %pad_add_fusion.1.refs_7_.slot_ref, bf16[2,384,1024]{2,1,0:T(8,128)(2,1)} %get-tuple-element.59.refs_0_.refs_5_, bf16[2,384,1024]{2,1,0:T(8,128)(2,1)} %get-tuple-element.60.refs_1_.refs_5_, bf16[4,2,2,2048,256]{4,3,2,1,0:T(8,128)(2,1)} %bitcast.268, ...), custom_call_target="tpu_custom_call" | custom-call | flops 6442450944 | bytes 23068672 | tf_op jit(solution)/shard_map/expert_combine/pallas_call | solution.py:495
  504.7 15.5 %expert_combine.10.refs_4_ = bf16[2,256,2048]{2,1,0:T(8,128)(2,1)} custom-call(s32[2,2,256]{2,1,0:T(2,128)} %pad_add_fusion.2.refs_5_.slot_ref, bf16[2,256,1024]{2,1,0:T(8,128)(2,1)} %get-tuple-element.57.refs_0_.refs_4_, bf16[2,256,1024]{2,1,0:T(8,128)(2,1)} %get-tuple-element.58.refs_1_.refs_4_, bf16[4,2,2,2048,256]{4,3,2,1,0:T(8,128)(2,1)} %bitcast.270, ...), custom_call_target="tpu_custom_call" | custom-call | flops 4294967296 | bytes 20971520 | tf_op jit(solution)/shard_map/expert_combine/pallas_call | solution.py:495
  520.2 19.1 %expert_combine.11.refs_6_ = bf16[3,256,2048]{2,1,0:T(8,128)(2,1)} custom-call(s32[2,3,256]{2,1,0:T(4,128)} %pad_add_fusion.refs_6_.slot_ref, bf16[2,384,1024]{2,1,0:T(8,128)(2,1)} %get-tuple-element.55.refs_0_.refs_3_, bf16[2,384,1024]{2,1,0:T(8,128)(2,1)} %get-tuple-element.56.refs_1_.refs_3_, bf16[4,2,2,2048,256]{4,3,2,1,0:T(8,128)(2,1)} %bitcast.272, ...), custom_call_target="tpu_custom_call" | custom-call | flops 6442450944 | bytes 23068672 | tf_op jit(solution)/shard_map/expert_combine/pallas_call | solution.py:495
  557.3 17.5 %expert_grad.3.refs_6_ = bf16[4,2,2048,256]{3,2,1,0:T(8,128)(2,1)} custom-call(bf16[2,384,2048]{2,1,0:T(8,128)(2,1)} %get-tuple-element.64.refs_0_, bf16[2,256,2048]{2,1,0:T(8,128)(2,1)} %get-tuple-element.65.refs_1_, bf16[2,384,2048]{2,1,0:T(8,128)(2,1)} %get-tuple-element.66.refs_2_, bf16[2,384,1024]{2,1,0:T(8,128)(2,1)} %get-tuple-element.55.refs_0_.refs_3_, ...), custom_call_target="tpu_custom_call" | custom-call | flops 8589934592 | bytes 33554432 | tf_op jit(solution)/shard_map/expert_grad/pallas_call | solution.py:542
  586.2 17.5 %expert_grad.4.refs_6_ = bf16[4,2,2048,256]{3,2,1,0:T(8,128)(2,1)} custom-call(bf16[2,384,2048]{2,1,0:T(8,128)(2,1)} %get-tuple-element.64.refs_0_, bf16[2,256,2048]{2,1,0:T(8,128)(2,1)} %get-tuple-element.65.refs_1_, bf16[2,384,2048]{2,1,0:T(8,128)(2,1)} %get-tuple-element.66.refs_2_, bf16[2,384,1024]{2,1,0:T(8,128)(2,1)} %get-tuple-element.56.refs_1_.refs_3_, ...), custom_call_target="tpu_custom_call" | custom-call | flops 8589934592 | bytes 33554432 | tf_op jit(solution)/shard_map/expert_grad/pallas_call | solution.py:542
  603.7 17.6 %expert_grad.5 = bf16[4,2,256,2048]{3,2,1,0:T(8,128)(2,1)} custom-call(bf16[2,384,1024]{2,1,0:T(8,128)(2,1)} %get-tuple-element.49.refs_0_, bf16[2,256,1024]{2,1,0:T(8,128)(2,1)} %get-tuple-element.51.refs_0_.refs_1_, bf16[2,384,1024]{2,1,0:T(8,128)(2,1)} %get-tuple-element.53.refs_0_.refs_2_, bf16[2,384,2048]{2,1,0:T(8,128)(2,1)} %get-tuple-element.61.refs_3_, ...), custom_call_target="tpu_custom_call" | custom-call | flops 8589934592 | bytes 11534336 | tf_op jit(solution)/shard_map/expert_grad/pallas_call | solution.py:542
  633.1 14.5 %collective-permute-done.47 = bf16[256,2048]{1,0:T(8,128)(2,1)S(1)} collective-permute-done((bf16[256,2048]{1,0:T(8,128)(2,1)S(1)}, bf16[256,2048]{1,0:T(8,128)(2,1)S(1)}, u32[]{:S(2)}, u32[]{:S(2)}) %collective-permute-start.47) | collective-permute-done | bytes 1048608 | tf_op jit(solution)/shard_map/ppermute | solution.py:141
  680.3 31.6 %attention_back.1 = (bf16[1024,512]{1,0:T(8,128)(2,1)}, bf16[1024,512]{1,0:T(8,128)(2,1)}, bf16[1024,512]{1,0:T(8,128)(2,1)}, f32[2,128]{1,0:T(2,128)}) custom-call(f32[1024,1536]{1,0:T(8,128)} %fusion.60.q_ref.k_ref.v_ref, f32[1024,1536]{1,0:T(8,128)} %fusion.60.q_ref.k_ref.v_ref, f32[1024,1536]{1,0:T(8,128)} %fusion.60.q_ref.k_ref.v_ref, ...), custom_call_target="tpu_custom_call" | custom-call | flops 5368709120 | bytes 10485760 | tf_op jit(solution)/shard_map/attention_back/pallas_call | solution.py:275
  728.6 17.5 %collective-permute-done.49 = bf16[128,1536]{1,0:T(8,128)(2,1)S(1)} collective-permute-done((bf16[128,1536]{1,0:T(8,128)(2,1)S(1)}, bf16[128,1536]{1,0:T(8,128)(2,1)S(1)}, u32[]{:S(2)}, u32[]{:S(2)}) %collective-permute-start.49) | collective-permute-done | bytes 393248 | tf_op jit(solution)/shard_map/ppermute | solution.py:120
  759.3 15.3 %collective-permute-done.58 = bf16[256,1536]{1,0:T(8,128)(2,1)} collective-permute-done((bf16[256,1536]{1,0:T(8,128)(2,1)}, bf16[256,1536]{1,0:T(8,128)(2,1)}, u32[]{:S(2)}, u32[]{:S(2)}) %collective-permute-start.58) | collective-permute-done | bytes 786464 | tf_op jit(solution)/shard_map/ppermute | solution.py:133
  778.4 13.9 %fusion.4 = (f32[2048]{0:T(1024)S(1)}, bf16[1024,2048]{1,0:T(8,128)(2,1)}) fusion(f32[1024]{0:T(1024)S(1)} %copy-done.43, bf16[256,2048]{1,0:T(8,128)(2,1)} %copy-done.25, bf16[256,2048]{1,0:T(8,128)(2,1)} %collective-permute-done.1, bf16[256,2048]{1,0:T(8,128)(2,1)} %copy-done.23, bf16[256,2048]{1,0:T(8,128)(2,1)S(1)} %copy-done.10, ...), kind=kOutput, calls=%fused_computation.11 | convolution fusion | flops 6469187584 | bytes 17838082 | tf_op jit(solution)/shard_map/dot_general | solution.py:19
  801.7 20.6 %all-to-all-done.4 = f32[4,1,9280]{2,1,0:T(1,128)S(1)} async-done(((f32[4,1,9280]{2,1,0:T(1,128)}), f32[4,1,9280]{2,1,0:T(1,128)S(1)}, u32[]{:S(2)}, u32[]{:S(2)}) %all-to-all-start.4) | async-done | bytes 148512 | tf_op jit(solution)/shard_map/all_to_all | solution.py:840
  934.1 13.5 %collective-permute-done.66 = bf16[64,6144]{1,0:T(8,128)(2,1)S(1)} collective-permute-done((bf16[64,6144]{1,0:T(8,128)(2,1)S(1)}, bf16[64,6144]{1,0:T(8,128)(2,1)S(1)}, u32[]{:S(2)}, u32[]{:S(2)}) %collective-permute-start.66) | collective-permute-done | bytes 786464 | tf_op jit(solution)/shard_map/ppermute | solution.py:88
  (474 shorter events, 487.8 us)
Async XLA Ops:
  7.2 297.2 %all-gather.7.cloned.1.call-start = ((), (), s32[]{:S(2)}) async-start(), calls=%async_computation.12 | async-start | bytes 10485760 | tf_op jit(solution)/shard_map/all_gather | solution.py:638
  7.9 296.5 %all-gather.5.cloned.1.call-start = ((), (), s32[]{:S(2)}) async-start(), calls=%async_computation.11 | async-start | bytes 20971520 | tf_op jit(solution)/shard_map/all_gather | solution.py:637
  8.7 42.7 %collective-permute-start.4 = (bf16[256,2048]{1,0:T(8,128)(2,1)}, bf16[256,2048]{1,0:T(8,128)(2,1)}, u32[]{:S(2)}, u32[]{:S(2)}) collective-permute-start(bf16[256,2048]{1,0:T(8,128)(2,1)} %refs_3_.1), channel_id=1, source_target_pairs={{8,0},{16,8},{24,16},{28,24},{20,28},{12,20},{4,12},{0,4},{9,1},{1... | collective-permute-start | bytes 3145736 | tf_op jit(solution)/shard_map/ppermute | solution.py:618
  11.7 39.7 %collective-permute-start.3 = (bf16[256,2048]{1,0:T(8,128)(2,1)}, bf16[256,2048]{1,0:T(8,128)(2,1)}, u32[]{:S(2)}, u32[]{:S(2)}) collective-permute-start(bf16[256,2048]{1,0:T(8,128)(2,1)} %refs_3_.1), channel_id=1, source_target_pairs={{0,8},{8,16},{16,24},{24,28},{28,20},{20,12},{12,4},{4,0},{1,9},{9... | collective-permute-start | bytes 3145736 | tf_op jit(solution)/shard_map/ppermute | solution.py:617
  49.4 50.2 %collective-permute-start.1 = (bf16[256,2048]{1,0:T(8,128)(2,1)S(1)}, bf16[256,2048]{1,0:T(8,128)(2,1)}, u32[]{:S(2)}, u32[]{:S(2)}) collective-permute-start(bf16[256,2048]{1,0:T(8,128)(2,1)S(1)} %copy-done.8), channel_id=1, source_target_pairs={{0,2},{1,3},{2,0},{3,1},{4,6},{5,7},{6,4},{7,5},{8,10},{9,11},{10,... | collective-permute-start | bytes 3145736 | tf_op jit(solution)/shard_map/ppermute | solution.py:141
  137.4 35.7 %collective-permute-start.17 = (bf16[256,2048]{1,0:T(8,128)(2,1)}, bf16[256,2048]{1,0:T(8,128)(2,1)}, u32[]{:S(2)}, u32[]{:S(2)}) collective-permute-start(bf16[256,2048]{1,0:T(8,128)(2,1)} %collective-permute-done.4.refs_5_), channel_id=1, source_target_pairs={{8,0},{16,8},{24,16},{28,24},{20,28},{12,20},{4,12},{0,4},{9,1},{1... | collective-permute-start | bytes 3145736 | tf_op jit(solution)/shard_map/ppermute | solution.py:88
  176.9 48.3 %collective-permute-start.16 = (bf16[256,2048]{1,0:T(8,128)(2,1)S(1)}, bf16[256,2048]{1,0:T(8,128)(2,1)S(1)}, u32[]{:S(2)}, u32[]{:S(2)}) collective-permute-start(bf16[256,2048]{1,0:T(8,128)(2,1)S(1)} %add_convert_fusion.2), channel_id=1, source_target_pairs={{0,2},{1,3},{2,0},{3,1},{4,6},{5,7},{6,4},{7,5},{8,10},{9,11},{10,... | collective-permute-start | bytes 3145736 | tf_op jit(solution)/shard_map/ppermute | solution.py:141
  257.0 45.9 %collective-permute-start.23 = (bf16[256,2048]{1,0:T(8,128)(2,1)}, bf16[256,2048]{1,0:T(8,128)(2,1)}, u32[]{:S(2)}, u32[]{:S(2)}) collective-permute-start(bf16[256,2048]{1,0:T(8,128)(2,1)} %collective-permute-done.21.refs_2_), channel_id=1, source_target_pairs={{8,0},{16,8},{24,16},{28,24},{20,28},{12,20},{4,12},{0,4},{9,1},{1... | collective-permute-start | bytes 3145736 | tf_op jit(solution)/shard_map/ppermute | solution.py:88
  278.9 51.1 %collective-permute-start.24 = (bf16[256,2048]{1,0:T(8,128)(2,1)}, bf16[256,2048]{1,0:T(8,128)(2,1)S(1)}, u32[]{:S(2)}, u32[]{:S(2)}) collective-permute-start(bf16[256,2048]{1,0:T(8,128)(2,1)} %collective-permute-done.22.refs_1_), channel_id=1, source_target_pairs={{0,8},{8,16},{16,24},{24,28},{28,20},{20,12},{12,4},{4,0},{1,9},{9... | collective-permute-start | bytes 3145736 | tf_op jit(solution)/shard_map/ppermute | solution.py:87
  487.6 373.7 %all-reduce.8.cloned.1.call-start = ((), (), s32[]{:S(2)}) async-start(), calls=%async_computation.8 | async-start | bytes 4194304 | tf_op jit(solution)/shard_map/psum | solution.py:818
  494.4 44.9 %collective-permute-start.35 = (bf16[256,2048]{1,0:T(8,128)(2,1)}, bf16[256,2048]{1,0:T(8,128)(2,1)}, u32[]{:S(2)}, u32[]{:S(2)}) collective-permute-start(bf16[256,2048]{1,0:T(8,128)(2,1)} %get-tuple-element.177), channel_id=1, source_target_pairs={{0,8},{8,16},{16,24},{24,28},{28,20},{20,12},{12,4},{4,0},{1,9},{9... | collective-permute-start | bytes 3145736 | tf_op jit(solution)/shard_map/ppermute | solution.py:133
  500.6 40.5 %collective-permute-start.41 = (bf16[256,2048]{1,0:T(8,128)(2,1)}, bf16[256,2048]{1,0:T(8,128)(2,1)}, u32[]{:S(2)}, u32[]{:S(2)}) collective-permute-start(bf16[256,2048]{1,0:T(8,128)(2,1)} %get-tuple-element.165), channel_id=1, source_target_pairs={{0,8},{8,16},{16,24},{24,28},{28,20},{20,12},{12,4},{4,0},{1,9},{9... | collective-permute-start | bytes 3145736 | tf_op jit(solution)/shard_map/ppermute | solution.py:133
  501.3 41.6 %collective-permute-start.39 = (bf16[256,2048]{1,0:T(8,128)(2,1)}, bf16[256,2048]{1,0:T(8,128)(2,1)}, u32[]{:S(2)}, u32[]{:S(2)}) collective-permute-start(bf16[256,2048]{1,0:T(8,128)(2,1)} %get-tuple-element.166), channel_id=1, source_target_pairs={{8,0},{16,8},{24,16},{28,24},{20,28},{12,20},{4,12},{0,4},{9,1},{1... | collective-permute-start | bytes 3145736 | tf_op jit(solution)/shard_map/ppermute | solution.py:132
  555.2 72.4 %collective-permute-start.36 = (bf16[256,2048]{1,0:T(8,128)(2,1)}, bf16[256,2048]{1,0:T(8,128)(2,1)}, u32[]{:S(2)}, u32[]{:S(2)}) collective-permute-start(bf16[256,2048]{1,0:T(8,128)(2,1)} %get-tuple-element.167), channel_id=1, source_target_pairs={{8,0},{16,8},{24,16},{28,24},{20,28},{12,20},{4,12},{0,4},{9,1},{1... | collective-permute-start | bytes 3145736 | tf_op jit(solution)/shard_map/ppermute | solution.py:132
  556.9 70.8 %collective-permute-start.37 = (bf16[256,2048]{1,0:T(8,128)(2,1)}, bf16[256,2048]{1,0:T(8,128)(2,1)}, u32[]{:S(2)}, u32[]{:S(2)}) collective-permute-start(bf16[256,2048]{1,0:T(8,128)(2,1)} %get-tuple-element.168), channel_id=1, source_target_pairs={{0,8},{8,16},{16,24},{24,28},{28,20},{20,12},{12,4},{4,0},{1,9},{9... | collective-permute-start | bytes 3145736 | tf_op jit(solution)/shard_map/ppermute | solution.py:133
  584.0 39.2 %collective-permute-start.44 = (bf16[256,2048]{1,0:T(8,128)(2,1)}, bf16[256,2048]{1,0:T(8,128)(2,1)}, u32[]{:S(2)}, u32[]{:S(2)}) collective-permute-start(bf16[256,2048]{1,0:T(8,128)(2,1)} %get-tuple-element.163), channel_id=1, source_target_pairs={{8,0},{16,8},{24,16},{28,24},{20,28},{12,20},{4,12},{0,4},{9,1},{1... | collective-permute-start | bytes 3145736 | tf_op jit(solution)/shard_map/ppermute | solution.py:132
  585.6 37.6 %collective-permute-start.45 = (bf16[256,2048]{1,0:T(8,128)(2,1)}, bf16[256,2048]{1,0:T(8,128)(2,1)}, u32[]{:S(2)}, u32[]{:S(2)}) collective-permute-start(bf16[256,2048]{1,0:T(8,128)(2,1)} %get-tuple-element.164), channel_id=1, source_target_pairs={{0,8},{8,16},{16,24},{24,28},{28,20},{20,12},{12,4},{4,0},{1,9},{9... | collective-permute-start | bytes 3145736 | tf_op jit(solution)/shard_map/ppermute | solution.py:133
  654.9 319.8 %reduce-scatter.3.cloned.1.call-start = ((), (), s32[]{:S(2)}) async-start(), calls=%async_computation.9 | async-start | bytes 10485760 | tf_op jit(solution)/shard_map/reduce_scatter | solution.py:776
  655.4 326.6 %reduce-scatter.5.cloned.1.call-start = ((), (), s32[]{:S(2)}) async-start(), calls=%async_computation.10 | async-start | bytes 10485760 | tf_op jit(solution)/shard_map/reduce_scatter | solution.py:776
  674.2 80.8 %collective-permute-start.72 = (bf16[2,2048,256]{2,1,0:T(8,128)(2,1)}, bf16[2,2048,256]{2,1,0:T(8,128)(2,1)}, u32[]{:S(2)}, u32[]{:S(2)}) collective-permute-start(bf16[2,2048,256]{2,1,0:T(8,128)(2,1)} %get-tuple-element.147), channel_id=1, source_target_pairs={{0,1},{1,0},{2,3},{3,2},{4,5},{5,4},{6,7},{7,6},{8,9},{9,8},{10,11... | collective-permute-start | bytes 6291464 | tf_op jit(solution)/shard_map/ppermute | solution.py:141
  754.8 72.9 %collective-permute-start.71 = (bf16[2,2048,256]{2,1,0:T(8,128)(2,1)}, bf16[2,2048,256]{2,1,0:T(8,128)(2,1)}, u32[]{:S(2)}, u32[]{:S(2)}) collective-permute-start(bf16[2,2048,256]{2,1,0:T(8,128)(2,1)} %get-tuple-element.146), channel_id=1, source_target_pairs={{0,1},{1,0},{2,3},{3,2},{4,5},{5,4},{6,7},{7,6},{8,9},{9,8},{10,11... | collective-permute-start | bytes 6291464 | tf_op jit(solution)/shard_map/ppermute | solution.py:141
  759.1 68.6 %collective-permute-start.73 = (bf16[2,2048,256]{2,1,0:T(8,128)(2,1)}, bf16[2,2048,256]{2,1,0:T(8,128)(2,1)}, u32[]{:S(2)}, u32[]{:S(2)}) collective-permute-start(bf16[2,2048,256]{2,1,0:T(8,128)(2,1)} %fusion.5), channel_id=1, source_target_pairs={{0,2},{1,3},{2,0},{3,1},{4,6},{5,7},{6,4},{7,5},{8,10},{9,11},{10,... | collective-permute-start | bytes 6291464 | tf_op jit(solution)/shard_map/ppermute | solution.py:141
  799.1 49.7 %collective-permute-start.59 = (bf16[256,1536]{1,0:T(8,128)(2,1)}, bf16[256,1536]{1,0:T(8,128)(2,1)}, u32[]{:S(2)}, u32[]{:S(2)}) collective-permute-start(bf16[256,1536]{1,0:T(8,128)(2,1)} %fusion.51), channel_id=1, source_target_pairs={{8,0},{16,8},{24,16},{28,24},{20,28},{12,20},{4,12},{0,4},{9,1},{1... | collective-permute-start | bytes 2359304 | tf_op jit(solution)/shard_map/ppermute | solution.py:132
  845.3 37.7 %collective-permute-start.51 = (bf16[256,2048]{1,0:T(8,128)(2,1)}, bf16[256,2048]{1,0:T(8,128)(2,1)}, u32[]{:S(2)}, u32[]{:S(2)}) collective-permute-start(bf16[256,2048]{1,0:T(8,128)(2,1)} %get-tuple-element.159), channel_id=1, source_target_pairs={{0,1},{1,0},{2,3},{3,2},{4,5},{5,4},{6,7},{7,6},{8,9},{9,8},{10,11... | collective-permute-start | bytes 3145736 | tf_op jit(solution)/shard_map/ppermute | solution.py:141
  (120 other events, 2047.1 us)
Sparse Core Ops, SparseCore 0:
  9.6 93.0 all-gather.6
  104.2 128.3 all-gather.4
  655.0 112.9 all-reduce.7
  770.4 84.9 reduce-scatter.2
  857.9 80.0 reduce-scatter.4
